TPU v7x, 32 devices: a whole 2x2x4 slice. The times are simulated.
32 devices in a mesh: wide: 8 (over z, x), narrow: 4 (over y, core).
Axes of the slice: x: 2, y: 2, z: 4, core: 2. Of those that a mesh axis runs over, the one named last changes fastest.
Arguments:
- block_input: bfloat16 [12288, 768], P('wide')
- cotangent: bfloat16 [12288, 768], P('wide'), may hold values from -6 to 6
- lengths: int32 [16, 12], P('wide'), may hold values from 0 to 384, as said below
- project_weight: float32 [3, 768, 768], P(None, 'wide', 'narrow'), may hold values from -0.125 to 0.125
- output_weight: float32 [768, 768], P('narrow', 'wide'), may hold values from -1.25 to 1.25
- expand_weight: float32 [2, 768, 2048], P(None, 'wide', 'narrow'), may hold values from -0.21875 to 0.21875
- shrink_weight: float32 [2048, 768], P('narrow', 'wide'), may hold values from -0.1875 to 0.1875
- bucket_bias: float32 [32, 12], replicated, may hold values from -3 to 3
- norm_gains: float32 [2, 768], P(None, 'wide'), may hold values from 0.5 to 1.5
- project_first: float32 [3, 768, 768], P(None, 'wide', 'narrow'), may hold values from -0.00061035156 to 0.00061035156
- output_first: float32 [768, 768], P('narrow', 'wide'), may hold values from -7.6293945e-05 to 7.6293945e-05
- expand_first: float32 [2, 768, 2048], P(None, 'wide', 'narrow'), may hold values from -0.00015258789 to 0.00015258789
- shrink_first: float32 [2048, 768], P('narrow', 'wide'), may hold values from -0.00015258789 to 0.00015258789
- bucket_first: float32 [32, 12], replicated, may hold values from -0.00010681152 to 0.00010681152
- gains_first: float32 [2, 768], P(None, 'wide'), may hold values from -0.00048828125 to 0.00048828125
- project_second: float32 [3, 768, 768], P(None, 'wide', 'narrow'), may hold values from 4.3798376e-10 to 7.064254e-09
- output_second: float32 [768, 768], P('narrow', 'wide'), may hold values from 6.3578288e-12 to 1.0172526e-10
- expand_second: float32 [2, 768, 2048], P(None, 'wide', 'narrow'), may hold values from 2.5431315e-11 to 4.0972675e-10
- shrink_second: float32 [2048, 768], P('narrow', 'wide'), may hold values from 2.5431315e-11 to 4.0972675e-10
- bucket_second: float32 [32, 12], replicated, may hold values from 1.1302807e-11 to 1.8084491e-10
- gains_second: float32 [2, 768], P(None, 'wide'), may hold values from 2.8257016e-10 to 4.5211226e-09
Outputs:
- block_output: bfloat16 [12288, 768], P('wide')
- input_gradient: bfloat16 [12288, 768], P('wide')
- global_norm: float32 [], replicated
- new_project: float32 [3, 768, 768], P(None, 'wide', 'narrow')
- new_output: float32 [768, 768], P('narrow', 'wide')
- new_expand: float32 [2, 768, 2048], P(None, 'wide', 'narrow')
- new_shrink: float32 [2048, 768], P('narrow', 'wide')
- new_bucket: float32 [32, 12], replicated
- new_gains: float32 [2, 768], P(None, 'wide')
- project_first_new: float32 [3, 768, 768], P(None, 'wide', 'narrow')
- output_first_new: float32 [768, 768], P('narrow', 'wide')
- expand_first_new: float32 [2, 768, 2048], P(None, 'wide', 'narrow')
- shrink_first_new: float32 [2048, 768], P('narrow', 'wide')
- bucket_first_new: float32 [32, 12], replicated
- gains_first_new: float32 [2, 768], P(None, 'wide')
- project_second_new: float32 [3, 768, 768], P(None, 'wide', 'narrow')
- output_second_new: float32 [768, 768], P('narrow', 'wide')
- expand_second_new: float32 [2, 768, 2048], P(None, 'wide', 'narrow')
- shrink_second_new: float32 [2048, 768], P('narrow', 'wide')
- bucket_second_new: float32 [32, 12], replicated
- gains_second_new: float32 [2, 768], P(None, 'wide')
Inputs may be any that keep to these rules, and one draw needn't show every extreme that they name: Each row lists one buffer's passage lengths in packing order, each from 64 to 384, followed by zeros; a row sums to at most 768, and every row holds one passage of exactly 384 tokens.
All inputs are finite; a program needn't handle non-finite values.
Results may differ from a plain program's by a relative error of at most 0.013.
The roundings to bfloat16 on the way count: a program that leaves them out, or rounds other values in their place, can miss the bound.
Values may be sent and summed in bfloat16 or wider, within the bound.
A program may use at most 128 MiB of HBM per device.

v0:
```python
import jax
import jax.numpy as jnp
from jax import lax
from jax.sharding import PartitionSpec as P

DH = 64
STEP = 10


bucket_edges = (12, 16, 23, 32, 46, 64, 91)
norm_eps = 1e-06
clip_limit = 1.0
beta_one = 0.9
beta_two = 0.999
adam_eps = 1e-08
step_rates = (0.06, 0.3, 0.07, 0.06, 1.0, 0.3)
decay_rates = (0.01, 0.01, 0.01, 0.01, 0.0, 0.0)
masked_score = -1000000000.0


def bucket_of(offsets):
    distance = jnp.abs(offsets)
    far_bucket = 8 + sum(((distance >= threshold).astype(jnp.int32) for threshold in bucket_edges))
    return jnp.where(distance < 8, distance, far_bucket) + 16 * (offsets > 0).astype(jnp.int32)


def rms_scale(values):
    return lax.rsqrt(jnp.mean(values * values, axis=-1, keepdims=True) + norm_eps)


def norm_back(values, scale_vec, gain_vec, upstream):
    weighted = upstream * gain_vec
    inner_mean = jnp.mean(weighted * values, axis=-1, keepdims=True)
    return scale_vec * weighted - values * (scale_vec * scale_vec * scale_vec) * inner_mean


def toeplitz_rows(values, length):
    padded = jnp.concatenate([values, jnp.zeros((1,), values.dtype)])
    tiled_flat = jnp.tile(padded, length)[: length * (2 * length - 1)]
    return tiled_flat.reshape(length, 2 * length - 1)[:, length - 1 :]


def diagonal_sums(matrix, length):
    padded = jnp.pad(matrix, ((0, 0), (length - 1, 1)))
    flat_vals = jnp.concatenate([padded.reshape(-1), jnp.zeros((length,), matrix.dtype)])
    return jnp.sum(flat_vals.reshape(length, 2 * length + 1), axis=0)[: 2 * length - 1]


def adam_update(weight, moment_one, moment_two, gradient, step_rate, decay_rate):
    new_first = beta_one * moment_one + (1.0 - beta_one) * gradient
    new_second = beta_two * moment_two + (1.0 - beta_two) * gradient * gradient
    first_hat = new_first / (1.0 - beta_one**STEP)
    second_hat = new_second / (1.0 - beta_two**STEP)
    new_weight = weight - step_rate * (
        first_hat / (jnp.sqrt(second_hat) + adam_eps) + decay_rate * weight
    )
    return (new_weight, new_first, new_second)


def body(
    block_input,
    cotangent,
    lengths,
    project_weight,
    output_weight,
    expand_weight,
    shrink_weight,
    bucket_bias,
    norm_gains,
    project_first,
    output_first,
    expand_first,
    shrink_first,
    bucket_first,
    gains_first,
    project_second,
    output_second,
    expand_second,
    shrink_second,
    bucket_second,
    gains_second,
):
    tokens, model_width = block_input.shape
    buffers = lengths.shape[0]
    length = tokens // buffers
    head_width = project_weight.shape[2]
    heads_local = head_width // DH
    hidden_local = expand_weight.shape[2]
    low_gains = norm_gains.astype(jnp.bfloat16)
    project_all, output_all, expand_all, shrink_all, gains_all = (
        lax.all_gather(project_weight.astype(jnp.bfloat16), "wide", axis=1, tiled=True),
        lax.all_gather(output_weight.astype(jnp.bfloat16), "wide", axis=1, tiled=True),
        lax.all_gather(expand_weight.astype(jnp.bfloat16), "wide", axis=1, tiled=True),
        lax.all_gather(shrink_weight.astype(jnp.bfloat16), "wide", axis=1, tiled=True),
        lax.all_gather(low_gains, "wide", axis=1, tiled=True),
    )
    gain_one = gains_all[0].astype(jnp.float32)
    gain_two = gains_all[1].astype(jnp.float32)
    positions = jnp.arange(length, dtype=jnp.int32)
    segment_ends = jnp.cumsum(lengths, axis=1)
    segment_ids = jnp.sum(
        (positions[None, :, None] >= segment_ends[:, None, :]).astype(jnp.int32), axis=2
    )
    offsets = jnp.arange(2 * length - 1, dtype=jnp.int32) - (length - 1)
    onehot = (
        bucket_of(offsets)[:, None] == jnp.arange(bucket_bias.shape[0], dtype=jnp.int32)[None, :]
    ).astype(jnp.float32)
    head_start = lax.axis_index("narrow") * heads_local
    bias_local = lax.dynamic_slice_in_dim(bucket_bias, head_start, heads_local, 1)
    head_bias = jnp.dot(onehot, bias_local, precision=lax.Precision.HIGHEST).T
    input_float = block_input.astype(jnp.float32)
    scale_one = rms_scale(input_float)
    normed_one = (input_float * scale_one * gain_one).astype(jnp.bfloat16)
    project_flat = jnp.transpose(project_all, (1, 0, 2)).reshape(model_width, 3 * head_width)
    qkv_rows = jnp.dot(normed_one, project_flat, preferred_element_type=jnp.float32).astype(
        jnp.bfloat16
    )
    buffer_rows = qkv_rows.reshape(buffers, length, 3 * head_width)

    def head_scores(query_rows, key_rows, bias_row, same_segment):
        scores = jnp.einsum("qd,kd->qk", query_rows, key_rows, preferred_element_type=jnp.float32)
        scores = scores + toeplitz_rows(bias_row, length)
        return jnp.where(same_segment, scores, masked_score)

    def split_heads(block_rows):
        return block_rows.reshape(length, 3, heads_local, DH).transpose(1, 2, 0, 3)

    def buffer_forward(block_items):
        block_rows, segment_row = block_items
        pieces = split_heads(block_rows)
        same_segment = segment_row[:, None] == segment_row[None, :]

        def head_forward(head_items):
            query_rows, key_rows, value_rows, bias_row = head_items
            scores = head_scores(query_rows, key_rows, bias_row, same_segment)
            row_max = jnp.max(scores, axis=1, keepdims=True)
            log_total = row_max + jnp.log(jnp.sum(jnp.exp(scores - row_max), axis=1, keepdims=True))
            attention_probs = jnp.exp(scores - log_total).astype(jnp.bfloat16)
            head_out = jnp.dot(
                attention_probs, value_rows, preferred_element_type=jnp.float32
            ).astype(jnp.bfloat16)
            return (head_out, log_total[:, 0])

        head_outs, log_rows = lax.map(head_forward, (pieces[0], pieces[1], pieces[2], head_bias))
        return (head_outs.transpose(1, 0, 2).reshape(length, head_width), log_rows)

    attended, log_totals = lax.map(buffer_forward, (buffer_rows, segment_ids))
    attended = attended.reshape(tokens, head_width)
    attention_terms = jnp.dot(attended, output_all, preferred_element_type=jnp.float32)
    middle = input_float + lax.psum(attention_terms, "narrow")
    scale_two = rms_scale(middle)
    normed_two = (middle * scale_two * gain_two).astype(jnp.bfloat16)
    expand_flat = jnp.transpose(expand_all, (1, 0, 2)).reshape(model_width, 2 * hidden_local)
    gate_up = jnp.dot(normed_two, expand_flat, preferred_element_type=jnp.float32)
    gate_pre = gate_up[:, :hidden_local]
    up_pre = gate_up[:, hidden_local:]
    activated, gelu_pull = jax.vjp(
        lambda gate_vals: jax.nn.gelu(gate_vals, approximate=True), gate_pre
    )
    hidden = (activated * up_pre).astype(jnp.bfloat16)
    feedforward_terms = jnp.dot(hidden, shrink_all, preferred_element_type=jnp.float32)
    block_output = (
        middle + lax.psum(feedforward_terms.astype(jnp.bfloat16), "narrow").astype(jnp.float32)
    ).astype(jnp.bfloat16)
    cotangent_float = cotangent.astype(jnp.float32)
    shrink_grad = jnp.einsum("tf,td->fd", hidden, cotangent, preferred_element_type=jnp.float32)
    d_hidden = jnp.einsum("td,fd->tf", cotangent, shrink_all, preferred_element_type=jnp.float32)
    d_gate = gelu_pull(d_hidden * up_pre)[0]
    d_up = d_hidden * activated
    d_gate_up = jnp.concatenate([d_gate, d_up], axis=1).astype(jnp.bfloat16)
    expand_grad = jnp.einsum("td,tf->df", normed_two, d_gate_up, preferred_element_type=jnp.float32)
    expand_grad = expand_grad.reshape(model_width, 2, hidden_local).transpose(1, 0, 2)
    second_terms = jnp.einsum(
        "tf,df->td", d_gate_up, expand_flat, preferred_element_type=jnp.float32
    )
    d_normed_two = lax.psum(second_terms, "narrow")
    gain_two_grad = jnp.sum(d_normed_two * middle * scale_two, axis=0)
    d_middle = cotangent_float + norm_back(middle, scale_two, gain_two, d_normed_two)
    d_middle_low = d_middle.astype(jnp.bfloat16)
    output_grad = jnp.einsum(
        "th,td->hd", attended, d_middle_low, preferred_element_type=jnp.float32
    )
    d_attended = jnp.einsum(
        "td,hd->th", d_middle_low, output_all, preferred_element_type=jnp.float32
    ).astype(jnp.bfloat16)

    def buffer_backward(block_items):
        block_rows, segment_row, log_row, grad_rows = block_items
        pieces = split_heads(block_rows)
        same_segment = segment_row[:, None] == segment_row[None, :]
        grad_heads = grad_rows.reshape(length, heads_local, DH).transpose(1, 0, 2)

        def head_backward(head_items):
            query_rows, key_rows, value_rows, bias_row, log_head, grad_head = head_items
            scores = head_scores(query_rows, key_rows, bias_row, same_segment)
            attention_probs = jnp.exp(scores - log_head[:, None])
            grad_probs = jnp.einsum(
                "qd,kd->qk", grad_head, value_rows, preferred_element_type=jnp.float32
            )
            grad_scores = (
                attention_probs
                * (grad_probs - jnp.sum(attention_probs * grad_probs, axis=1, keepdims=True))
            ).astype(jnp.bfloat16)
            grad_query = jnp.dot(grad_scores, key_rows, preferred_element_type=jnp.float32)
            grad_key = jnp.einsum(
                "qk,qd->kd", grad_scores, query_rows, preferred_element_type=jnp.float32
            )
            grad_value = jnp.einsum(
                "qk,qd->kd",
                attention_probs.astype(jnp.bfloat16),
                grad_head,
                preferred_element_type=jnp.float32,
            )
            grad_bias = diagonal_sums(grad_scores.astype(jnp.float32), length)
            return (jnp.stack([grad_query, grad_key, grad_value]).astype(jnp.bfloat16), grad_bias)

        grad_pieces, grad_biases = lax.map(
            head_backward, (pieces[0], pieces[1], pieces[2], head_bias, log_row, grad_heads)
        )
        return (grad_pieces.transpose(2, 1, 0, 3).reshape(length, 3 * head_width), grad_biases)

    grad_qkv, bias_rows = lax.map(
        buffer_backward,
        (buffer_rows, segment_ids, log_totals, d_attended.reshape(buffers, length, head_width)),
    )
    grad_qkv = grad_qkv.reshape(tokens, 3 * head_width)
    project_grad = jnp.einsum("td,tc->dc", normed_one, grad_qkv, preferred_element_type=jnp.float32)
    project_grad = project_grad.reshape(model_width, 3, head_width).transpose(1, 0, 2)
    first_terms = jnp.einsum(
        "tc,dc->td", grad_qkv, project_flat, preferred_element_type=jnp.float32
    )
    d_normed_one = lax.psum(first_terms, "narrow")
    gain_one_grad = jnp.sum(d_normed_one * input_float * scale_one, axis=0)
    input_gradient = (d_middle + norm_back(input_float, scale_one, gain_one, d_normed_one)).astype(
        jnp.bfloat16
    )
    local_bucket = jnp.einsum(
        "hr,rb->bh", jnp.sum(bias_rows, axis=0), onehot, precision=lax.Precision.HIGHEST
    )
    bucket_full = lax.dynamic_update_slice(
        jnp.zeros(bucket_bias.shape, jnp.float32), local_bucket, (jnp.int32(0), head_start)
    )
    project_red, output_red, expand_red, shrink_red, gains_red = (
        lax.psum_scatter(project_grad, "wide", scatter_dimension=1, tiled=True),
        lax.psum_scatter(output_grad, "wide", scatter_dimension=1, tiled=True),
        lax.psum_scatter(expand_grad, "wide", scatter_dimension=1, tiled=True),
        lax.psum_scatter(shrink_grad, "wide", scatter_dimension=1, tiled=True),
        lax.psum_scatter(
            jnp.stack([gain_one_grad, gain_two_grad]), "wide", scatter_dimension=1, tiled=True
        ),
    )
    square_sum = sum(
        (
            jnp.sum(part_grad * part_grad)
            for part_grad in (project_red, output_red, expand_red, shrink_red)
        )
    )
    square_sum = square_sum + jnp.where(
        lax.axis_index("narrow") == 0, jnp.sum(gains_red * gains_red), 0.0
    )
    square_total, bucket_grad = lax.psum((square_sum, bucket_full), ("wide", "narrow"))
    global_norm = jnp.sqrt(square_total + jnp.sum(bucket_grad * bucket_grad))
    factor = jnp.minimum(1.0, clip_limit / (global_norm + 1e-06))
    params = (project_weight, output_weight, expand_weight, shrink_weight, bucket_bias, norm_gains)
    firsts = (project_first, output_first, expand_first, shrink_first, bucket_first, gains_first)
    seconds = (
        project_second,
        output_second,
        expand_second,
        shrink_second,
        bucket_second,
        gains_second,
    )
    reduced = (project_red, output_red, expand_red, shrink_red, bucket_grad, gains_red)
    results = [
        adam_update(weight, moment_one, moment_two, factor * gradient, step_rate, decay_rate)
        for weight, moment_one, moment_two, gradient, step_rate, decay_rate in zip(
            params, firsts, seconds, reduced, step_rates, decay_rates
        )
    ]
    return (
        block_output,
        input_gradient,
        global_norm,
        results[0][0],
        results[1][0],
        results[2][0],
        results[3][0],
        results[4][0],
        results[5][0],
        results[0][1],
        results[1][1],
        results[2][1],
        results[3][1],
        results[4][1],
        results[5][1],
        results[0][2],
        results[1][2],
        results[2][2],
        results[3][2],
        results[4][2],
        results[5][2],
    )


def solution(mesh):
    in_specs = (
        P("wide", None),
        P("wide", None),
        P("wide", None),
        P(None, "wide", "narrow"),
        P("narrow", "wide"),
        P(None, "wide", "narrow"),
        P("narrow", "wide"),
        P(),
        P(None, "wide"),
        P(None, "wide", "narrow"),
        P("narrow", "wide"),
        P(None, "wide", "narrow"),
        P("narrow", "wide"),
        P(),
        P(None, "wide"),
        P(None, "wide", "narrow"),
        P("narrow", "wide"),
        P(None, "wide", "narrow"),
        P("narrow", "wide"),
        P(),
        P(None, "wide"),
    )
    out_specs = (
        P("wide", None),
        P("wide", None),
        P(),
        P(None, "wide", "narrow"),
        P("narrow", "wide"),
        P(None, "wide", "narrow"),
        P("narrow", "wide"),
        P(),
        P(None, "wide"),
        P(None, "wide", "narrow"),
        P("narrow", "wide"),
        P(None, "wide", "narrow"),
        P("narrow", "wide"),
        P(),
        P(None, "wide"),
        P(None, "wide", "narrow"),
        P("narrow", "wide"),
        P(None, "wide", "narrow"),
        P("narrow", "wide"),
        P(),
        P(None, "wide"),
    )
    return jax.shard_map(body, mesh=mesh, in_specs=in_specs, out_specs=out_specs, check_vma=False)
```

profile of v0, /device:TPU:0, one launch (start us, length us, event | category | flops | bytes accessed | tf_op | source)
XLA Modules:
  0.0 1325.8 jit_solution(2225824823571973719)
XLA Ops:
  9.7 22.1 %all-gather = bf16[8,96,2]{1,2,0:T(2,128)(2,1)S(1)} all-gather(bf16[1,96,2]{1,2,0:T(2,128)(2,1)S(1)} %convert_bitcast_fusion), channel_id=1, replica_groups=mesh['wide'=8,'narrow'=4] {'wide'}, dimensions={0}, use_global_device_ids=true | all-gather | bytes 3456 | tf_op jit(solution)/shard_map/all_gather | solution.py:95
  38.3 33.1 %all_gather.17 = bf16[192,768]{0,1:T(8,128)(2,1)} all-gather(bf16[192,96]{0,1:T(8,128)(2,1)S(1)} %copy.186), channel_id=1, replica_groups=mesh['wide'=8,'narrow'=4] {'wide'}, dimensions={1}, use_global_device_ids=true | all-gather | bytes 331776 | tf_op jit(solution)/shard_map/all_gather | solution.py:92
  71.5 35.7 %all_gather.16 = bf16[3,768,192]{2,0,1:T(4,128)(2,1)} all-gather(bf16[3,96,192]{2,0,1:T(4,128)(2,1)S(1)} %copy.181), channel_id=1, replica_groups=mesh['wide'=8,'narrow'=4] {'wide'}, dimensions={1}, use_global_device_ids=true | all-gather | bytes 995328 | tf_op jit(solution)/shard_map/all_gather | solution.py:91
  114.7 152.8 %while.65 = (s32[]{:T(128)}, bf16[2,768,192]{1,2,0:T(8,128)(2,1)}, f32[2,3,768]{2,1,0:T(4,128)}, bf16[2,768,576]{1,2,0:T(8,128)(2,1)}, s32[2,768]{1,0:T(2,128)},...) while((s32[]{:T(128)}, bf16[2,768,192]{1,2,0:T(8,128)(2,1)}, ...), condition=%wide.region_8.9_spmd, body=%wide.region_3.8_spmd.sunk | while | flops 155763456 | bytes 47086936 | solution.py:147
  116.7 73.0 %while.68 = (s32[]{:T(128)}, bf16[3,768,64]{1,2,0:T(8,128)(2,1)S(1)}, f32[3,768]{1,0:T(4,128)S(1)}, bf16[3,768,64]{1,2,0:T(8,128)(2,1)S(1)}, bf16[3,768,64]{1,2,...) while((s32[]{:T(128)}, ...), condition=%wide.region_7.7_spmd.clone, body=%wide.region_4.6_spmd.clone.sunk | while | flops 155763456 | bytes 42930292 | solution.py:144
  193.1 73.0 %while.68 = (s32[]{:T(128)}, bf16[3,768,64]{1,2,0:T(8,128)(2,1)S(1)}, f32[3,768]{1,0:T(4,128)S(1)}, bf16[3,768,64]{1,2,0:T(8,128)(2,1)S(1)}, bf16[3,768,64]{1,2,...) while((s32[]{:T(128)}, ...), condition=%wide.region_7.7_spmd.clone, body=%wide.region_4.6_spmd.clone.sunk | while | flops 155763456 | bytes 42930292 | solution.py:144
  275.6 33.6 %all_gather.19 = bf16[512,768]{0,1:T(8,128)(2,1)S(1)} all-gather(bf16[512,96]{0,1:T(8,128)(2,1)S(1)} %convert_element_type.180), channel_id=1, replica_groups=mesh['wide'=8,'narrow'=4] {'wide'}, dimensions={1}, use_global_device_ids=true | all-gather | bytes 884736 | tf_op jit(solution)/shard_map/all_gather | solution.py:94
  309.2 57.2 %all-reduce.8.cloned.1.call-done = f32[1536,768]{1,0:T(8,128)} async-done(((f32[1536,768]{1,0:T(8,128)}), f32[1536,768]{1,0:T(8,128)}) %all-reduce.8.cloned.1.call-update) | async-done | bytes 4718608 | tf_op jit(solution)/shard_map/psum | solution.py:150
  397.1 89.9 %all-reduce.12.cloned.1.call-done = f32[1536,768]{1,0:T(8,128)} async-done(((f32[1536,768]{1,0:T(8,128)}), f32[1536,768]{1,0:T(8,128)}) %all-reduce.12.cloned.1.call-update) | async-done | bytes 4718608 | tf_op jit(solution)/shard_map/psum | solution.py:176
  492.1 53.7 %all-reduce.10.cloned.1.call-done = bf16[1536,768]{1,0:T(8,128)(2,1)} async-done(((bf16[1536,768]{1,0:T(8,128)(2,1)}), bf16[1536,768]{1,0:T(8,128)(2,1)}) %all-reduce.10.cloned.1.call-update) | async-done | bytes 2359312 | tf_op jit(solution)/shard_map/psum | solution.py:163
  554.5 346.1 %while.67 = (s32[]{:T(128)}, bf16[2,768,576]{1,2,0:T(8,128)(2,1)}, f32[2,3,1535]{2,1,0:T(4,128)}, bf16[2,768,576]{1,2,0:T(8,128)(2,1)}, f32[2,3,768]{2,1,0:T(4,1...) while((s32[]{:T(128)}, bf16[2,768,576]{1,2,0:T(8,128)(2,1)}, ...), condition=%wide.region_19.20_spmd, body=%wide.region_14.19_spmd.sunk | while | flops 386777856 | bytes 102011568 | solution.py:222
  559.0 165.0 %while.69 = (s32[]{:T(128)}, bf16[3,3,768,64]{2,3,0,1:T(8,128)(2,1)}, f32[3,1535]{1,0:T(4,128)}, bf16[3,768,64]{1,2,0:T(8,128)(2,1)S(1)}, bf16[3,768,64]{1,2,0:T...) while((s32[]{:T(128)}, ...), condition=%wide.region_18.18_spmd.clone, body=%wide.region_15.17_spmd.clone.sunk | while | flops 386777856 | bytes 96039304 | solution.py:217
  601.5 8.2 reshape.315
  656.5 8.2 reshape.315
  711.5 8.2 reshape.315
  731.8 165.0 %while.69 = (s32[]{:T(128)}, bf16[3,3,768,64]{2,3,0,1:T(8,128)(2,1)}, f32[3,1535]{1,0:T(4,128)}, bf16[3,768,64]{1,2,0:T(8,128)(2,1)S(1)}, bf16[3,768,64]{1,2,0:T...) while((s32[]{:T(128)}, ...), condition=%wide.region_18.18_spmd.clone, body=%wide.region_15.17_spmd.clone.sunk | while | flops 386777856 | bytes 96039304 | solution.py:217
  774.4 8.2 reshape.315
  884.4 8.2 reshape.315
  918.2 83.9 %all-reduce.14.cloned.1.call-done = f32[1536,768]{1,0:T(8,128)} async-done(((f32[1536,768]{1,0:T(8,128)}), f32[1536,768]{1,0:T(8,128)}) %all-reduce.14.cloned.1.call-update) | async-done | bytes 4718608 | tf_op jit(solution)/shard_map/psum | solution.py:232
  1035.0 8.6 reduce-scatter.18.cloned.1.call-done
  1045.2 62.9 %reduce-scatter.20.cloned.1.call-done = f32[96,2]{1,0:T(8,128)} async-done(((f32[768,2]{1,0:T(8,128)}), f32[96,2]{1,0:T(8,128)}) %reduce-scatter.20.cloned.1.call-update) | async-done | bytes 784
  1110.3 67.8 %reduce-scatter.16.cloned.1.call-done = f32[96,576]{1,0:T(8,128)} async-done(((f32[768,576]{1,0:T(8,128)}), f32[96,576]{1,0:T(8,128)}) %reduce-scatter.16.cloned.1.call-update) | async-done | bytes 221200
  1181.3 73.8 %reduce-scatter.12.cloned.1.call-done = f32[2,96,512]{2,1,0:T(8,128)} async-done(((f32[2,768,512]{2,1,0:T(8,128)}), f32[2,96,512]{2,1,0:T(8,128)}) %reduce-scatter.12.cloned.1.call-update) | async-done | bytes 393232 | tf_op jit(solution)/shard_map/reduce_scatter | solution.py:246
  1263.8 39.9 %all-reduce.2 = (f32[]{:T(128)}, f32[32,12]{0,1:T(8,128)S(1)}) all-reduce(f32[]{:T(128)S(6)} %add.321, f32[32,12]{0,1:T(8,128)S(1)} %dynamic_update_slice.47), channel_id=1, replica_groups=mesh['wide'=8,'narrow'=4] {'wide','narrow'}, use_global_device_ids=true, to_apply=%region_34.35 | all-reduce | flops 385 | bytes 3080 | tf_op jit(solution)/shard_map/psum | solution.py:261
  (526 shorter events, 599.0 us)
Async XLA Ops:
  8.0 358.3 %all-reduce.8.cloned.1.call-start = ((), (), s32[]{:S(2)}) async-start(), calls=%async_computation.5 | async-start | bytes 9437184 | tf_op jit(solution)/shard_map/psum | solution.py:150
  8.1 104.7 %copy-start.46 = (s32[1535]{0:T(1024)}, s32[1535]{0:T(1024)S(1)}, u32[]{:S(2)}) copy-start(s32[1535]{0:T(1024)S(1)} %fusion.86) | copy-start | bytes 18424
  32.5 77.3 %copy-start.39 = (f32[768]{0:T(1024)}, f32[768]{0:T(1024)S(1)}, u32[]{:S(2)}) copy-start(f32[768]{0:T(1024)S(1)} %get-tuple-element.696) | copy-start | bytes 9220
  35.5 74.3 %copy-start.9 = (bf16[1536,768]{1,0:T(8,128)(2,1)S(1)}, bf16[1536,768]{1,0:T(8,128)(2,1)}, u32[]{:S(2)}) copy-start(bf16[1536,768]{1,0:T(8,128)(2,1)} %param.29) | copy-start | bytes 7077892
  36.1 75.3 %copy-start.34 = (f32[1536]{0:T(1024)}, f32[1536]{0:T(1024)S(1)}, u32[]{:S(2)}) copy-start(f32[1536]{0:T(1024)S(1)} %get-tuple-element.799) | copy-start | bytes 18436
  273.5 92.8 %copy-start.10 = (bf16[1536,768]{1,0:T(8,128)(2,1)S(1)}, bf16[1536,768]{1,0:T(8,128)(2,1)}, u32[]{:S(2)}) copy-start(bf16[1536,768]{1,0:T(8,128)(2,1)} %param.29) | copy-start | bytes 7077892
  273.5 98.0 %all-gather.3.cloned.1.call-start = ((), (), s32[]{:S(2)}) async-start(), calls=%async_computation.6 | async-start | bytes 1769472 | tf_op jit(solution)/shard_map/all_gather | solution.py:93
  275.5 211.5 %all-reduce.12.cloned.1.call-start = ((), (), s32[]{:S(2)}) async-start(), calls=%async_computation.8 | async-start | bytes 9437184 | tf_op jit(solution)/shard_map/psum | solution.py:176
  371.5 174.3 %copy-start.36 = (f32[1536]{0:T(1024)}, f32[1536]{0:T(1024)S(1)}, u32[]{:S(2)}) copy-start(f32[1536]{0:T(1024)S(1)} %get-tuple-element.801) | copy-start | bytes 18436
  392.7 153.1 %all-reduce.10.cloned.1.call-start = ((), (), s32[]{:S(2)}) async-start(), calls=%async_computation.7 | async-start | bytes 4718592 | tf_op jit(solution)/shard_map/psum | solution.py:163
  397.0 605.0 %all-reduce.14.cloned.1.call-start = ((), (), s32[]{:S(2)}) async-start(), calls=%async_computation.9 | async-start | bytes 9437184 | tf_op jit(solution)/shard_map/psum | solution.py:232
  907.7 125.6 %reduce-scatter.14.cloned.1.call-start = ((), (), s32[]{:S(2)}) async-start(), calls=%async_computation.11 | async-start | bytes 1769472 | tf_op jit(solution)/shard_map/reduce_scatter | solution.py:247
  913.4 88.6 %copy-start.11 = (bf16[1536,768]{1,0:T(8,128)(2,1)S(1)}, bf16[1536,768]{1,0:T(8,128)(2,1)}, u32[]{:S(2)}) copy-start(bf16[1536,768]{1,0:T(8,128)(2,1)} %param.29) | copy-start | bytes 7077892
  913.4 88.6 %copy-start.35 = (f32[1536]{0:T(1024)S(1)}, f32[1536]{0:T(1024)}, u32[]{:S(2)}) copy-start(f32[1536]{0:T(1024)} %copy-done.34) | copy-start | bytes 18436
  913.4 88.6 %copy-start.40 = (f32[768]{0:T(1024)S(1)}, f32[768]{0:T(1024)}, u32[]{:S(2)}) copy-start(f32[768]{0:T(1024)} %copy-done.39) | copy-start | bytes 9220
  913.4 130.2 %reduce-scatter.18.cloned.1.call-start = ((), (), s32[]{:S(2)}) async-start(), calls=%async_computation.13 | async-start | bytes 884736
  918.1 190.1 %reduce-scatter.20.cloned.1.call-start = ((), (), s32[]{:S(2)}) async-start(), calls=%async_computation.14 | async-start | bytes 442368
  1006.8 171.3 %reduce-scatter.16.cloned.1.call-start = ((), (), s32[]{:S(2)}) async-start(), calls=%async_computation.12 | async-start | bytes 2211840
  1020.3 234.9 %reduce-scatter.12.cloned.1.call-start = ((), (), s32[]{:S(2)}) async-start(), calls=%async_computation.10 | async-start | bytes 3538944 | tf_op jit(solution)/shard_map/reduce_scatter | solution.py:246
  1028.9 229.3 %copy-start.43 = (f32[1536]{0:T(1024)S(1)}, f32[1536]{0:T(1024)}, u32[]{:S(2)}) copy-start(f32[1536]{0:T(1024)} %get-tuple-element.798) | copy-start | bytes 18436
  1109.0 149.2 %copy-start.48 = (f32[2,96]{1,0:T(2,128)}, f32[2,96]{1,0:T(2,128)S(1)}, u32[]{:S(2)}) copy-start(f32[2,96]{1,0:T(2,128)S(1)} %copy.205) | copy-start | bytes 2308
  1263.7 49.2 %copy-start.27 = (f32[512,96]{0,1:T(8,128)S(1)}, f32[512,96]{0,1:T(8,128)}, u32[]{:S(2)}) copy-start(f32[512,96]{0,1:T(8,128)} %param.35) | copy-start | bytes 589828
  1263.8 51.0 %copy-start.20 = (f32[2,96,512]{2,1,0:T(8,128)S(1)}, f32[2,96,512]{2,1,0:T(8,128)}, u32[]{:S(2)}) copy-start(f32[2,96,512]{2,1,0:T(8,128)} %param.34) | copy-start | bytes 1179652
  1263.8 51.0 %copy-start.21 = (f32[2,96,512]{2,1,0:T(8,128)S(1)}, f32[2,96,512]{2,1,0:T(8,128)}, u32[]{:S(2)}) copy-start(f32[2,96,512]{2,1,0:T(8,128)} %reduce-scatter.12.cloned.1.call-done) | copy-start | bytes 1179652
  (77 other events, 831.4 us)
Sparse Core Ops, SparseCore 0:
  273.7 92.6 all-reduce.7
  392.8 94.1 all-reduce.11
  490.0 55.8 all-reduce.9
  907.8 94.1 all-reduce.13
Sparse Core Ops, SparseCore 1:
  276.8 44.0 all-gather.2
  913.5 65.2 reduce-scatter.13
  982.2 61.3 reduce-scatter.17
  1047.4 60.6 reduce-scatter.19
  1112.2 65.8 reduce-scatter.15
  1182.1 73.0 reduce-scatter.11
where the time goes:
time: 1340 us; the launch traced here: 1330 us
  waiting for transfers between devices  498 us (37%)
  local copies, waits for them, and re-layouts  451 us (34%)
  blocking collectives  164 us (12%)
  matrix products  99.9 us (7%)
  other arithmetic  88 us (7%)
  between operations  22.1 us (2%)
    unnamed x13, waiting for transfers between devices  140 us
    another operation x24, local copies, waits for them, and re-layouts, toeplitz_rows(): tiled_flat = jnp.tile(padded, length)[:length * (2 * length - 1)]  100 us
    reshape x12, local copies, waits for them, and re-layouts, toeplitz_rows(): return tiled_flat.reshape(length, 2 * length - 1)[:, length - 1:]  92.6 us
    psum x1, waiting for transfers between devices, body(): d_normed_two = lax.psum(second_terms, 'narrow')  89.9 us
    psum x1, waiting for transfers between devices, body(): d_normed_one = lax.psum(first_terms, 'narrow')  83.9 us
    reduce_scatter x1, waiting for transfers between devices, body(): lax.psum_scatter(expand_grad, 'wide', scatter_dimension=1, tiled=True)  73.8 us
    psum x1, waiting for transfers between devices, body(): middle = input_float + lax.psum(attention_terms, 'narrow')  57.2 us
    psum x1, waiting for transfers between devices, body(): lax.psum(feedforward_terms.astype(jnp.bfloat16), 'narrow')  53.7 us
  transfers between devices with their start and end apart: 10, of which 8 were waited for; matrix products, arithmetic and copies ran while one was open for 5% of the time, Pallas kernels for 0%

commit v1 on v0

v1 whole, which is shorter than its diff:
```python
import functools

import jax
import jax.numpy as jnp
from jax import lax
from jax.experimental import pallas as pl
from jax.experimental.pallas import tpu as pltpu
from jax.sharding import PartitionSpec as P

DH = 64
STEP = 10
LANES = 128
MESH = pl.DeviceIdType.MESH
F32 = jnp.float32
BF16 = jnp.bfloat16
ANY = pl.ANY

bucket_edges = (12, 16, 23, 32, 46, 64, 91)
norm_eps = 1e-06
clip_limit = 1.0
beta_one = 0.9
beta_two = 0.999
adam_eps = 1e-08
step_rates = (0.06, 0.3, 0.07, 0.06, 1.0, 0.3)
decay_rates = (0.01, 0.01, 0.01, 0.01, 0.0, 0.0)
masked_score = -1000000000.0
VMEM_LIMIT = 58 << 20

NN = (((1,), (0,)), ((), ()))
NT = (((1,), (1,)), ((), ()))
TN = (((0,), (0,)), ((), ()))


def mm(left, right, dims=NN):
    return lax.dot_general(left, right, dims, preferred_element_type=F32)


def bucket_of(offsets):
    distance = jnp.abs(offsets)
    far_bucket = 8 + sum(((distance >= threshold).astype(jnp.int32) for threshold in bucket_edges))
    return jnp.where(distance < 8, distance, far_bucket) + 16 * (offsets > 0).astype(jnp.int32)


def rms_scale(values):
    return lax.rsqrt(jnp.mean(values * values, axis=-1, keepdims=True) + norm_eps)


def norm_back(values, scale_vec, gain_vec, upstream):
    weighted = upstream * gain_vec
    inner_mean = jnp.mean(weighted * values, axis=-1, keepdims=True)
    return scale_vec * weighted - values * (scale_vec * scale_vec * scale_vec) * inner_mean


def adam_update(weight, moment_one, moment_two, gradient, step_rate, decay_rate):
    new_first = beta_one * moment_one + (1.0 - beta_one) * gradient
    new_second = beta_two * moment_two + (1.0 - beta_two) * gradient * gradient
    first_hat = new_first / (1.0 - beta_one**STEP)
    second_hat = new_second / (1.0 - beta_two**STEP)
    new_weight = weight - step_rate * (
        first_hat / (jnp.sqrt(second_hat) + adam_eps) + decay_rate * weight
    )
    return (new_weight, new_first, new_second)


def fold_rows(values):
    rows, cols = values.shape
    return jnp.sum(values.reshape(rows // 8, 8, cols), axis=0)


def start_rows(pieces, target, offs_ref, sems):
    copies = []
    for at, piece in enumerate(pieces):
        rows = piece.shape[0]
        begin = pl.multiple_of(offs_ref[at], 16)
        copies.append(
            pltpu.make_async_copy(piece, target.at[pl.ds(begin, rows)], sems.at[at])
        )
    for copy in copies:
        copy.start()
    return copies


def segments(index, ends_ref, buffer, slots):
    total = jnp.zeros(index.shape, jnp.int32)
    for slot in range(slots):
        total = total + (index >= ends_ref[buffer, slot]).astype(jnp.int32)
    return total


def params(**more):
    return pltpu.CompilerParams(vmem_limit_bytes=VMEM_LIMIT, **more)


def attend_kernel(
    buffer, slots, heads, count, ends_ref, offs_ref, x_ref, strip_ref, *refs
):
    pieces = refs[:count]
    normed_ref, qkv_ref, att_ref, log_ref, gains_ref, wbuf, qs, ks, vs, os, sems = refs[count:]
    length, width = x_ref.shape
    head_cols = heads * DH
    copies = start_rows(pieces, wbuf, offs_ref, sems)
    for copy in copies:
        copy.wait()
    gain_cols = wbuf[:, 4 * LANES :].astype(F32).T
    first = 3 * head_cols - 4 * LANES
    gains = gain_cols[first : first + 8]
    gains_ref[...] = gains
    gain_one = gains[0:1]
    step = 256

    @pl.loop(0, length // step)
    def _(block):
        rows = pl.ds(pl.multiple_of(block * step, step), step)
        values = x_ref[rows].astype(F32)
        normed = (values * rms_scale(values) * gain_one).astype(BF16)
        normed_ref[rows] = normed
        qkv = mm(normed, wbuf[...]).astype(BF16)
        qkv_ref[rows] = qkv[:, : 3 * head_cols]
        for h in range(heads):
            qs[h, rows] = qkv[:, h * DH : (h + 1) * DH]
            ks[h, rows] = qkv[:, head_cols + h * DH : head_cols + (h + 1) * DH]
            vs[h, rows] = qkv[:, 2 * head_cols + h * DH : 2 * head_cols + (h + 1) * DH]

    blocks = length // LANES
    seg_keys = segments(
        lax.broadcasted_iota(jnp.int32, (1, length), 1), ends_ref, buffer, slots
    )

    @pl.loop(0, blocks)
    def _(block):
        begin = pl.multiple_of(block * LANES, LANES)
        rows = pl.ds(begin, LANES)
        window = pl.ds(pl.multiple_of((blocks - 1 - block) * LANES, LANES), length)
        seg_rows = segments(
            lax.broadcasted_iota(jnp.int32, (LANES, 1), 0) + begin, ends_ref, buffer, slots
        )
        same = seg_rows == seg_keys
        lane = lax.broadcasted_iota(jnp.int32, (LANES, LANES), 1)
        logs = jnp.zeros((LANES, LANES), F32)
        for h in range(heads):
            scores = mm(qs[h, rows], ks[h], NT) + strip_ref[h, :, window]
            scores = jnp.where(same, scores, masked_score)
            row_max = jnp.max(scores, axis=1, keepdims=True)
            raised = jnp.exp(scores - row_max)
            total = jnp.sum(raised, axis=1, keepdims=True)
            probs = (raised * (1.0 / total)).astype(BF16)
            os[h, rows] = mm(probs, vs[h]).astype(BF16)
            logs = jnp.where(lane == h, row_max + jnp.log(total), logs)
        log_ref[rows] = logs

    att_ref[...] = jnp.concatenate([os[h] for h in range(heads)], axis=1)


def attend(buffer, ends, offs, x, strip, pieces, length, heads):
    width = x.shape[1]
    count = len(pieces)
    cols = pieces[0].shape[1]
    head_cols = heads * DH
    whole = lambda i, *_: (0, 0)
    spec = pltpu.PrefetchScalarGridSpec(
        num_scalar_prefetch=2,
        grid=(1,),
        in_specs=[
            pl.BlockSpec((length, width), lambda i, *_: (buffer, 0)),
            pl.BlockSpec(strip.shape, lambda i, *_: (0, 0, 0)),
        ]
        + [pl.BlockSpec(memory_space=ANY)] * count,
        out_specs=[
            pl.BlockSpec((length, width), whole),
            pl.BlockSpec((length, 3 * head_cols), whole),
            pl.BlockSpec((length, head_cols), whole),
            pl.BlockSpec((length, LANES), whole),
            pl.BlockSpec((8, width), whole),
        ],
        scratch_shapes=[
            pltpu.VMEM((width, cols), BF16),
            pltpu.VMEM((heads, length, DH), BF16),
            pltpu.VMEM((heads, length, DH), BF16),
            pltpu.VMEM((heads, length, DH), BF16),
            pltpu.VMEM((heads, length, DH), BF16),
            pltpu.SemaphoreType.DMA((count,)),
        ],
    )
    flops = 2 * length * (width * cols + 2 * heads * DH * length)
    return pl.pallas_call(
        functools.partial(attend_kernel, buffer, ends.shape[1], heads, count),
        grid_spec=spec,
        out_shape=[
            jax.ShapeDtypeStruct((length, width), BF16),
            jax.ShapeDtypeStruct((length, 3 * head_cols), BF16),
            jax.ShapeDtypeStruct((length, head_cols), BF16),
            jax.ShapeDtypeStruct((length, LANES), F32),
            jax.ShapeDtypeStruct((8, width), F32),
        ],
        compiler_params=params(),
        cost_estimate=pl.CostEstimate(
            flops=4 * flops, bytes_accessed=8 << 20, transcendentals=heads * length * length
        ),
        name="attend",
    )(ends, offs, x, strip, *pieces)


def feed_kernel(hidden_cols, counts, order_ref, offs_ref, *refs):
    own, across, beside, diagonal, x_ref, cot_ref, gains_ref = refs[:7]
    at = 7
    groups = []
    for count in counts:
        groups.append(refs[at : at + count])
        at += count
    (
        normed_ref,
        hidden_ref,
        gate_ref,
        ff_send,
        ff_keep,
        dn_send,
        dn_keep,
        middle_keep,
        gain_sum,
        ebuf,
        sbuf,
        oabuf,
        obbuf,
        sems,
    ) = refs[at:]
    step = pl.program_id(0)
    bufs = (oabuf, obbuf, ebuf, sbuf)

    @pl.when(step == 0)
    def _():
        copies = []
        for which, (group, target) in enumerate(zip(groups, bufs)):
            copies += start_rows(group, target, offs_ref, sems.at[which])
        for copy in copies:
            copy.wait()

    cols = own.shape[1]
    upper = order_ref[2] == 0
    pairs = []
    for near, far, weights in ((own, across, oabuf), (beside, diagonal, obbuf)):
        near_sum = mm(near[...], weights[:, :cols], NT)
        far_sum = mm(far[...], weights[:, cols:], NT)
        pairs.append(
            jnp.where(upper, near_sum, far_sum) + jnp.where(upper, far_sum, near_sum)
        )
    swap = order_ref[0] == 0
    attention = jnp.where(swap, pairs[0], pairs[1]) + jnp.where(swap, pairs[1], pairs[0])
    middle = x_ref[...].astype(F32) + attention
    scale_two = rms_scale(middle)
    gain_two = gains_ref[1:2]
    normed = (middle * scale_two * gain_two).astype(BF16)
    normed_ref[...] = normed
    cot = cot_ref[...]
    part = 256
    k0 = 0.7978845608028654
    k1 = 0.044715
    for begin in range(0, hidden_cols, part):
        gate = mm(normed, ebuf[:, begin : begin + part])
        up = mm(normed, ebuf[:, hidden_cols + begin : hidden_cols + begin + part])
        square = gate * gate
        tanh = jnp.tanh(k0 * (gate + k1 * (square * gate)))
        half = 0.5 * (1.0 + tanh)
        active = gate * half
        slope = half + (0.5 * gate) * (1.0 - tanh * tanh) * (k0 + (3.0 * k0 * k1) * square)
        d_hidden = mm(cot, sbuf[:, begin : begin + part])
        hidden_ref[:, begin : begin + part] = (active * up).astype(BF16)
        gate_ref[:, begin : begin + part] = (d_hidden * up * slope).astype(BF16)
        gate_ref[:, hidden_cols + begin : hidden_cols + begin + part] = (
            d_hidden * active
        ).astype(BF16)
    ff = mm(hidden_ref[...], sbuf[...], NT).astype(BF16)
    dn = mm(gate_ref[...], ebuf[...], NT)
    sums = fold_rows(dn * middle * scale_two)
    dn = dn.astype(BF16)

    @pl.when(step == 0)
    def _():
        ff_send[...] = ff
        dn_send[...] = dn
        gain_sum[...] = sums

    @pl.when(step == 1)
    def _():
        ff_keep[...] = ff
        dn_keep[...] = dn
        middle_keep[...] = middle
        gain_sum[...] = gain_sum[...] + sums


def feed(buffer, order, offs, parts, x, cot, gains, groups, length, hidden_cols):
    width = x.shape[1]
    half = length // 2
    cols = parts[0].shape[1]
    counts = [len(group) for group in groups]
    natural = lambda i, order, *_: (order[i], 0)
    rows = lambda i, order, *_: (2 * buffer + order[i], 0)
    whole = lambda i, *_: (0, 0)
    spec = pltpu.PrefetchScalarGridSpec(
        num_scalar_prefetch=2,
        grid=(2,),
        in_specs=[pl.BlockSpec((half, cols), natural)] * 4
        + [pl.BlockSpec((half, width), rows)] * 2
        + [pl.BlockSpec((8, width), whole)]
        + [pl.BlockSpec(memory_space=ANY)] * sum(counts),
        out_specs=[
            pl.BlockSpec((half, width), natural),
            pl.BlockSpec((half, hidden_cols), natural),
            pl.BlockSpec((half, 2 * hidden_cols), natural),
        ]
        + [pl.BlockSpec((half, width), whole)] * 5
        + [pl.BlockSpec((8, width), whole)],
        scratch_shapes=[
            pltpu.VMEM((width, 2 * hidden_cols), BF16),
            pltpu.VMEM((width, hidden_cols), BF16),
            pltpu.VMEM((width, 2 * cols), BF16),
            pltpu.VMEM((width, 2 * cols), BF16),
            pltpu.SemaphoreType.DMA((4, max(counts))),
        ],
    )
    flops = 2 * length * width * (4 * cols + 7 * hidden_cols)
    return pl.pallas_call(
        functools.partial(feed_kernel, hidden_cols, counts),
        grid_spec=spec,
        out_shape=[
            jax.ShapeDtypeStruct((length, width), BF16),
            jax.ShapeDtypeStruct((length, hidden_cols), BF16),
            jax.ShapeDtypeStruct((length, 2 * hidden_cols), BF16),
            jax.ShapeDtypeStruct((half, width), BF16),
            jax.ShapeDtypeStruct((half, width), BF16),
            jax.ShapeDtypeStruct((half, width), BF16),
            jax.ShapeDtypeStruct((half, width), BF16),
            jax.ShapeDtypeStruct((half, width), F32),
            jax.ShapeDtypeStruct((8, width), F32),
        ],
        compiler_params=params(),
        cost_estimate=pl.CostEstimate(
            flops=flops, bytes_accessed=12 << 20, transcendentals=length * hidden_cols
        ),
        name="feed",
    )(order, offs, *parts, x, cot, gains, *[piece for group in groups for piece in group])


def middle_kernel(order_ref, near, far, middle_ref, cot_ref, gains_ref, d_ref, low_ref):
    upstream = near[...].astype(F32) + far[...].astype(F32)
    middle = middle_ref[...]
    d_middle = cot_ref[...].astype(F32) + norm_back(
        middle, rms_scale(middle), gains_ref[1:2], upstream
    )
    d_ref[...] = d_middle
    low_ref[...] = d_middle.astype(BF16)


def input_kernel(order_ref, near, far, x_ref, d_ref, gains_ref, out_ref):
    upstream = near[...].astype(F32) + far[...].astype(F32)
    values = x_ref[...].astype(F32)
    out_ref[...] = (
        d_ref[...] + norm_back(values, rms_scale(values), gains_ref[0:1], upstream)
    ).astype(BF16)


def output_kernel(order_ref, near, far, middle_ref, out_ref):
    out_ref[...] = (
        middle_ref[...] + (near[...].astype(F32) + far[...].astype(F32)).astype(BF16).astype(F32)
    ).astype(BF16)


def half_call(kernel, name, buffer, order, arrays, placed, outs, gains=None):
    half, width = arrays[0].shape
    steps = 3
    block = half // steps
    mine = lambda i, *_: (i, 0)
    rows = lambda i, order, *_: ((2 * buffer + order[1]) * steps + i, 0)
    in_specs = [
        pl.BlockSpec((block, width), rows if at in placed else mine)
        for at in range(len(arrays))
    ]
    operands = list(arrays)
    if gains is not None:
        in_specs.append(pl.BlockSpec((8, width), lambda i, *_: (0, 0)))
        operands.append(gains)
    return pl.pallas_call(
        kernel,
        grid_spec=pltpu.PrefetchScalarGridSpec(
            num_scalar_prefetch=1,
            grid=(steps,),
            in_specs=in_specs,
            out_specs=[pl.BlockSpec((block, width), mine) for _ in outs],
        ),
        out_shape=[jax.ShapeDtypeStruct((half, width), kind) for kind in outs],
        compiler_params=params(),
        cost_estimate=pl.CostEstimate(
            flops=20 * half * width, bytes_accessed=12 * half * width, transcendentals=0
        ),
        name=name,
    )(order, *operands)


def back_kernel(buffer, slots, heads, counts, ends_ref, offs_ref, order_ref, *refs):
    near, far, qkv_ref, log_ref, strip_ref, x_ref = refs[:6]
    at = 6
    o_pieces = refs[at : at + counts[0]]
    at += counts[0]
    p_pieces = refs[at : at + counts[1]]
    at += counts[1]
    (
        low_ref,
        dqkv_ref,
        dn_send,
        dn_keep,
        gain_sum,
        dstrip,
        wbuf,
        obuf,
        qs,
        ks,
        vs,
        gs,
        qt,
        gt,
        dkt,
        dvt,
        dq,
        sems,
    ) = refs[at:]
    length = qkv_ref.shape[0]
    half = length // 2
    head_cols = heads * DH
    o_copies = start_rows(o_pieces, obuf, offs_ref, sems.at[0])
    p_copies = start_rows(p_pieces, wbuf, offs_ref, sems.at[1])
    mine = pl.ds(pl.multiple_of(order_ref[1] * half, LANES), half)
    other = pl.ds(pl.multiple_of(order_ref[0] * half, LANES), half)
    low_ref[mine] = near[...]
    low_ref[other] = far[...]
    for h in range(heads):
        qs[h] = qkv_ref[:, h * DH : (h + 1) * DH]
        ks[h] = qkv_ref[:, head_cols + h * DH : head_cols + (h + 1) * DH]
        vs[h] = qkv_ref[:, 2 * head_cols + h * DH : 2 * head_cols + (h + 1) * DH]
        qt[h] = qs[h].T
    dstrip[...] = jnp.zeros_like(dstrip)
    dkt[...] = jnp.zeros_like(dkt)
    dvt[...] = jnp.zeros_like(dvt)
    for copy in o_copies + p_copies:
        copy.wait()
    grads = mm(low_ref[...], obuf[:, :head_cols]).astype(BF16)
    for h in range(heads):
        gs[h] = grads[:, h * DH : (h + 1) * DH]
        gt[h] = gs[h].T
    blocks = length // LANES
    seg_keys = segments(
        lax.broadcasted_iota(jnp.int32, (1, length), 1), ends_ref, buffer, slots
    )

    @pl.loop(0, blocks)
    def _(block):
        begin = pl.multiple_of(block * LANES, LANES)
        rows = pl.ds(begin, LANES)
        window = pl.ds(pl.multiple_of((blocks - 1 - block) * LANES, LANES), length)
        seg_rows = segments(
            lax.broadcasted_iota(jnp.int32, (LANES, 1), 0) + begin, ends_ref, buffer, slots
        )
        same = seg_rows == seg_keys
        logs = log_ref[rows]
        for h in range(heads):
            scores = mm(qs[h, rows], ks[h], NT) + strip_ref[h, :, window]
            scores = jnp.where(same, scores, masked_score)
            probs = jnp.exp(scores - logs[:, h : h + 1])
            d_probs = mm(gs[h, rows], vs[h], NT)
            inner = jnp.sum(probs * d_probs, axis=1, keepdims=True)
            d_scores = (probs * (d_probs - inner)).astype(BF16)
            dstrip[h, :, window] = dstrip[h, :, window] + d_scores.astype(F32)
            dq[h, rows] = mm(d_scores, ks[h]).astype(BF16)
            dkt[h] = dkt[h] + mm(qt[h, :, rows], d_scores)
            dvt[h] = dvt[h] + mm(gt[h, :, rows], probs.astype(BF16))

    outs = [dq[h] for h in range(heads)]
    outs += [dkt[h].T.astype(BF16) for h in range(heads)]
    outs += [dvt[h].T.astype(BF16) for h in range(heads)]
    dqkv_ref[...] = jnp.concatenate(outs, axis=1)
    sums = []
    for target, which in ((dn_send, other), (dn_keep, mine)):
        dn = mm(dqkv_ref[which], wbuf[:, : 3 * head_cols], NT)
        values = x_ref[which].astype(F32)
        sums.append(fold_rows(dn * values * rms_scale(values)))
        target[...] = dn.astype(BF16)
    gain_sum[...] = sums[0] + sums[1]


def back(buffer, ends, offs, order, near, far, qkv, logs, strip, x, o_pieces, p_pieces, heads):
    length = qkv.shape[0]
    half = length // 2
    width = x.shape[1]
    head_cols = heads * DH
    counts = (len(o_pieces), len(p_pieces))
    whole = lambda i, *_: (0, 0)
    whole3 = lambda i, *_: (0, 0, 0)
    spec = pltpu.PrefetchScalarGridSpec(
        num_scalar_prefetch=3,
        grid=(1,),
        in_specs=[
            pl.BlockSpec((half, width), whole),
            pl.BlockSpec((half, width), whole),
            pl.BlockSpec(qkv.shape, whole),
            pl.BlockSpec(logs.shape, whole),
            pl.BlockSpec(strip.shape, whole3),
            pl.BlockSpec((length, width), lambda i, *_: (buffer, 0)),
        ]
        + [pl.BlockSpec(memory_space=ANY)] * sum(counts),
        out_specs=[
            pl.BlockSpec((length, width), whole),
            pl.BlockSpec((length, 3 * head_cols), whole),
            pl.BlockSpec((half, width), whole),
            pl.BlockSpec((half, width), whole),
            pl.BlockSpec((8, width), whole),
            pl.BlockSpec(strip.shape, whole3),
        ],
        scratch_shapes=[
            pltpu.VMEM((width, p_pieces[0].shape[1]), BF16),
            pltpu.VMEM((width, o_pieces[0].shape[1]), BF16),
            pltpu.VMEM((heads, length, DH), BF16),
            pltpu.VMEM((heads, length, DH), BF16),
            pltpu.VMEM((heads, length, DH), BF16),
            pltpu.VMEM((heads, length, DH), BF16),
            pltpu.VMEM((heads, DH, length), BF16),
            pltpu.VMEM((heads, DH, length), BF16),
            pltpu.VMEM((heads, DH, length), F32),
            pltpu.VMEM((heads, DH, length), F32),
            pltpu.VMEM((heads, length, DH), BF16),
            pltpu.SemaphoreType.DMA((2, max(counts))),
        ],
    )
    return pl.pallas_call(
        functools.partial(back_kernel, buffer, ends.shape[1], heads, counts),
        grid_spec=spec,
        out_shape=[
            jax.ShapeDtypeStruct((length, width), BF16),
            jax.ShapeDtypeStruct((length, 3 * head_cols), BF16),
            jax.ShapeDtypeStruct((half, width), BF16),
            jax.ShapeDtypeStruct((half, width), BF16),
            jax.ShapeDtypeStruct((8, width), F32),
            jax.ShapeDtypeStruct(strip.shape, F32),
        ],
        compiler_params=params(),
        cost_estimate=pl.CostEstimate(
            flops=40 * heads * DH * length * length,
            bytes_accessed=16 << 20,
            transcendentals=heads * length * length,
        ),
        name="back",
    )(ends, offs, order, near, far, qkv, logs, strip, x, *o_pieces, *p_pieces)


def scatter_rows(total, offs_ref, evens, odds):
    rows = evens[0].shape[0]
    for at in range(2 * len(evens)):
        begin = pl.multiple_of(offs_ref[at], 8)
        block = total[pl.ds(begin, rows)]
        if at % 2:
            odds[at // 2][...] = block.astype(BF16)
        else:
            evens[at // 2][...] = block


def feed_grad_kernel(count, hidden_cols, offs_ref, *refs):
    buffers = 2
    normed = refs[:buffers]
    gates = refs[buffers : 2 * buffers]
    hiddens = refs[2 * buffers : 3 * buffers]
    cot_ref = refs[3 * buffers]
    outs = refs[3 * buffers + 1 : -1]
    total = refs[-1]
    length = normed[0].shape[0]
    width = normed[0].shape[1]
    part = 256
    for begin in range(0, width, part):
        cols = slice(begin, begin + part)
        total[cols, : 2 * hidden_cols] = mm(normed[0][:, cols], gates[0][...], TN) + mm(
            normed[1][:, cols], gates[1][...], TN
        )
        total[cols, 2 * hidden_cols :] = mm(
            cot_ref[:length, cols], hiddens[0][...], TN
        ) + mm(cot_ref[length:, cols], hiddens[1][...], TN)
    if count > 1:
        scatter_rows(total, offs_ref, outs[: count // 2], outs[count // 2 :])
    else:
        outs[0][...] = total[...]


def attend_grad_kernel(count, heads, offs_ref, *refs):
    buffers = 2
    normed = refs[:buffers]
    dqkv = refs[buffers : 2 * buffers]
    lows = refs[2 * buffers : 3 * buffers]
    atts = refs[3 * buffers : 4 * buffers]
    sums_ref = refs[4 * buffers]
    outs = refs[4 * buffers + 1 : -1]
    total = refs[-1]
    width = normed[0].shape[1]
    head_cols = heads * DH
    qkv_cols = 3 * head_cols
    part = 256
    rows = lax.broadcasted_iota(jnp.int32, (LANES, width), 0)
    first = sums_ref[0] + sums_ref[1]
    second = sums_ref[2] + sums_ref[3]
    gain_rows = jnp.where(
        rows == DH,
        jnp.sum(first, axis=0, keepdims=True),
        jnp.where(rows == DH + 1, jnp.sum(second, axis=0, keepdims=True), 0.0),
    )
    gain_cols = gain_rows.T
    for begin in range(0, width, part):
        cols = slice(begin, begin + part)
        total[cols, :qkv_cols] = mm(normed[0][:, cols], dqkv[0][...], TN) + mm(
            normed[1][:, cols], dqkv[1][...], TN
        )
        total[cols, qkv_cols : qkv_cols + DH] = gain_cols[cols, DH:]
        total[cols, qkv_cols + DH : qkv_cols + DH + head_cols] = mm(
            lows[0][:, cols], atts[0][...], TN
        ) + mm(lows[1][:, cols], atts[1][...], TN)
    if count > 1:
        scatter_rows(total, offs_ref, outs[: count // 2], outs[count // 2 :])
    else:
        outs[0][...] = total[...]


def grad_call(kernel, name, offs, operands, width, cols, count, rows, flops):
    vmem = pl.BlockSpec(memory_space=pltpu.VMEM)
    if count > 1:
        shapes = [jax.ShapeDtypeStruct((rows, cols), F32)] * (count // 2)
        shapes += [jax.ShapeDtypeStruct((rows, cols), BF16)] * (count // 2)
    else:
        shapes = [jax.ShapeDtypeStruct((width, cols), F32)]
    return pl.pallas_call(
        kernel,
        in_specs=[pl.BlockSpec(memory_space=pltpu.SMEM)] + [vmem] * len(operands),
        out_specs=[vmem] * len(shapes),
        out_shape=shapes,
        scratch_shapes=[pltpu.VMEM((width, cols), F32)],
        compiler_params=params(),
        cost_estimate=pl.CostEstimate(flops=2 * flops, bytes_accessed=14 << 20, transcendentals=0),
        name=name,
    )(offs, *operands)


def bucket_kernel(heads, near_ref, far_ref, out_ref):
    lanes = near_ref.shape[2]
    blocks = (lanes // LANES + 1) // 2
    begin = (blocks - 2) * LANES
    end = begin + 3 * LANES
    rows = lax.broadcasted_iota(jnp.int32, (LANES, 3 * LANES), 0)
    ids = bucket_of(
        lax.broadcasted_iota(jnp.int32, (LANES, 3 * LANES), 1) - LANES - rows
    )
    lane = lax.broadcasted_iota(jnp.int32, (1, LANES), 1)
    out = jnp.zeros((1, LANES), F32)
    for h in range(heads):
        strip = near_ref[h] + far_ref[h]
        left = jnp.sum(jnp.sum(strip[:, :begin], axis=0, keepdims=True), axis=1, keepdims=True)
        right = jnp.sum(jnp.sum(strip[:, end:], axis=0, keepdims=True), axis=1, keepdims=True)
        out = out + jnp.where(lane == h * 32 + 15, left, 0.0)
        out = out + jnp.where(lane == h * 32 + 31, right, 0.0)
        middle = strip[:, begin:end]
        for b in range(32):
            if b == 16:
                continue
            part = jnp.sum(jnp.where(ids == b, middle, 0.0), axis=0, keepdims=True)
            part = jnp.sum(part, axis=1, keepdims=True)
            out = out + jnp.where(lane == h * 32 + b, part, 0.0)
    out_ref[...] = jnp.broadcast_to(out, (8, LANES))


def norm_kernel(wide, narrow, lists, gain_at, *refs):
    at = 0
    groups = []
    for count in lists:
        groups.append(refs[at : at + count])
        at += count
    bucket_ref = refs[at]
    outs = refs[at + 1 : at + 1 + len(lists)]
    stat_ref, gain_ref, table_ref, block, inbox, padded, send_sems, recv_sems = refs[
        at + 1 + len(lists) :
    ]
    total = wide * narrow
    w = lax.axis_index("wide")
    n = lax.axis_index("narrow")
    me = w * narrow + n
    barrier = pltpu.get_barrier_semaphore()

    @pl.loop(1, total)
    def _(k):
        peer = (me + k) % total
        pl.semaphore_signal(
            barrier, inc=1, device_id=(peer // narrow, peer % narrow), device_id_type=MESH
        )

    squares = jnp.zeros((8, LANES), F32)
    for which, (group, out) in enumerate(zip(groups, outs)):
        value = group[0][...].astype(F32)
        for more in group[1:]:
            value = value + more[...].astype(F32)
        out[...] = value
        squared = value * value
        if which == 0:
            lane = lax.broadcasted_iota(jnp.int32, value.shape, 1)
            inside = (lane >= gain_at) & (lane < gain_at + DH)
            squared = jnp.where(inside, 0.0, squared)
        squared = jnp.sum(squared, axis=1, keepdims=True)
        squares = squares + jnp.sum(squared, axis=0, keepdims=True)
    rows = outs[0].shape[0]
    low = gain_at // LANES * LANES
    padded[...] = jnp.zeros_like(padded)
    padded[0:rows] = outs[0][:, low : low + LANES]
    turned = padded[...].T
    row = lax.broadcasted_iota(jnp.int32, (8, LANES), 0)
    here = gain_at - low
    mine = jnp.where(row == 0, squares, 0.0)
    mine = jnp.where(row == 1, turned[here : here + 1], mine)
    mine = jnp.where(row == 2, turned[here + 1 : here + 2], mine)
    mine = jnp.where(row == 3, bucket_ref[...], mine)
    block[...] = mine
    inbox[me] = mine
    pl.semaphore_wait(barrier, total - 1)

    @pl.loop(1, total)
    def _(k):
        peer = (me + k) % total
        pltpu.make_async_remote_copy(
            src_ref=block,
            dst_ref=inbox.at[me],
            send_sem=send_sems.at[k],
            recv_sem=recv_sems.at[total - k],
            device_id=(peer // narrow, peer % narrow),
            device_id_type=MESH,
        ).start()

    @pl.loop(1, total)
    def _(k):
        peer = (me + k) % total
        copy = pltpu.make_async_remote_copy(
            src_ref=block,
            dst_ref=inbox.at[peer],
            send_sem=send_sems.at[k],
            recv_sem=recv_sems.at[k],
            device_id=(peer // narrow, peer % narrow),
            device_id_type=MESH,
        )
        copy.wait_send()
        copy.wait_recv()

    columns = [jnp.zeros((8, LANES), F32) for _ in range(narrow)]
    gain_square = jnp.zeros((8, LANES), F32)
    square_total = jnp.zeros((8, LANES), F32)
    for a in range(wide):
        gains = jnp.zeros((8, LANES), F32)
        for b in range(narrow):
            got = inbox[a * narrow + b]
            gains = gains + got
            columns[b] = columns[b] + got
        square_total = square_total + gains
        gain_square = gain_square + gains * gains
    own = inbox[w * narrow]
    for b in range(1, narrow):
        own = own + inbox[w * narrow + b]
    gain_ref[...] = own
    pick = (row == 1) | (row == 2)
    gain_square = jnp.where(pick, gain_square, 0.0)
    norm_square = square_total[0:1, 0:1] + jnp.sum(
        jnp.sum(gain_square, axis=0, keepdims=True), axis=1, keepdims=True
    )
    heads = LANES // 32 - 1
    lane = lax.broadcasted_iota(jnp.int32, (32, LANES), 1)
    depth = lax.broadcasted_iota(jnp.int32, (32, LANES), 0)
    table = jnp.zeros((32, LANES), F32)
    for b in range(narrow):
        line = columns[b][3:4]
        norm_square = norm_square + jnp.sum(line * line, axis=1, keepdims=True)
        for h in range(heads):
            column = jnp.sum(
                jnp.where(lane == depth + 32 * h, line, 0.0), axis=1, keepdims=True
            )
            table = jnp.where(lane == b * heads + h, column, table)
    table_ref[...] = table
    global_norm = jnp.sqrt(norm_square)
    factor = jnp.minimum(1.0, clip_limit / (global_norm + 1e-06))
    stat_ref[...] = jnp.where(row == 0, global_norm, factor)


def norm_call(wide, narrow, groups, bucket, gain_at):
    vmem = pl.BlockSpec(memory_space=pltpu.VMEM)
    lists = tuple(len(group) for group in groups)
    total = wide * narrow
    operands = [piece for group in groups for piece in group] + [bucket]
    return pl.pallas_call(
        functools.partial(norm_kernel, wide, narrow, lists, gain_at),
        in_specs=[vmem] * len(operands),
        out_specs=[vmem] * (len(lists) + 3),
        out_shape=[jax.ShapeDtypeStruct(group[0].shape, F32) for group in groups]
        + [
            jax.ShapeDtypeStruct((8, LANES), F32),
            jax.ShapeDtypeStruct((8, LANES), F32),
            jax.ShapeDtypeStruct((32, LANES), F32),
        ],
        scratch_shapes=[
            pltpu.VMEM((8, LANES), F32),
            pltpu.VMEM((total, 8, LANES), F32),
            pltpu.VMEM((LANES, LANES), F32),
            pltpu.SemaphoreType.DMA((total,)),
            pltpu.SemaphoreType.DMA((total,)),
        ],
        compiler_params=params(collective_id=0, has_side_effects=True),
        cost_estimate=pl.CostEstimate(flops=1 << 20, bytes_accessed=4 << 20, transcendentals=0),
        name="norm",
    )(*operands)


def adam_kernel(heads, hidden_cols, att_ref, feed_ref, gain_ref, table_ref, stat_ref, *refs):
    weights, firsts, seconds = refs[:6], refs[6:12], refs[12:18]
    outs = refs[18:36]
    o_pad, s_pad = refs[36:]
    factor = stat_ref[1:2, 0:1]
    head_cols = heads * DH
    rows = att_ref.shape[0]
    gain_at = 3 * head_cols

    def update(which, index, gradient):
        results = adam_update(
            weights[which][index],
            firsts[which][index],
            seconds[which][index],
            factor * gradient,
            step_rates[which],
            decay_rates[which],
        )
        for at in range(3):
            outs[6 * at + which][index] = results[at]

    for i in range(3):
        update(0, i, att_ref[:, i * head_cols : (i + 1) * head_cols])
    for i in range(2):
        update(2, i, feed_ref[:, i * hidden_cols : (i + 1) * hidden_cols])
    o_pad[...] = jnp.zeros_like(o_pad)
    s_pad[...] = jnp.zeros_like(s_pad)
    o_pad[0:rows] = att_ref[:, gain_at + DH :]
    s_pad[0:rows] = feed_ref[:, 2 * hidden_cols :]
    update(1, slice(None), o_pad[...].T[:head_cols, :rows])
    update(3, slice(None), s_pad[...].T[:, :rows])
    columns = weights[4].shape[1]
    update(4, slice(None), table_ref[:, :columns])
    update(5, slice(None), gain_ref[1:3, :rows])


def adam_call(att, feed_grad, gain, table, stat, params_in, firsts, seconds, heads, hidden_cols):
    vmem = pl.BlockSpec(memory_space=pltpu.VMEM)
    operands = [att, feed_grad, gain, table, stat, *params_in, *firsts, *seconds]
    pad_cols = att.shape[1] - (3 * heads * DH + DH)
    return pl.pallas_call(
        functools.partial(adam_kernel, heads, hidden_cols),
        in_specs=[vmem] * len(operands),
        out_specs=[vmem] * 18,
        out_shape=[jax.ShapeDtypeStruct(a.shape, F32) for a in params_in] * 3,
        scratch_shapes=[
            pltpu.VMEM((LANES, pad_cols), F32),
            pltpu.VMEM((LANES, hidden_cols), F32),
        ],
        compiler_params=params(),
        cost_estimate=pl.CostEstimate(flops=4 << 20, bytes_accessed=8 << 20, transcendentals=0),
        name="adam",
    )(*operands)


def place_kernel(half, offs_ref, *refs):
    pieces = refs[:-2]
    out_ref, sems = refs[-2:]
    copies = []
    for at, piece in enumerate(pieces):
        begin = pl.multiple_of(offs_ref[at], LANES)
        copies.append(
            pltpu.make_async_copy(piece, out_ref.at[pl.ds(begin, half)], sems.at[at])
        )
    for copy in copies:
        copy.start()
    for copy in copies:
        copy.wait()


def place(pieces, offs, rows):
    half, width = pieces[0].shape
    hbm = pl.BlockSpec(memory_space=ANY)
    return pl.pallas_call(
        functools.partial(place_kernel, half),
        in_specs=[pl.BlockSpec(memory_space=pltpu.SMEM)] + [hbm] * len(pieces),
        out_specs=hbm,
        out_shape=jax.ShapeDtypeStruct((rows, width), pieces[0].dtype),
        scratch_shapes=[pltpu.SemaphoreType.DMA((len(pieces),))],
        compiler_params=params(),
        cost_estimate=pl.CostEstimate(
            flops=0, bytes_accessed=4 * rows * width, transcendentals=0
        ),
        name="place",
    )(offs, *pieces)


def body(wide, narrow, *arguments):
    (
        block_input,
        cotangent,
        lengths,
        project_weight,
        output_weight,
        expand_weight,
        shrink_weight,
        bucket_bias,
        norm_gains,
    ) = arguments[:9]
    firsts = arguments[9:15]
    seconds = arguments[15:21]
    tokens, width = block_input.shape
    buffers = lengths.shape[0]
    length = tokens // buffers
    rows = norm_gains.shape[1]
    head_cols = project_weight.shape[2]
    heads = head_cols // DH
    hidden_cols = expand_weight.shape[2]
    w = lax.axis_index("wide")
    n = lax.axis_index("narrow")
    core = n % 2
    direct = wide == 8 and rows % 16 == 0

    def swap(value, wide_mask, narrow_mask):
        pairs = [
            (a * narrow + b, (a ^ wide_mask) * narrow + (b ^ narrow_mask))
            for a in range(wide)
            for b in range(narrow)
        ]
        return lax.ppermute(value, ("wide", "narrow"), pairs)

    def gather(piece):
        if not direct:
            return [lax.all_gather(piece, "wide", axis=0, tiled=True)]
        found = {0: piece}
        for mask in (2, 4, 6):
            found[mask] = swap(piece, mask, 0)
        for mask in (0, 2, 4, 6):
            found[mask + 1] = swap(found[mask], 1, 0)
        return [found[mask] for mask in range(8)]

    def reduce_wide(outs):
        if not direct:
            return [lax.psum_scatter(outs[0], "wide", scatter_dimension=0, tiled=True)]
        evens, odds = outs[:4], outs[4:]
        got = []
        for e in (1, 2, 3, 0):
            came = swap(odds[e], 1, 0)
            if e:
                mixed = (evens[e] + came.astype(F32)).astype(BF16)
                got.append(swap(mixed, 2 * e, 0))
            else:
                kept = [evens[0], came]
        return kept + got

    if direct:
        offs = (jnp.arange(8, dtype=jnp.int32) ^ w) * rows
    else:
        offs = jnp.zeros((1,), jnp.int32)
    order = jnp.stack([1 - core, core, n // 2])

    p_piece = jnp.concatenate(
        [
            project_weight[0],
            project_weight[1],
            project_weight[2],
            norm_gains.T,
            jnp.zeros((rows, DH - 2), F32),
        ],
        axis=1,
    ).astype(BF16)
    p_pieces = gather(p_piece)
    o_piece = output_weight.astype(BF16).T
    o_pair = jnp.concatenate([o_piece, swap(o_piece, 0, 2)], axis=1)
    oa_pieces = gather(o_pair)
    ob_pieces = [swap(piece, 0, 1) for piece in oa_pieces]
    e_pieces = gather(
        jnp.concatenate([expand_weight[0], expand_weight[1]], axis=1).astype(BF16)
    )
    s_pieces = gather(shrink_weight.astype(BF16).T)

    ends = jnp.cumsum(lengths, axis=1)
    table = lax.dynamic_slice_in_dim(bucket_bias, n * heads, heads, 1).T
    blocks = length // LANES
    near_r = (
        jnp.arange(3 * LANES, dtype=jnp.int32)[None, :]
        - LANES
        - jnp.arange(LANES, dtype=jnp.int32)[:, None]
    )
    near_ids = bucket_of(near_r)
    near = sum(
        jnp.where(near_ids == b, table[:, b][:, None, None], 0.0) for b in range(32) if b != 16
    )
    far_shape = (heads, LANES, (blocks - 2) * LANES)
    strip = jnp.concatenate(
        [
            jnp.broadcast_to(table[:, 15][:, None, None], far_shape),
            near,
            jnp.broadcast_to(table[:, 31][:, None, None], far_shape),
        ],
        axis=2,
    )

    normed_one, qkv, atts, logs, fours = [], [], [], [], []
    for b in range(buffers):
        normed, rows_b, att, log, gains = attend(
            b, ends, offs, block_input, strip, p_pieces, length, heads
        )
        normed_one.append(normed)
        qkv.append(rows_b)
        atts.append(att)
        logs.append(log)
        across = swap(att, 0, 2)
        fours.append((att, across, swap(att, 0, 1), swap(across, 0, 1)))

    def core_sum(kept, sent):
        return (kept.astype(F32) + swap(sent, 0, 1).astype(F32)).astype(BF16)

    normed_two, hiddens, gates, middles, ff_sums, dn_sums, sums_two = [], [], [], [], [], [], []
    for b in range(buffers):
        normed, hidden, gate, ff_send, ff_keep, dn_send, dn_keep, middle, sums = feed(
            b,
            order,
            offs,
            fours[b],
            block_input,
            cotangent,
            gains,
            (oa_pieces, ob_pieces, e_pieces, s_pieces),
            length,
            hidden_cols,
        )
        normed_two.append(normed)
        hiddens.append(hidden)
        gates.append(gate)
        middles.append(middle)
        sums_two.append(sums)
        dn_sums.append(core_sum(dn_keep, dn_send))
        ff_sums.append(core_sum(ff_keep, ff_send))

    d_middles, lows = [], []
    for b in range(buffers):
        d_middle, low = half_call(
            middle_kernel,
            "middle",
            b,
            order,
            [dn_sums[b], swap(dn_sums[b], 0, 2), middles[b], cotangent],
            (3,),
            (F32, BF16),
            gains,
        )
        d_middles.append(d_middle)
        lows.append((low, swap(low, 0, 1)))

    count = 8 if direct else 1
    feed_outs = grad_call(
        functools.partial(feed_grad_kernel, count, hidden_cols),
        "feed_grad",
        offs,
        [*normed_two, *gates, *hiddens, cotangent],
        width,
        3 * hidden_cols,
        count,
        rows,
        2 * tokens * width * 3 * hidden_cols,
    )
    feed_group = reduce_wide(feed_outs)

    low_full, dqkv, dn_one, sums_one, strips = [], [], [], [], []
    for b in range(buffers):
        low, grads, dn_send, dn_keep, sums, dstrip = back(
            b,
            ends,
            offs,
            order,
            lows[b][0],
            lows[b][1],
            qkv[b],
            logs[b],
            strip,
            block_input,
            oa_pieces,
            p_pieces,
            heads,
        )
        low_full.append(low)
        dqkv.append(grads)
        sums_one.append(sums)
        strips.append(dstrip)
        dn_one.append(core_sum(dn_keep, dn_send))

    gain_at = 3 * head_cols
    att_outs = grad_call(
        functools.partial(attend_grad_kernel, count, heads),
        "attend_grad",
        offs,
        [*normed_one, *dqkv, *low_full, *atts, jnp.stack(sums_one + sums_two)],
        width,
        gain_at + DH + head_cols,
        count,
        rows,
        2 * tokens * width * 4 * head_cols,
    )
    att_group = reduce_wide(att_outs)
    vmem = pl.BlockSpec(memory_space=pltpu.VMEM)
    bucket = pl.pallas_call(
        functools.partial(bucket_kernel, heads),
        in_specs=[vmem, vmem],
        out_specs=vmem,
        out_shape=jax.ShapeDtypeStruct((8, LANES), F32),
        compiler_params=params(),
        cost_estimate=pl.CostEstimate(flops=8 << 20, bytes_accessed=4 << 20, transcendentals=0),
        name="bucket",
    )(*strips)

    half_offs = jnp.stack(
        [
            b * length + which * (length // 2)
            for b in range(buffers)
            for which in (core, 1 - core)
        ]
    )
    out_halves, in_halves = [], []
    for b in range(buffers):
        (half,) = half_call(
            output_kernel,
            "output",
            b,
            order,
            [ff_sums[b], swap(ff_sums[b], 0, 2), middles[b]],
            (),
            (BF16,),
        )
        out_halves += [half, swap(half, 0, 1)]
        (half,) = half_call(
            input_kernel,
            "input",
            b,
            order,
            [dn_one[b], swap(dn_one[b], 0, 2), block_input, d_middles[b]],
            (2,),
            (BF16,),
            gains,
        )
        in_halves += [half, swap(half, 0, 1)]
    block_output = place(out_halves, half_offs, tokens)
    input_gradient = place(in_halves, half_offs, tokens)

    att_grad, feed_grad, stat, gain, table_sum = norm_call(
        wide, narrow, [att_group, feed_group], bucket, gain_at
    )
    results = adam_call(
        att_grad,
        feed_grad,
        gain,
        table_sum,
        stat,
        arguments[3:9],
        firsts,
        seconds,
        heads,
        hidden_cols,
    )
    return (block_output, input_gradient, stat[0, 0], *results)


def solution(mesh):
    wide, narrow = mesh.shape["wide"], mesh.shape["narrow"]
    state = (
        P(None, "wide", "narrow"),
        P("narrow", "wide"),
        P(None, "wide", "narrow"),
        P("narrow", "wide"),
        P(),
        P(None, "wide"),
    )
    rows = P("wide", None)
    return jax.shard_map(
        functools.partial(body, wide, narrow),
        mesh=mesh,
        in_specs=(rows, rows, rows, *state, *state, *state),
        out_specs=(rows, rows, P(), *state, *state, *state),
        check_vma=False,
    )
```

time: 1340 us -> 494 us (0.37)
  waiting for transfers between devices: 498 us -> 69.5 us
  local copies, waits for them, and re-layouts: 451 us -> 23.6 us
  Pallas kernels: 0 us -> 306 us
  blocking collectives: 164 us -> 0 us
  matrix products: 99.9 us -> 0 us
  other arithmetic: 88 us -> 13.8 us
  starting transfers between devices: 0.68 us -> 72.9 us
  between operations: 22.1 us -> 2.13 us
    pallas_call x0 -> x19, Pallas kernels: none -> 306 us  [the longest x2 147 us: place(): pl.pallas_call(functools.partial(place_kernel, half), in_specs=[pl.BlockS...]
    psum x4 -> x0, waiting for transfers between devices: 285 us -> none  [the longest x1 89.9 us: body(): d_normed_two = lax.psum(second_terms, 'narrow')]
    reshape x29 -> x0, local copies, waits for them, and re-layouts: 177 us -> none  [the longest x12 92.6 us: toeplitz_rows(): return tiled_flat.reshape(length, 2 * length - 1)[:, length - 1:]]
    unnamed x13 -> x0, waiting for transfers between devices: 140 us -> none
    all_gather x4 -> x0, blocking collectives: 125 us -> none  [the longest x1 35.7 us: body(): lax.all_gather(project_weight.astype(jnp.bfloat16), 'wide', axis=1, tiled...]
    another operation x28 -> x1, local copies, waits for them, and re-layouts: 100 us -> 0.12 us  [the longest x24 100 us: toeplitz_rows(): tiled_flat = jnp.tile(padded, length)[:length * (2 * length - 1)]]
    dot_general x55 -> x0, matrix products: 95.3 us -> none  [the longest x12 18.5 us: head_scores(): jnp.einsum('qd,kd->qk', query_rows, key_rows, preferred_element_type=jnp....]
    reduce_scatter x2 -> x0, waiting for transfers between devices: 73.9 us -> none  [the longest x1 73.8 us: body(): lax.psum_scatter(expand_grad, 'wide', scatter_dimension=1, tiled=True)]
  transfers between devices with their start and end apart: 10 -> 75, of which waited for: 8 -> 18; matrix products, arithmetic and copies ran while one was open for 5% -> 6% of each run, Pallas kernels for 0% -> 48%
where the time goes in v1:
time: 494 us; the launch traced here: 488 us
  Pallas kernels  306 us (62%)
  starting transfers between devices  72.9 us (15%)
  waiting for transfers between devices  69.5 us (14%)
  local copies, waits for them, and re-layouts  23.6 us (5%)
  other arithmetic  13.8 us (3%)
    pallas_call x2, Pallas kernels, place(): pl.pallas_call(functools.partial(place_kernel, half), in_specs=[pl.BlockS...  147 us
    ppermute x75, starting transfers between devices, swap(): return lax.ppermute(value, ('wide', 'narrow'), pairs)  72.9 us
    ppermute x75, waiting for transfers between devices, swap(): return lax.ppermute(value, ('wide', 'narrow'), pairs)  69.5 us
    pallas_call x2, Pallas kernels, back(): pl.pallas_call(functools.partial(back_kernel, buffer, ends.shape[1], head...  36.2 us
    pallas_call x2, Pallas kernels, attend(): pl.pallas_call(functools.partial(attend_kernel, buffer, ends.shape[1], he...  30.5 us
    pallas_call x2, Pallas kernels, feed(): pl.pallas_call(functools.partial(feed_kernel, hidden_cols, counts), grid_...  28.2 us
    pallas_call x6, Pallas kernels, half_call(): pl.pallas_call(kernel, grid_spec=pltpu.PrefetchScalarGridSpec(num_scalar_...  27.1 us
    unnamed x217, local copies, waits for them, and re-layouts  20.3 us
  transfers between devices with their start and end apart: 75, of which 18 were waited for; matrix products, arithmetic and copies ran while one was open for 6% of the time, Pallas kernels for 48%

profile of v1, /device:TPU:0, one launch (start us, length us, event | category | flops | bytes accessed | tf_op | source)
XLA Modules:
  0.0 487.6 jit_solution(7096452875074348977)
XLA Ops:
  1.6 5.1 %collective-permute-start.38 = (bf16[96,512]{1,0:T(8,128)(2,1)S(1)}, bf16[96,512]{1,0:T(8,128)(2,1)S(1)}, u32[]{:S(2)}, u32[]{:S(2)}) collective-permute-start(bf16[96,512]{1,0:T(8,128)(2,1)S(1)} %convert_bitcast_fusion.refs_31_), channel_id=1, source_target_pairs={{0,24},{1,25},{2,26},{3,27},{4,28},{5,29},{6,30},{7,31},{8,16},{9,... | collective-permute-start | bytes 294920 | tf_op jit(solution)/shard_map/ppermute | solution.py:934
  25.4 5.4 %collective-permute-start.12 = (bf16[96,384]{1,0:T(8,128)(2,1)S(1)}, bf16[96,384]{1,0:T(8,128)(2,1)S(1)}, u32[]{:S(2)}, u32[]{:S(2)}) collective-permute-start(bf16[96,384]{1,0:T(8,128)(2,1)S(1)} %pad_maximum_fusion.3.refs_7_.refs_6_), channel_id=1, source_target_pairs={{0,8},{1,9},{2,10},{3,11},{4,12},{5,13},{6,14},{7,15},{8,0},{9,1},... | collective-permute-start | bytes 221192 | tf_op jit(solution)/shard_map/ppermute | solution.py:934
  61.1 15.3 %attend.2 = (bf16[768,768]{1,0:T(8,128)(2,1)}, bf16[768,576]{1,0:T(8,128)(2,1)}, bf16[768,192]{1,0:T(8,128)(2,1)}, f32[768,128]{1,0:T(8,128)}, f32[8,768]{1,0:T(8,128)}) custom-call(s32[2,12]{1,0:T(2,128)} %reduce_window_sum.11.ends_ref, s32[8]{0:T(128)} %xor_multiply_fusion.offs_ref, bf16[1536,768]{1,0:T(8,128)(2,1)} %x_ref.7, ...), custom_call_target="tpu_custom_call" | custom-call | flops 4831838208 | bytes 8388608 | tf_op jit(solution)/shard_map/attend/pallas_call | solution.py:185
  79.8 15.2 %attend.3 = (bf16[768,768]{1,0:T(8,128)(2,1)}, bf16[768,576]{1,0:T(8,128)(2,1)}, bf16[768,192]{1,0:T(8,128)(2,1)}, f32[768,128]{1,0:T(8,128)}, f32[8,768]{1,0:T(8,128)}) custom-call(s32[2,12]{1,0:T(2,128)} %reduce_window_sum.11.ends_ref, s32[8]{0:T(128)} %xor_multiply_fusion.offs_ref, bf16[1536,768]{1,0:T(8,128)(2,1)} %x_ref.7, ...), custom_call_target="tpu_custom_call" | custom-call | flops 4831838208 | bytes 8388608 | tf_op jit(solution)/shard_map/attend/pallas_call | solution.py:185
  101.9 5.1 %collective-permute-done.30.refs_28_ = bf16[96,1024]{1,0:T(8,128)(2,1)S(1)} collective-permute-done((bf16[96,1024]{1,0:T(8,128)(2,1)S(1)}, bf16[96,1024]{1,0:T(8,128)(2,1)S(1)}, u32[]{:S(2)}, u32[]{:S(2)}) %collective-permute-start.30) | collective-permute-done | bytes 196640 | tf_op jit(solution)/shard_map/ppermute | solution.py:934
  111.3 14.1 %feed.2 = (bf16[768,768]{1,0:T(8,128)(2,1)}, bf16[768,512]{1,0:T(8,128)(2,1)}, bf16[768,1024]{1,0:T(8,128)(2,1)}, bf16[384,768]{1,0:T(8,128)(2,1)}, bf16[384,768...) custom-call(s32[3]{0:T(128)} %pad_add_fusion.1.order_ref, ...), custom_call_target="tpu_custom_call" | custom-call | flops 5133828096 | bytes 12582912 | tf_op jit(solution)/shard_map/feed/pallas_call | solution.py:321
  127.5 14.1 %feed.3 = (bf16[768,768]{1,0:T(8,128)(2,1)}, bf16[768,512]{1,0:T(8,128)(2,1)}, bf16[768,1024]{1,0:T(8,128)(2,1)}, bf16[384,768]{1,0:T(8,128)(2,1)}, bf16[384,768...) custom-call(s32[3]{0:T(128)} %pad_add_fusion.1.order_ref, ...), custom_call_target="tpu_custom_call" | custom-call | flops 5133828096 | bytes 12582912 | tf_op jit(solution)/shard_map/feed/pallas_call | solution.py:321
  141.8 9.5 %feed_grad.1 = (f32[96,1536]{1,0:T(8,128)}, f32[96,1536]{1,0:T(8,128)}, f32[96,1536]{1,0:T(8,128)}, f32[96,1536]{1,0:T(8,128)}, bf16[96,1536]{1,0:T(8,128)(2,1)}...) custom-call(s32[8]{0:T(128)} %xor_multiply_fusion.offs_ref, ...), custom_call_target="tpu_custom_call" | custom-call | flops 7247757312 | bytes 14680064 | tf_op jit(solution)/shard_map/feed_grad/pallas_call | solution.py:632
  155.1 12.6 %collective-permute-done.69 = bf16[96,1536]{1,0:T(8,128)(2,1)S(1)} collective-permute-done((bf16[96,1536]{1,0:T(8,128)(2,1)}, bf16[96,1536]{1,0:T(8,128)(2,1)S(1)}, u32[]{:S(2)}, u32[]{:S(2)}) %collective-permute-start.69) | collective-permute-done | bytes 294944 | tf_op jit(solution)/shard_map/ppermute | solution.py:934
  170.7 4.9 %middle.2 = (f32[384,768]{1,0:T(8,128)}, bf16[384,768]{1,0:T(8,128)(2,1)}) custom-call(s32[3]{0:T(128)} %pad_add_fusion.1.order_ref, bf16[384,768]{1,0:T(8,128)(2,1)} %copy-done.1, bf16[384,768]{1,0:T(8,128)(2,1)} %copy-done.15, f32[384,768]{1,0:T(8,128)} %get-tuple-element.107.middle_ref, bf16[1536,768]{1,0:T(8,128)(2,1)} %refs_6_.2, ...), custom_call_target="tpu_custom_call" | custom-call | flops 5898240 | bytes 3538944 | tf_op jit(solution)/shard_map/middle/pallas_call | solution.py:381
  176.5 5.4 %collective-permute-done.56.far = bf16[384,768]{1,0:T(8,128)(2,1)S(1)} collective-permute-done((bf16[384,768]{1,0:T(8,128)(2,1)S(1)}, bf16[384,768]{1,0:T(8,128)(2,1)S(1)}, u32[]{:S(2)}, u32[]{:S(2)}) %collective-permute-start.56) | collective-permute-done | bytes 589856 | tf_op jit(solution)/shard_map/ppermute | solution.py:934
  182.8 4.9 %middle.3 = (f32[384,768]{1,0:T(8,128)}, bf16[384,768]{1,0:T(8,128)(2,1)}) custom-call(s32[3]{0:T(128)} %pad_add_fusion.1.order_ref, bf16[384,768]{1,0:T(8,128)(2,1)} %copy-done, bf16[384,768]{1,0:T(8,128)(2,1)} %copy-done.14, f32[384,768]{1,0:T(8,128)} %get-tuple-element.111.middle_ref, bf16[1536,768]{1,0:T(8,128)(2,1)} %refs_6_.2, ...), custom_call_target="tpu_custom_call" | custom-call | flops 5898240 | bytes 3538944 | tf_op jit(solution)/shard_map/middle/pallas_call | solution.py:381
  188.8 18.2 %back.2 = (bf16[768,768]{1,0:T(8,128)(2,1)}, bf16[768,576]{1,0:T(8,128)(2,1)}, bf16[384,768]{1,0:T(8,128)(2,1)}, bf16[384,768]{1,0:T(8,128)(2,1)}, f32[8,768]{1,0:T(8,128)}, /*index=5*/f32[3,128,1408]{2,1,0:T(8,128)}) custom-call(s32[2,12]{1,0:T(2,128)} %reduce_window_sum.11.ends_ref, s32[8]{0:T(128)} %xor_multiply_fusion.offs_ref, ...), custom_call_target="tpu_custom_call" | custom-call | flops 4529848320 | bytes 16777216 | tf_op jit(solution)/shard_map/back/pallas_call | solution.py:531
  207.9 18.0 %back.3 = (bf16[768,768]{1,0:T(8,128)(2,1)}, bf16[768,576]{1,0:T(8,128)(2,1)}, bf16[384,768]{1,0:T(8,128)(2,1)}, bf16[384,768]{1,0:T(8,128)(2,1)}, f32[8,768]{1,0:T(8,128)}, /*index=5*/f32[3,128,1408]{2,1,0:T(8,128)}) custom-call(s32[2,12]{1,0:T(2,128)} %reduce_window_sum.11.ends_ref, s32[8]{0:T(128)} %xor_multiply_fusion.offs_ref, ...), custom_call_target="tpu_custom_call" | custom-call | flops 4529848320 | bytes 16777216 | tf_op jit(solution)/shard_map/back/pallas_call | solution.py:531
  231.9 7.2 %attend_grad.1 = (f32[96,832]{1,0:T(8,128)}, f32[96,832]{1,0:T(8,128)}, f32[96,832]{1,0:T(8,128)}, f32[96,832]{1,0:T(8,128)}, bf16[96,832]{1,0:T(8,128)(2,1)}, /...) custom-call(s32[8]{0:T(128)} %xor_multiply_fusion.offs_ref, ...), custom_call_target="tpu_custom_call" | custom-call | flops 3623878656 | bytes 14680064 | tf_op jit(solution)/shard_map/attend_grad/pallas_call | solution.py:632
  245.4 10.8 %collective-permute-done.47.far = bf16[384,768]{1,0:T(8,128)(2,1)S(1)} collective-permute-done((bf16[384,768]{1,0:T(8,128)(2,1)S(1)}, bf16[384,768]{1,0:T(8,128)(2,1)S(1)}, u32[]{:S(2)}, u32[]{:S(2)}) %collective-permute-start.47) | collective-permute-done | bytes 589856 | tf_op jit(solution)/shard_map/ppermute | solution.py:934
  268.8 12.2 %collective-permute-done.59.far = bf16[384,768]{1,0:T(8,128)(2,1)S(1)} collective-permute-done((bf16[384,768]{1,0:T(8,128)(2,1)S(1)}, bf16[384,768]{1,0:T(8,128)(2,1)S(1)}, u32[]{:S(2)}, u32[]{:S(2)}) %collective-permute-start.59) | collective-permute-done | bytes 589856 | tf_op jit(solution)/shard_map/ppermute | solution.py:934
  282.2 4.5 input.2.refs_0_
  286.7 4.7 input.3.refs_2_
  309.1 73.3 %place.2 = bf16[1536,768]{1,0:T(8,128)(2,1)} custom-call(s32[4]{0:T(128)} %pad_add_fusion.offs_ref, bf16[384,768]{1,0:T(8,128)(2,1)} %output.2.refs_0_, bf16[384,768]{1,0:T(8,128)(2,1)} %copy-done.13, bf16[384,768]{1,0:T(8,128)(2,1)} %output.3.refs_2_, bf16[384,768]{1,0:T(8,128)(2,1)} %collective-permute-done.48.refs_3_), custom_call_target="tpu_custom_call" | custom-call | bytes 4718592 | tf_op jit(solution)/shard_map/place/pallas_call | solution.py:888
  382.4 5.1 %bucket.1.refs_10_ = f32[8,128]{1,0:T(8,128)} custom-call(f32[3,128,1408]{2,1,0:T(8,128)} %get-tuple-element.160.near_ref, f32[3,128,1408]{2,1,0:T(8,128)} %get-tuple-element.161.far_ref), custom_call_target="tpu_custom_call" | custom-call | flops 8388608 | bytes 4194304 | tf_op jit(solution)/shard_map/bucket/pallas_call | solution.py:1111
  387.5 11.0 %norm.1 = (f32[96,832]{1,0:T(8,128)}, f32[96,1536]{1,0:T(8,128)}, f32[8,128]{1,0:T(8,128)}, f32[8,128]{1,0:T(8,128)}, f32[32,128]{1,0:T(8,128)}) custom-call(f32[96,832]{1,0:T(8,128)} %get-tuple-element.138.refs_0_, bf16[96,832]{1,0:T(8,128)(2,1)} %collective-permute-done.61.refs_1_, bf16[96,832]{1,0:T(8,128)(2,1)} %collective-permute-done.63.refs_2_, ...), custom_call_target="tpu_custom_call" | custom-call | flops 1048576 | bytes 4194304 | tf_op jit(solution)/shard_map/norm/pallas_call | solution.py:792
  399.7 4.2 adam.1
  414.1 73.3 %place.3 = bf16[1536,768]{1,0:T(8,128)(2,1)} custom-call(s32[4]{0:T(128)} %pad_add_fusion.offs_ref, bf16[384,768]{1,0:T(8,128)(2,1)} %input.2.refs_0_, bf16[384,768]{1,0:T(8,128)(2,1)} %copy-done.11, bf16[384,768]{1,0:T(8,128)(2,1)} %input.3.refs_2_, bf16[384,768]{1,0:T(8,128)(2,1)} %copy-done.12), custom_call_target="tpu_custom_call" | custom-call | bytes 4718592 | tf_op jit(solution)/shard_map/place/pallas_call | solution.py:888
  (400 shorter events, 131.4 us)
Async XLA Ops:
  48.4 29.0 %collective-permute-start.31 = (bf16[96,1024]{1,0:T(8,128)(2,1)S(1)}, bf16[96,1024]{1,0:T(8,128)(2,1)S(1)}, u32[]{:S(2)}, u32[]{:S(2)}) collective-permute-start(bf16[96,1024]{1,0:T(8,128)(2,1)S(1)} %pad_maximum_fusion.1.refs_23_), channel_id=1, source_target_pairs={{0,24},{1,25},{2,26},{3,27},{4,28},{5,29},{6,30},{7,31},{8,16},{9,... | collective-permute-start | bytes 589832 | tf_op jit(solution)/shard_map/ppermute | solution.py:934
  55.1 22.9 %collective-permute-start.29 = (bf16[96,1024]{1,0:T(8,128)(2,1)S(1)}, bf16[96,1024]{1,0:T(8,128)(2,1)S(1)}, u32[]{:S(2)}, u32[]{:S(2)}) collective-permute-start(bf16[96,1024]{1,0:T(8,128)(2,1)S(1)} %pad_maximum_fusion.1.refs_23_), channel_id=1, source_target_pairs={{0,16},{1,17},{2,18},{3,19},{4,20},{5,21},{6,22},{7,23},{8,24},{9,... | collective-permute-start | bytes 589832 | tf_op jit(solution)/shard_map/ppermute | solution.py:934
  56.1 23.2 %collective-permute-start.27 = (bf16[96,1024]{1,0:T(8,128)(2,1)S(1)}, bf16[96,1024]{1,0:T(8,128)(2,1)S(1)}, u32[]{:S(2)}, u32[]{:S(2)}) collective-permute-start(bf16[96,1024]{1,0:T(8,128)(2,1)S(1)} %pad_maximum_fusion.1.refs_23_), channel_id=1, source_target_pairs={{0,8},{1,9},{2,10},{3,11},{4,12},{5,13},{6,14},{7,15},{8,0},{9,1},... | collective-permute-start | bytes 589832 | tf_op jit(solution)/shard_map/ppermute | solution.py:934
  78.0 21.9 %collective-permute-start.32 = (bf16[96,1024]{1,0:T(8,128)(2,1)S(1)}, bf16[96,1024]{1,0:T(8,128)(2,1)S(1)}, u32[]{:S(2)}, u32[]{:S(2)}) collective-permute-start(bf16[96,1024]{1,0:T(8,128)(2,1)S(1)} %collective-permute-done.31.refs_29_), channel_id=1, source_target_pairs={{0,4},{1,5},{2,6},{3,7},{4,0},{5,1},{6,2},{7,3},{8,12},{9,13},{10,... | collective-permute-start | bytes 589832 | tf_op jit(solution)/shard_map/ppermute | solution.py:934
  125.4 62.3 %collective-permute-start.40 = (bf16[384,768]{1,0:T(8,128)(2,1)}, bf16[384,768]{1,0:T(8,128)(2,1)S(1)}, u32[]{:S(2)}, u32[]{:S(2)}) collective-permute-start(bf16[384,768]{1,0:T(8,128)(2,1)} %get-tuple-element.106), channel_id=1, source_target_pairs={{0,1},{1,0},{2,3},{3,2},{4,5},{5,4},{6,7},{7,6},{8,9},{9,8},{10,11... | collective-permute-start | bytes 1769480 | tf_op jit(solution)/shard_map/ppermute | solution.py:934
  125.5 27.9 %collective-permute-start.49 = (bf16[384,768]{1,0:T(8,128)(2,1)}, bf16[384,768]{1,0:T(8,128)(2,1)S(1)}, u32[]{:S(2)}, u32[]{:S(2)}) collective-permute-start(bf16[384,768]{1,0:T(8,128)(2,1)} %get-tuple-element.113), channel_id=1, source_target_pairs={{0,1},{1,0},{2,3},{3,2},{4,5},{5,4},{6,7},{7,6},{8,9},{9,8},{10,11... | collective-permute-start | bytes 1769480 | tf_op jit(solution)/shard_map/ppermute | solution.py:934
  151.3 78.5 %collective-permute-start.68 = (bf16[96,1536]{1,0:T(8,128)(2,1)}, bf16[96,1536]{1,0:T(8,128)(2,1)S(1)}, u32[]{:S(2)}, u32[]{:S(2)}) collective-permute-start(bf16[96,1536]{1,0:T(8,128)(2,1)} %get-tuple-element.153), channel_id=1, source_target_pairs={{0,4},{1,5},{2,6},{3,7},{4,0},{5,1},{6,2},{7,3},{8,12},{9,13},{10,... | collective-permute-start | bytes 884744 | tf_op jit(solution)/shard_map/ppermute | solution.py:934
  153.4 22.2 %collective-permute-start.71 = (bf16[96,1536]{1,0:T(8,128)(2,1)}, bf16[96,1536]{1,0:T(8,128)(2,1)S(1)}, u32[]{:S(2)}, u32[]{:S(2)}) collective-permute-start(bf16[96,1536]{1,0:T(8,128)(2,1)} %get-tuple-element.157), channel_id=1, source_target_pairs={{0,4},{1,5},{2,6},{3,7},{4,0},{5,1},{6,2},{7,3},{8,12},{9,13},{10,... | collective-permute-start | bytes 884744 | tf_op jit(solution)/shard_map/ppermute | solution.py:934
  169.1 61.6 %collective-permute-start.73 = (bf16[96,1536]{1,0:T(8,128)(2,1)S(1)}, bf16[96,1536]{1,0:T(8,128)(2,1)S(1)}, u32[]{:S(2)}, u32[]{:S(2)}) collective-permute-start(bf16[96,1536]{1,0:T(8,128)(2,1)S(1)} %copy-done.63), channel_id=1, source_target_pairs={{0,4},{1,5},{2,6},{3,7},{4,0},{5,1},{6,2},{7,3},{8,12},{9,13},{10,... | collective-permute-start | bytes 884744 | tf_op jit(solution)/shard_map/ppermute | solution.py:934
  181.9 44.0 %collective-permute-start.46 = (bf16[384,768]{1,0:T(8,128)(2,1)S(1)}, bf16[384,768]{1,0:T(8,128)(2,1)S(1)}, u32[]{:S(2)}, u32[]{:S(2)}) collective-permute-start(bf16[384,768]{1,0:T(8,128)(2,1)S(1)} %copy-done.53), channel_id=1, source_target_pairs={{0,1},{1,0},{2,3},{3,2},{4,5},{5,4},{6,7},{7,6},{8,9},{9,8},{10,11... | collective-permute-start | bytes 1769480 | tf_op jit(solution)/shard_map/ppermute | solution.py:934
  188.0 51.2 %collective-permute-start.70 = (bf16[96,1536]{1,0:T(8,128)(2,1)}, bf16[96,1536]{1,0:T(8,128)(2,1)S(1)}, u32[]{:S(2)}, u32[]{:S(2)}) collective-permute-start(bf16[96,1536]{1,0:T(8,128)(2,1)} %add_convert_fusion.8), channel_id=1, source_target_pairs={{0,8},{1,9},{2,10},{3,11},{4,12},{5,13},{6,14},{7,15},{8,0},{9,1},... | collective-permute-start | bytes 884744 | tf_op jit(solution)/shard_map/ppermute | solution.py:934
  228.4 27.8 %collective-permute-start.47 = (bf16[384,768]{1,0:T(8,128)(2,1)S(1)}, bf16[384,768]{1,0:T(8,128)(2,1)S(1)}, u32[]{:S(2)}, u32[]{:S(2)}) collective-permute-start(bf16[384,768]{1,0:T(8,128)(2,1)S(1)} %add_convert_fusion.4.near), channel_id=1, source_target_pairs={{0,2},{1,3},{2,0},{3,1},{4,6},{5,7},{6,4},{7,5},{8,10},{9,11},{10,... | collective-permute-start | bytes 1769480 | tf_op jit(solution)/shard_map/ppermute | solution.py:934
  229.8 39.0 %collective-permute-start.53 = (bf16[384,768]{1,0:T(8,128)(2,1)S(1)}, bf16[384,768]{1,0:T(8,128)(2,1)S(1)}, u32[]{:S(2)}, u32[]{:S(2)}) collective-permute-start(bf16[384,768]{1,0:T(8,128)(2,1)S(1)} %add_convert_fusion.2.near), channel_id=1, source_target_pairs={{0,2},{1,3},{2,0},{3,1},{4,6},{5,7},{6,4},{7,5},{8,10},{9,11},{10,... | collective-permute-start | bytes 1769480 | tf_op jit(solution)/shard_map/ppermute | solution.py:934
  230.7 50.3 %collective-permute-start.59 = (bf16[384,768]{1,0:T(8,128)(2,1)S(1)}, bf16[384,768]{1,0:T(8,128)(2,1)S(1)}, u32[]{:S(2)}, u32[]{:S(2)}) collective-permute-start(bf16[384,768]{1,0:T(8,128)(2,1)S(1)} %add_convert_fusion.near), channel_id=1, source_target_pairs={{0,2},{1,3},{2,0},{3,1},{4,6},{5,7},{6,4},{7,5},{8,10},{9,11},{10,... | collective-permute-start | bytes 1769480 | tf_op jit(solution)/shard_map/ppermute | solution.py:934
  239.2 52.3 %collective-permute-start.72 = (bf16[96,1536]{1,0:T(8,128)(2,1)}, bf16[96,1536]{1,0:T(8,128)(2,1)}, u32[]{:S(2)}, u32[]{:S(2)}) collective-permute-start(bf16[96,1536]{1,0:T(8,128)(2,1)} %add_convert_fusion.7), channel_id=1, source_target_pairs={{0,16},{1,17},{2,18},{3,19},{4,20},{5,21},{6,22},{7,23},{8,24},{9,... | collective-permute-start | bytes 884744 | tf_op jit(solution)/shard_map/ppermute | solution.py:934
  243.5 22.6 %collective-permute-start.62 = (bf16[96,832]{1,0:T(8,128)(2,1)}, bf16[96,832]{1,0:T(8,128)(2,1)S(1)}, u32[]{:S(2)}, u32[]{:S(2)}) collective-permute-start(bf16[96,832]{1,0:T(8,128)(2,1)} %get-tuple-element.141), channel_id=1, source_target_pairs={{0,4},{1,5},{2,6},{3,7},{4,0},{5,1},{6,2},{7,3},{8,12},{9,13},{10,... | collective-permute-start | bytes 479240 | tf_op jit(solution)/shard_map/ppermute | solution.py:934
  256.2 36.3 %collective-permute-start.74 = (bf16[96,1536]{1,0:T(8,128)(2,1)}, bf16[96,1536]{1,0:T(8,128)(2,1)S(1)}, u32[]{:S(2)}, u32[]{:S(2)}) collective-permute-start(bf16[96,1536]{1,0:T(8,128)(2,1)} %add_convert_fusion.6), channel_id=1, source_target_pairs={{0,24},{1,25},{2,26},{3,27},{4,28},{5,29},{6,30},{7,31},{8,16},{9,... | collective-permute-start | bytes 884744 | tf_op jit(solution)/shard_map/ppermute | solution.py:934
  266.1 32.8 %collective-permute-start.42 = (bf16[384,768]{1,0:T(8,128)(2,1)S(1)}, bf16[384,768]{1,0:T(8,128)(2,1)S(1)}, u32[]{:S(2)}, u32[]{:S(2)}) collective-permute-start(bf16[384,768]{1,0:T(8,128)(2,1)S(1)} %copy-done.3), channel_id=1, source_target_pairs={{0,1},{1,0},{2,3},{3,2},{4,5},{5,4},{6,7},{7,6},{8,9},{9,8},{10,11... | collective-permute-start | bytes 1769480 | tf_op jit(solution)/shard_map/ppermute | solution.py:934
  268.8 30.8 %collective-permute-start.48 = (bf16[384,768]{1,0:T(8,128)(2,1)}, bf16[384,768]{1,0:T(8,128)(2,1)}, u32[]{:S(2)}, u32[]{:S(2)}) collective-permute-start(bf16[384,768]{1,0:T(8,128)(2,1)} %output.3.refs_2_), channel_id=1, source_target_pairs={{0,1},{1,0},{2,3},{3,2},{4,5},{5,4},{6,7},{7,6},{8,9},{9,8},{10,11... | collective-permute-start | bytes 1769480 | tf_op jit(solution)/shard_map/ppermute | solution.py:934
  292.4 120.0 %collective-permute-start.54 = (bf16[384,768]{1,0:T(8,128)(2,1)S(1)}, bf16[384,768]{1,0:T(8,128)(2,1)S(1)}, u32[]{:S(2)}, u32[]{:S(2)}) collective-permute-start(bf16[384,768]{1,0:T(8,128)(2,1)S(1)} %copy-done.2), channel_id=1, source_target_pairs={{0,1},{1,0},{2,3},{3,2},{4,5},{5,4},{6,7},{7,6},{8,9},{9,8},{10,11... | collective-permute-start | bytes 1769480 | tf_op jit(solution)/shard_map/ppermute | solution.py:934
  292.5 119.9 %collective-permute-start.60 = (bf16[384,768]{1,0:T(8,128)(2,1)}, bf16[384,768]{1,0:T(8,128)(2,1)S(1)}, u32[]{:S(2)}, u32[]{:S(2)}) collective-permute-start(bf16[384,768]{1,0:T(8,128)(2,1)} %input.3.refs_2_), channel_id=1, source_target_pairs={{0,1},{1,0},{2,3},{3,2},{4,5},{5,4},{6,7},{7,6},{8,9},{9,8},{10,11... | collective-permute-start | bytes 1769480 | tf_op jit(solution)/shard_map/ppermute | solution.py:934
  298.8 88.7 %collective-permute-start.63 = (bf16[96,832]{1,0:T(8,128)(2,1)S(1)}, bf16[96,832]{1,0:T(8,128)(2,1)}, u32[]{:S(2)}, u32[]{:S(2)}) collective-permute-start(bf16[96,832]{1,0:T(8,128)(2,1)S(1)} %add_convert_fusion.11), channel_id=1, source_target_pairs={{0,8},{1,9},{2,10},{3,11},{4,12},{5,13},{6,14},{7,15},{8,0},{9,1},... | collective-permute-start | bytes 479240 | tf_op jit(solution)/shard_map/ppermute | solution.py:934
  299.6 87.9 %collective-permute-start.65 = (bf16[96,832]{1,0:T(8,128)(2,1)}, bf16[96,832]{1,0:T(8,128)(2,1)}, u32[]{:S(2)}, u32[]{:S(2)}) collective-permute-start(bf16[96,832]{1,0:T(8,128)(2,1)} %add_convert_fusion.10), channel_id=1, source_target_pairs={{0,16},{1,17},{2,18},{3,19},{4,20},{5,21},{6,22},{7,23},{8,24},{9,... | collective-permute-start | bytes 479240 | tf_op jit(solution)/shard_map/ppermute | solution.py:934
  302.7 84.8 %collective-permute-start.67 = (bf16[96,832]{1,0:T(8,128)(2,1)}, bf16[96,832]{1,0:T(8,128)(2,1)}, u32[]{:S(2)}, u32[]{:S(2)}) collective-permute-start(bf16[96,832]{1,0:T(8,128)(2,1)} %add_convert_fusion.9), channel_id=1, source_target_pairs={{0,24},{1,25},{2,26},{3,27},{4,28},{5,29},{6,30},{7,31},{8,16},{9,... | collective-permute-start | bytes 479240 | tf_op jit(solution)/shard_map/ppermute | solution.py:934
  (153 other events, 1904.0 us)

commit v2 on v1

--- a/solution.py
+++ b/solution.py
@@ -812,7 +812,7 @@
     )(*operands)
 
 
-def adam_kernel(heads, hidden_cols, att_ref, feed_ref, gain_ref, table_ref, stat_ref, *refs):
+def adam_kernel(heads, hidden_cols, parts, att_ref, feed_ref, gain_ref, table_ref, stat_ref, *refs):
     weights, firsts, seconds = refs[:6], refs[6:12], refs[12:18]
     outs = refs[18:36]
     o_pad, s_pad = refs[36:]
@@ -835,12 +835,18 @@
 
     for i in range(3):
         update(0, i, att_ref[:, i * head_cols : (i + 1) * head_cols])
-    for i in range(2):
-        update(2, i, feed_ref[:, i * hidden_cols : (i + 1) * hidden_cols])
+    part = hidden_cols // parts
+    for j in range(parts):
+        span = slice(j * part, (j + 1) * part)
+        for i in range(2):
+            begin = (3 * j + i) * part if parts > 1 else i * part
+            update(2, (i, slice(None), span), feed_ref[:, begin : begin + part])
     o_pad[...] = jnp.zeros_like(o_pad)
     s_pad[...] = jnp.zeros_like(s_pad)
     o_pad[0:rows] = att_ref[:, gain_at + DH :]
-    s_pad[0:rows] = feed_ref[:, 2 * hidden_cols :]
+    for j in range(parts):
+        begin = (3 * j + 2) * part
+        s_pad[0:rows, j * part : (j + 1) * part] = feed_ref[:, begin : begin + part]
     update(1, slice(None), o_pad[...].T[:head_cols, :rows])
     update(3, slice(None), s_pad[...].T[:, :rows])
     columns = weights[4].shape[1]
@@ -848,12 +854,14 @@
     update(5, slice(None), gain_ref[1:3, :rows])
 
 
-def adam_call(att, feed_grad, gain, table, stat, params_in, firsts, seconds, heads, hidden_cols):
+def adam_call(
+    att, feed_grad, gain, table, stat, params_in, firsts, seconds, heads, hidden_cols, direct=False
+):
     vmem = pl.BlockSpec(memory_space=pltpu.VMEM)
     operands = [att, feed_grad, gain, table, stat, *params_in, *firsts, *seconds]
     pad_cols = att.shape[1] - (3 * heads * DH + DH)
     return pl.pallas_call(
-        functools.partial(adam_kernel, heads, hidden_cols),
+        functools.partial(adam_kernel, heads, hidden_cols, 2 if direct else 1),
         in_specs=[vmem] * len(operands),
         out_specs=[vmem] * 18,
         out_shape=[jax.ShapeDtypeStruct(a.shape, F32) for a in params_in] * 3,
@@ -867,30 +875,27 @@
     )(*operands)
 
 
-def place_kernel(half, offs_ref, *refs):
-    pieces = refs[:-2]
-    out_ref, sems = refs[-2:]
-    copies = []
-    for at, piece in enumerate(pieces):
-        begin = pl.multiple_of(offs_ref[at], LANES)
-        copies.append(
-            pltpu.make_async_copy(piece, out_ref.at[pl.ds(begin, half)], sems.at[at])
-        )
-    for copy in copies:
-        copy.start()
-    for copy in copies:
-        copy.wait()
+def place_kernel(offs_ref, *refs):
+    step = pl.program_id(0)
+    for at, piece in enumerate(refs[:-1]):
+
+        @pl.when(step == at)
+        def _(piece=piece):
+            refs[-1][...] = piece[...]
 
 
 def place(pieces, offs, rows):
     half, width = pieces[0].shape
-    hbm = pl.BlockSpec(memory_space=ANY)
+    count = len(pieces)
     return pl.pallas_call(
-        functools.partial(place_kernel, half),
-        in_specs=[pl.BlockSpec(memory_space=pltpu.SMEM)] + [hbm] * len(pieces),
-        out_specs=hbm,
+        place_kernel,
+        grid_spec=pltpu.PrefetchScalarGridSpec(
+            num_scalar_prefetch=1,
+            grid=(count,),
+            in_specs=[pl.BlockSpec((half, width), lambda i, *_: (0, 0))] * count,
+            out_specs=pl.BlockSpec((half, width), lambda i, offs: (offs[i] // half, 0)),
+        ),
         out_shape=jax.ShapeDtypeStruct((rows, width), pieces[0].dtype),
-        scratch_shapes=[pltpu.SemaphoreType.DMA((len(pieces),))],
         compiler_params=params(),
         cost_estimate=pl.CostEstimate(
             flops=0, bytes_accessed=4 * rows * width, transcendentals=0
@@ -899,7 +904,30 @@
     )(offs, *pieces)
 
 
-def body(wide, narrow, *arguments):
+def bias_strip(bucket_bias, n, heads, length):
+    table = lax.dynamic_slice_in_dim(bucket_bias, n * heads, heads, 1).T
+    blocks = length // LANES
+    near_r = (
+        jnp.arange(3 * LANES, dtype=jnp.int32)[None, :]
+        - LANES
+        - jnp.arange(LANES, dtype=jnp.int32)[:, None]
+    )
+    near_ids = bucket_of(near_r)
+    near = sum(
+        jnp.where(near_ids == b, table[:, b][:, None, None], 0.0) for b in range(32) if b != 16
+    )
+    far_shape = (heads, LANES, (blocks - 2) * LANES)
+    return jnp.concatenate(
+        [
+            jnp.broadcast_to(table[:, 15][:, None, None], far_shape),
+            near,
+            jnp.broadcast_to(table[:, 31][:, None, None], far_shape),
+        ],
+        axis=2,
+    )
+
+
+def general_body(wide, narrow, *arguments):
     (
         block_input,
         cotangent,
@@ -923,7 +951,6 @@
     w = lax.axis_index("wide")
     n = lax.axis_index("narrow")
     core = n % 2
-    direct = wide == 8 and rows % 16 == 0
 
     def swap(value, wide_mask, narrow_mask):
         pairs = [
@@ -934,33 +961,12 @@
         return lax.ppermute(value, ("wide", "narrow"), pairs)
 
     def gather(piece):
-        if not direct:
-            return [lax.all_gather(piece, "wide", axis=0, tiled=True)]
-        found = {0: piece}
-        for mask in (2, 4, 6):
-            found[mask] = swap(piece, mask, 0)
-        for mask in (0, 2, 4, 6):
-            found[mask + 1] = swap(found[mask], 1, 0)
-        return [found[mask] for mask in range(8)]
+        return [lax.all_gather(piece, "wide", axis=0, tiled=True)]
 
     def reduce_wide(outs):
-        if not direct:
-            return [lax.psum_scatter(outs[0], "wide", scatter_dimension=0, tiled=True)]
-        evens, odds = outs[:4], outs[4:]
-        got = []
-        for e in (1, 2, 3, 0):
-            came = swap(odds[e], 1, 0)
-            if e:
-                mixed = (evens[e] + came.astype(F32)).astype(BF16)
-                got.append(swap(mixed, 2 * e, 0))
-            else:
-                kept = [evens[0], came]
-        return kept + got
-
-    if direct:
-        offs = (jnp.arange(8, dtype=jnp.int32) ^ w) * rows
-    else:
-        offs = jnp.zeros((1,), jnp.int32)
+        return [lax.psum_scatter(outs[0], "wide", scatter_dimension=0, tiled=True)]
+
+    offs = jnp.zeros((1,), jnp.int32)
     order = jnp.stack([1 - core, core, n // 2])
 
     p_piece = jnp.concatenate(
@@ -984,26 +990,7 @@
     s_pieces = gather(shrink_weight.astype(BF16).T)
 
     ends = jnp.cumsum(lengths, axis=1)
-    table = lax.dynamic_slice_in_dim(bucket_bias, n * heads, heads, 1).T
-    blocks = length // LANES
-    near_r = (
-        jnp.arange(3 * LANES, dtype=jnp.int32)[None, :]
-        - LANES
-        - jnp.arange(LANES, dtype=jnp.int32)[:, None]
-    )
-    near_ids = bucket_of(near_r)
-    near = sum(
-        jnp.where(near_ids == b, table[:, b][:, None, None], 0.0) for b in range(32) if b != 16
-    )
-    far_shape = (heads, LANES, (blocks - 2) * LANES)
-    strip = jnp.concatenate(
-        [
-            jnp.broadcast_to(table[:, 15][:, None, None], far_shape),
-            near,
-            jnp.broadcast_to(table[:, 31][:, None, None], far_shape),
-        ],
-        axis=2,
-    )
+    strip = bias_strip(bucket_bias, n, heads, length)
 
     normed_one, qkv, atts, logs, fours = [], [], [], [], []
     for b in range(buffers):
@@ -1057,7 +1044,7 @@
         d_middles.append(d_middle)
         lows.append((low, swap(low, 0, 1)))
 
-    count = 8 if direct else 1
+    count = 1
     feed_outs = grad_call(
         functools.partial(feed_grad_kernel, count, hidden_cols),
         "feed_grad",
@@ -1169,8 +1156,755 @@
     return (block_output, input_gradient, stat[0, 0], *results)
 
 
+class Place:
+    def __init__(self):
+        self.w = lax.axis_index("wide")
+        self.n = lax.axis_index("narrow")
+        self.z, self.x = self.w // 2, self.w % 2
+        self.y, self.core = self.n // 2, self.n % 2
+        self.n_far = (self.n + 2) % 4
+        self.across = (self.w, self.n_far)
+        self.beside = (self.w, self.n + 1 - 2 * self.core)
+        self.flip = (self.z * 2 + 1 - self.x, self.n)
+
+    def along(self, m):
+        return (((self.z + m) % 4) * 2 + self.x, self.n)
+
+    def from_z(self, m):
+        return ((self.z + 4 - m) % 4) * 2 + self.x
+
+    def from_x(self, m):
+        return ((self.z + 4 - m) % 4) * 2 + 1 - self.x
+
+    def meet(self):
+        barrier = pltpu.get_barrier_semaphore()
+        peers = [self.along(1), self.along(2), self.along(3), self.flip, self.across, self.beside]
+        for peer in peers:
+            pl.semaphore_signal(barrier, inc=1, device_id=peer, device_id_type=MESH)
+        pl.semaphore_wait(barrier, len(peers))
+
+
+def remote(source, target, send_sem, recv_sem, peer):
+    return pltpu.make_async_remote_copy(
+        src_ref=source,
+        dst_ref=target,
+        send_sem=send_sem,
+        recv_sem=recv_sem,
+        device_id=peer,
+        device_id_type=MESH,
+    )
+
+
+class Gather:
+    def __init__(self, spot, view, ssem, rsem):
+        self.spot, self.view, self.ssem, self.rsem = spot, view, ssem, rsem
+        self.sent = []
+
+    def push(self, owner, slot, peer):
+        copy = remote(
+            self.view(owner), self.view(owner), self.ssem.at[slot], self.rsem.at[owner], peer
+        )
+        copy.start()
+        self.sent.append((owner, slot, peer))
+
+    def begin(self):
+        for m in (1, 2, 3):
+            self.push(self.spot.w, m - 1, self.spot.along(m))
+        self.push(self.spot.w, 3, self.spot.flip)
+
+    def arrived(self, owner):
+        remote(
+            self.view(owner), self.view(owner), self.ssem.at[0], self.rsem.at[owner], self.spot.flip
+        ).wait_recv()
+
+    def forward(self, m):
+        owner = self.spot.from_z(m)
+        self.arrived(owner)
+        self.push(owner, 3 + m, self.spot.flip)
+
+    def finish(self):
+        for m in range(4):
+            self.arrived(self.spot.from_x(m))
+
+    def drain(self):
+        for m in (1, 2, 3):
+            remote(
+                self.view(self.spot.w),
+                self.view(self.spot.w),
+                self.ssem.at[m - 1],
+                self.rsem.at[0],
+                self.spot.along(m),
+            ).wait_send()
+        for m in range(4):
+            owner = self.spot.from_z(m)
+            remote(
+                self.view(owner), self.view(owner), self.ssem.at[3 + m], self.rsem.at[0], self.spot.flip
+            ).wait_send()
+
+
+def gather_attend_kernel(
+    buffers,
+    slots,
+    heads,
+    hidden_cols,
+    ends_ref,
+    x_ref,
+    strip_ref,
+    pw_ref,
+    ow_ref,
+    ew_ref,
+    sw_ref,
+    gn_ref,
+    normed_ref,
+    qkv_ref,
+    att_ref,
+    log_ref,
+    gains_ref,
+    pbuf,
+    obuf,
+    fbuf,
+    qs,
+    kt,
+    vs,
+    opad,
+    spad,
+    gpad,
+    ssems,
+    rsems,
+    lone_s,
+    lone_r,
+):
+    spot = Place()
+    spot.meet()
+    tokens, width = x_ref.shape
+    length = tokens // buffers
+    head_cols = heads * DH
+    rows = gn_ref.shape[1]
+    part = hidden_cols // 2
+    chunk = 3 * part
+
+    def at_rows(owner):
+        return pl.ds(pl.multiple_of(owner * rows, 16), rows)
+
+    mine = at_rows(spot.w)
+    gpad[...] = jnp.zeros_like(gpad)
+    gpad[0:2, 0:rows] = gn_ref[...]
+    pbuf[mine] = jnp.concatenate(
+        [pw_ref[0], pw_ref[1], pw_ref[2], gpad[...].T[:rows, :DH]], axis=1
+    ).astype(BF16)
+    projection = Gather(spot, lambda v: pbuf.at[at_rows(v)], ssems.at[0], rsems.at[0])
+    projection.begin()
+    opad[...] = jnp.zeros_like(opad)
+    opad[0:head_cols, 0:rows] = ow_ref[...]
+    obuf[spot.n, mine] = opad[...].T[:rows, :head_cols].astype(BF16)
+
+    def o_view(which):
+        return lambda v: obuf.at[which, at_rows(v)]
+
+    def o_across():
+        return remote(
+            obuf.at[spot.n, mine],
+            obuf.at[spot.n, mine],
+            lone_s.at[0],
+            lone_r.at[0],
+            spot.across,
+        )
+
+    def o_across_in():
+        return remote(
+            obuf.at[spot.n_far, mine],
+            obuf.at[spot.n_far, mine],
+            lone_s.at[0],
+            lone_r.at[0],
+            spot.across,
+        )
+
+    o_across().start()
+    spad[...] = jnp.zeros_like(spad)
+    spad[:, 0:rows] = sw_ref[...]
+    turned = spad[...].T[:rows].astype(BF16)
+    for j in range(2):
+        span = slice(j * part, (j + 1) * part)
+        fbuf[mine, j * chunk : j * chunk + part] = ew_ref[0, :, span].astype(BF16)
+        fbuf[mine, j * chunk + part : j * chunk + 2 * part] = ew_ref[1, :, span].astype(BF16)
+        fbuf[mine, j * chunk + 2 * part : (j + 1) * chunk] = turned[:, span]
+    out_near = Gather(spot, o_view(spot.n), ssems.at[1], rsems.at[1])
+    out_far = Gather(spot, o_view(spot.n_far), ssems.at[2], rsems.at[2])
+    feeds = [
+        Gather(
+            spot,
+            lambda v, j=j: fbuf.at[at_rows(v), j * chunk : (j + 1) * chunk],
+            ssems.at[3 + j],
+            rsems.at[3 + j],
+        )
+        for j in range(2)
+    ]
+    for m in (1, 2, 3):
+        projection.forward(m)
+    o_across_in().wait_recv()
+    out_near.begin()
+    out_far.begin()
+    feeds[0].begin()
+    projection.finish()
+
+    gain_cols = pbuf[:, 4 * LANES :].astype(F32).T
+    first = 3 * head_cols - 4 * LANES
+    gains = gain_cols[first : first + 8]
+    gains_ref[...] = gains
+    gain_one = gains[0:1]
+    step = 256
+    per = length // step
+
+    for b in range(buffers):
+
+        @pl.loop(0, per)
+        def _(block, b=b):
+            begin = pl.multiple_of(block * step, step)
+            here = pl.ds(begin, step)
+            span = pl.ds(pl.multiple_of(b * length + begin, step), step)
+            values = x_ref[span].astype(F32)
+            normed = (values * rms_scale(values) * gain_one).astype(BF16)
+            normed_ref[span] = normed
+            qkv = mm(normed, pbuf[...]).astype(BF16)
+            qkv_ref[span] = qkv[:, : 3 * head_cols]
+            for h in range(heads):
+                qs[b, h, here] = qkv[:, h * DH : (h + 1) * DH]
+                kt[b, h, :, here] = qkv[:, head_cols + h * DH : head_cols + (h + 1) * DH].T
+                vs[b, h, here] = qkv[:, 2 * head_cols + h * DH : 2 * head_cols + (h + 1) * DH]
+
+    def relay_out():
+        for m in (1, 2, 3):
+            out_near.forward(m)
+            out_far.forward(m)
+
+    def att_view(which, b):
+        return att_ref.at[which, b * length : (b + 1) * length]
+
+    def share(which, slot, peer):
+        return remote(which, which, lone_s.at[slot], lone_r.at[slot], peer)
+
+    n_beside = spot.beside[1]
+    n_diag = (n_beside + 2) % 4
+
+    def out_beside():
+        out_near.finish()
+        out_far.finish()
+        share(obuf.at[spot.n], 1, spot.beside).start()
+        share(obuf.at[spot.n_far], 2, spot.beside).start()
+
+    def att_send(b):
+        share(att_view(spot.n, b), 3 + 3 * b, spot.across).start()
+        share(att_view(spot.n, b), 4 + 3 * b, spot.beside).start()
+
+    def att_relay(b):
+        share(att_view(spot.n_far, b), 3 + 3 * b, spot.across).wait_recv()
+        share(att_view(spot.n_far, b), 5 + 3 * b, spot.beside).start()
+
+    blocks = length // LANES
+
+    def run(b, events):
+        seg_keys = segments(
+            lax.broadcasted_iota(jnp.int32, (1, length), 1), ends_ref, b, slots
+        )
+
+        @pl.loop(0, blocks)
+        def _(block):
+            for when, what in events.items():
+                pl.when(block == when)(what)
+            begin = pl.multiple_of(block * LANES, LANES)
+            here = pl.ds(begin, LANES)
+            span = pl.ds(pl.multiple_of(b * length + begin, LANES), LANES)
+            window = pl.ds(pl.multiple_of((blocks - 1 - block) * LANES, LANES), length)
+            seg_rows = segments(
+                lax.broadcasted_iota(jnp.int32, (LANES, 1), 0) + begin, ends_ref, b, slots
+            )
+            same = seg_rows == seg_keys
+            lane = lax.broadcasted_iota(jnp.int32, (LANES, LANES), 1)
+            logs = jnp.zeros((LANES, LANES), F32)
+            outs = []
+            for h in range(heads):
+                scores = mm(qs[b, h, here], kt[b, h]) + strip_ref[h, :, window]
+                scores = jnp.where(same, scores, masked_score)
+                row_max = jnp.max(scores, axis=1, keepdims=True)
+                raised = jnp.exp(scores - row_max)
+                total = jnp.sum(raised, axis=1, keepdims=True)
+                probs = (raised * (1.0 / total)).astype(BF16)
+                outs.append(mm(probs, vs[b, h]).astype(BF16))
+                logs = jnp.where(lane == h, row_max + jnp.log(total), logs)
+            log_ref[span] = logs
+            att_ref[spot.n, span] = jnp.concatenate(outs, axis=1)
+
+    def feed_turn():
+        feeds[0].forward(3)
+        feeds[1].begin()
+
+    run(
+        0,
+        {
+            0: relay_out,
+            2: lambda: feeds[0].forward(1),
+            3: lambda: feeds[0].forward(2),
+            4: feed_turn,
+            5: out_beside,
+        },
+    )
+    att_send(0)
+    run(
+        1,
+        {
+            2: lambda: att_relay(0),
+            3: lambda: feeds[1].forward(1),
+            4: lambda: feeds[1].forward(2),
+            5: lambda: feeds[1].forward(3),
+        },
+    )
+    att_send(1)
+    att_relay(1)
+    feeds[0].finish()
+    feeds[1].finish()
+    share(obuf.at[n_beside], 1, spot.beside).wait_recv()
+    share(obuf.at[n_diag], 2, spot.beside).wait_recv()
+    for b in range(buffers):
+        share(att_view(n_beside, b), 4 + 3 * b, spot.beside).wait_recv()
+        share(att_view(n_diag, b), 5 + 3 * b, spot.beside).wait_recv()
+    o_across().wait_send()
+    for group in (projection, out_near, out_far, *feeds):
+        group.drain()
+    share(obuf.at[spot.n], 1, spot.beside).wait_send()
+    share(obuf.at[spot.n_far], 2, spot.beside).wait_send()
+    for b in range(buffers):
+        share(att_view(spot.n, b), 3 + 3 * b, spot.across).wait_send()
+        share(att_view(spot.n, b), 4 + 3 * b, spot.beside).wait_send()
+        share(att_view(spot.n_far, b), 5 + 3 * b, spot.beside).wait_send()
+
+
+def gather_attend(ends, x, strip, pw, ow, ew, sw, gn, length):
+    tokens, width = x.shape
+    buffers = tokens // length
+    heads = strip.shape[0]
+    head_cols = heads * DH
+    hidden_cols = ew.shape[2]
+    vmem = pl.BlockSpec(memory_space=pltpu.VMEM)
+    return pl.pallas_call(
+        functools.partial(gather_attend_kernel, buffers, ends.shape[1], heads, hidden_cols),
+        in_specs=[pl.BlockSpec(memory_space=pltpu.SMEM)] + [vmem] * 7,
+        out_specs=[vmem] * 8,
+        out_shape=[
+            jax.ShapeDtypeStruct((tokens, width), BF16),
+            jax.ShapeDtypeStruct((tokens, 3 * head_cols), BF16),
+            jax.ShapeDtypeStruct((4, tokens, head_cols), BF16),
+            jax.ShapeDtypeStruct((tokens, LANES), F32),
+            jax.ShapeDtypeStruct((8, width), F32),
+            jax.ShapeDtypeStruct((width, 3 * head_cols + DH), BF16),
+            jax.ShapeDtypeStruct((4, width, head_cols), BF16),
+            jax.ShapeDtypeStruct((width, 3 * hidden_cols), BF16),
+        ],
+        scratch_shapes=[
+            pltpu.VMEM((buffers, heads, length, DH), BF16),
+            pltpu.VMEM((buffers, heads, DH, length), BF16),
+            pltpu.VMEM((buffers, heads, length, DH), BF16),
+            pltpu.VMEM((2 * LANES, LANES), F32),
+            pltpu.VMEM((hidden_cols, LANES), F32),
+            pltpu.VMEM((LANES, LANES), F32),
+            pltpu.SemaphoreType.DMA((5, 7)),
+            pltpu.SemaphoreType.DMA((5, 8)),
+            pltpu.SemaphoreType.DMA((9,)),
+            pltpu.SemaphoreType.DMA((9,)),
+        ],
+        compiler_params=params(collective_id=1, has_side_effects=True),
+        cost_estimate=pl.CostEstimate(
+            flops=16 << 30, bytes_accessed=24 << 20, transcendentals=8 << 20
+        ),
+        name="gather_attend",
+    )(ends, x, strip, pw, ow, ew, sw, gn)
+
+
+def feed_forward_kernel(
+    buffers,
+    hidden_cols,
+    x_ref,
+    cot_ref,
+    att_ref,
+    gains_ref,
+    obuf,
+    fbuf,
+    low_ref,
+    d_ref,
+    middle_ref,
+    ff_sum,
+    gain_sum,
+    even_ref,
+    odd_ref,
+    normed,
+    hid,
+    dg,
+    total,
+    ff_out,
+    ff_in,
+    dn_out,
+    dn_keep,
+    dn_in,
+    dn_sum,
+    dn_far,
+    sends,
+    recvs,
+):
+    spot = Place()
+    spot.meet()
+    tokens, width = x_ref.shape
+    length = tokens // buffers
+    half = length // 2
+    part = hidden_cols // 2
+    chunk = 3 * part
+    core = spot.core
+    k0 = 0.7978845608028654
+    k1 = 0.044715
+    gain_two = gains_ref[1:2]
+
+    def ff_core(b):
+        return remote(ff_out.at[b], ff_in.at[b], sends.at[b], recvs.at[b], spot.beside)
+
+    def dn_core(b):
+        return remote(dn_out.at[b], dn_in.at[b], sends.at[2 + b], recvs.at[2 + b], spot.beside)
+
+    def dn_across(b):
+        return remote(dn_sum.at[b], dn_far.at[b], sends.at[4 + b], recvs.at[4 + b], spot.across)
+
+    def low_rows(b, which):
+        return pl.ds(pl.multiple_of(b * length + which * half, LANES), half)
+
+    def low_core(b):
+        view = low_ref.at[low_rows(b, core)]
+        return remote(view, view, sends.at[6 + b], recvs.at[6 + b], spot.beside)
+
+    def low_core_in(b):
+        view = low_ref.at[low_rows(b, 1 - core)]
+        return remote(view, view, sends.at[6 + b], recvs.at[6 + b], spot.beside)
+
+    gain_sum[...] = jnp.zeros_like(gain_sum)
+
+    @pl.loop(0, 2 * buffers)
+    def _(i):
+        b = i // 2
+        keep = i % 2
+        which = (1 - core) * (1 - keep) + core * keep
+        rows = low_rows(b, which)
+        attention = jnp.zeros((half, width), F32)
+        for a in range(4):
+            attention = attention + mm(att_ref[a, rows], obuf[a], NT)
+        middle = x_ref[rows].astype(F32) + attention
+        scale_two = rms_scale(middle)
+        normed_rows = (middle * scale_two * gain_two).astype(BF16)
+        normed[rows] = normed_rows
+        cot = cot_ref[rows]
+        ff = jnp.zeros((half, width), F32)
+        dn = jnp.zeros((half, width), F32)
+        for j in range(2):
+            at = j * chunk
+            both = mm(normed_rows, fbuf[:, at : at + 2 * part])
+            gate, up = both[:, :part], both[:, part:]
+            square = gate * gate
+            tanh = jnp.tanh(k0 * (gate + k1 * (square * gate)))
+            lift = 0.5 * (1.0 + tanh)
+            active = gate * lift
+            slope = lift + (0.5 * gate) * (1.0 - tanh * tanh) * (k0 + (3.0 * k0 * k1) * square)
+            d_hidden = mm(cot, fbuf[:, at + 2 * part : at + 3 * part])
+            hid[rows, j * part : (j + 1) * part] = (active * up).astype(BF16)
+            dg[rows, 2 * j * part : (2 * j + 1) * part] = (d_hidden * up * slope).astype(BF16)
+            dg[rows, (2 * j + 1) * part : (2 * j + 2) * part] = (d_hidden * active).astype(BF16)
+            ff = ff + mm(
+                hid[rows, j * part : (j + 1) * part], fbuf[:, at + 2 * part : at + 3 * part], NT
+            )
+            dn = dn + mm(
+                dg[rows, 2 * j * part : (2 * j + 2) * part], fbuf[:, at : at + 2 * part], NT
+            )
+        gain_sum[...] = gain_sum[...] + fold_rows(dn * middle * scale_two)
+
+        @pl.when(keep == 0)
+        def _():
+            dn_out[b] = dn.astype(BF16)
+            dn_core(b).start()
+            ff_out[b] = ff.astype(BF16)
+            ff_core(b).start()
+
+        @pl.when(keep == 1)
+        def _():
+            middle_ref[b] = middle
+            dn_core(b).wait_recv()
+            dn_sum[b] = (dn.astype(BF16).astype(F32) + dn_in[b].astype(F32)).astype(BF16)
+            dn_across(b).start()
+            ff_core(b).wait_recv()
+            ff_sum[b] = (ff.astype(BF16).astype(F32) + ff_in[b].astype(F32)).astype(BF16)
+
+    def finish_middle(b):
+        dn_across(b).wait_recv()
+
+        @pl.loop(0, 3)
+        def _(i):
+            span = pl.ds(pl.multiple_of(i * LANES, LANES), LANES)
+            rows = pl.ds(
+                pl.multiple_of(b * length + core * half + i * LANES, LANES), LANES
+            )
+            upstream = dn_sum[b, span].astype(F32) + dn_far[b, span].astype(F32)
+            middle = middle_ref[b, span]
+            d_middle = cot_ref[rows].astype(F32) + norm_back(
+                middle, rms_scale(middle), gain_two, upstream
+            )
+            d_ref[b, span] = d_middle
+            low_ref[rows] = d_middle.astype(BF16)
+
+        low_core(b).start()
+
+    finish_middle(0)
+    step = 256
+    for begin in range(0, width, step):
+        cols = slice(begin, begin + step)
+        for j in range(2):
+            at = j * chunk
+            total[cols, at : at + 2 * part] = mm(
+                normed[:, cols], dg[:, 2 * j * part : (2 * j + 2) * part], TN
+            )
+            total[cols, at + 2 * part : at + 3 * part] = mm(
+                cot_ref[:, cols], hid[:, j * part : (j + 1) * part], TN
+            )
+    spread(spot, total, even_ref, odd_ref)
+    finish_middle(1)
+    for b in range(buffers):
+        low_core_in(b).wait_recv()
+        ff_core(b).wait_send()
+        dn_core(b).wait_send()
+        dn_across(b).wait_send()
+        low_core(b).wait_send()
+
+
+def spread(spot, total, even_ref, odd_ref):
+    rows = even_ref.shape[1]
+    for m in range(4):
+        base = ((spot.z + m) % 4) * 2
+        near = pl.ds(pl.multiple_of((base + spot.x) * rows, 8), rows)
+        far = pl.ds(pl.multiple_of((base + 1 - spot.x) * rows, 8), rows)
+        even_ref[m] = total[near]
+        odd_ref[m] = total[far].astype(BF16)
+
+
+def feed_forward(x, cot, att, gains, obuf, fbuf, length, rows):
+    tokens, width = x.shape
+    buffers = tokens // length
+    half = length // 2
+    hidden_cols = fbuf.shape[1] // 3
+    vmem = pl.BlockSpec(memory_space=pltpu.VMEM)
+    return pl.pallas_call(
+        functools.partial(feed_forward_kernel, buffers, hidden_cols),
+        in_specs=[vmem] * 6,
+        out_specs=[vmem] * 7,
+        out_shape=[
+            jax.ShapeDtypeStruct((tokens, width), BF16),
+            jax.ShapeDtypeStruct((buffers, half, width), F32),
+            jax.ShapeDtypeStruct((buffers, half, width), F32),
+            jax.ShapeDtypeStruct((buffers, half, width), BF16),
+            jax.ShapeDtypeStruct((8, width), F32),
+            jax.ShapeDtypeStruct((4, rows, 3 * hidden_cols), F32),
+            jax.ShapeDtypeStruct((4, rows, 3 * hidden_cols), BF16),
+        ],
+        scratch_shapes=[
+            pltpu.VMEM((tokens, width), BF16),
+            pltpu.VMEM((tokens, hidden_cols), BF16),
+            pltpu.VMEM((tokens, 2 * hidden_cols), BF16),
+            pltpu.VMEM((width, 3 * hidden_cols), F32),
+        ]
+        + [pltpu.VMEM((buffers, half, width), BF16)] * 7
+        + [pltpu.SemaphoreType.DMA((8,)), pltpu.SemaphoreType.DMA((8,))],
+        compiler_params=params(collective_id=2, has_side_effects=True),
+        cost_estimate=pl.CostEstimate(
+            flops=20 << 30, bytes_accessed=24 << 20, transcendentals=1 << 20
+        ),
+        name="feed_forward",
+    )(x, cot, att, gains, obuf, fbuf)
+
+
+def direct_body(wide, narrow, *arguments):
+    (
+        block_input,
+        cotangent,
+        lengths,
+        project_weight,
+        output_weight,
+        expand_weight,
+        shrink_weight,
+        bucket_bias,
+        norm_gains,
+    ) = arguments[:9]
+    firsts = arguments[9:15]
+    seconds = arguments[15:21]
+    tokens, width = block_input.shape
+    buffers = lengths.shape[0]
+    length = tokens // buffers
+    rows = norm_gains.shape[1]
+    head_cols = project_weight.shape[2]
+    heads = head_cols // DH
+    hidden_cols = expand_weight.shape[2]
+    w = lax.axis_index("wide")
+    n = lax.axis_index("narrow")
+    core = n % 2
+
+    def move(value, wide_step=0, flip=0, narrow_mask=0):
+        def target(a):
+            return ((a // 2 + wide_step) % 4) * 2 + (a % 2 ^ flip)
+
+        pairs = [
+            (a * narrow + b, target(a) * narrow + (b ^ narrow_mask))
+            for a in range(wide)
+            for b in range(narrow)
+        ]
+        return lax.ppermute(value, ("wide", "narrow"), pairs)
+
+    def reduce_wide(evens, odds):
+        kept = [evens[0], move(odds[0], flip=1)]
+        for m in (1, 2, 3):
+            mixed = (evens[m] + move(odds[m], flip=1).astype(F32)).astype(BF16)
+            kept.append(move(mixed, wide_step=m))
+        return kept
+
+    ends = jnp.cumsum(lengths, axis=1)
+    order = jnp.stack([1 - core, core, n // 2])
+    strip = bias_strip(bucket_bias, n, heads, length)
+    normed_one, qkv, att, logs, gains, pbuf, obuf, fbuf = gather_attend(
+        ends,
+        block_input,
+        strip,
+        project_weight,
+        output_weight,
+        expand_weight,
+        shrink_weight,
+        norm_gains,
+        length,
+    )
+    low, d_middle, middle, ff_sum, gain_two, feed_even, feed_odd = feed_forward(
+        block_input, cotangent, att, gains, obuf, fbuf, length, rows
+    )
+    feed_group = reduce_wide(feed_even, feed_odd)
+
+    def core_sum(kept, sent):
+        return (kept.astype(F32) + move(sent, narrow_mask=1).astype(F32)).astype(BF16)
+
+    offs = jnp.zeros((1,), jnp.int32)
+    own = lax.dynamic_index_in_dim(obuf, n, 0, keepdims=False)
+    att_own = lax.dynamic_index_in_dim(att, n, 0, keepdims=False)
+    dqkv, dn_one, sums_one, strips = [], [], [], []
+    half = length // 2
+    for b in range(buffers):
+        part = lambda which: lax.dynamic_slice_in_dim(low, b * length + which * half, half, 0)
+        span = slice(b * length, (b + 1) * length)
+        _, grads, dn_send, dn_keep, sums, dstrip = back(
+            b,
+            ends,
+            offs,
+            order,
+            part(core),
+            part(1 - core),
+            qkv[span],
+            logs[span],
+            strip,
+            block_input,
+            [own],
+            [pbuf],
+            heads,
+        )
+        dqkv.append(grads)
+        sums_one.append(sums)
+        strips.append(dstrip)
+        dn_one.append(core_sum(dn_keep, dn_send))
+
+    gain_at = 3 * head_cols
+    halves = lambda value: [value[b * length : (b + 1) * length] for b in range(buffers)]
+    (att_total,) = grad_call(
+        functools.partial(attend_grad_kernel, 1, heads),
+        "attend_grad",
+        offs,
+        [
+            *halves(normed_one),
+            *dqkv,
+            *halves(low),
+            *halves(att_own),
+            jnp.stack(sums_one + [gain_two, jnp.zeros_like(gain_two)]),
+        ],
+        width,
+        gain_at + DH + head_cols,
+        1,
+        rows,
+        2 * tokens * width * 4 * head_cols,
+    )
+    near = [
+        lax.dynamic_slice_in_dim(att_total, ((w // 2 + m) % 4 * 2 + w % 2) * rows, rows, 0)
+        for m in range(4)
+    ]
+    far = [
+        lax.dynamic_slice_in_dim(att_total, ((w // 2 + m) % 4 * 2 + 1 - w % 2) * rows, rows, 0)
+        for m in range(4)
+    ]
+    att_group = reduce_wide(near, [value.astype(BF16) for value in far])
+    vmem = pl.BlockSpec(memory_space=pltpu.VMEM)
+    bucket = pl.pallas_call(
+        functools.partial(bucket_kernel, heads),
+        in_specs=[vmem, vmem],
+        out_specs=vmem,
+        out_shape=jax.ShapeDtypeStruct((8, LANES), F32),
+        compiler_params=params(),
+        cost_estimate=pl.CostEstimate(flops=8 << 20, bytes_accessed=4 << 20, transcendentals=0),
+        name="bucket",
+    )(*strips)
+
+    half_offs = jnp.stack(
+        [b * length + which * half for b in range(buffers) for which in (core, 1 - core)]
+    )
+    out_halves, in_halves = [], []
+    for b in range(buffers):
+        (out_half,) = half_call(
+            output_kernel,
+            "output",
+            b,
+            order,
+            [ff_sum[b], move(ff_sum[b], narrow_mask=2), middle[b]],
+            (),
+            (BF16,),
+        )
+        out_halves += [out_half, move(out_half, narrow_mask=1)]
+        (in_half,) = half_call(
+            input_kernel,
+            "input",
+            b,
+            order,
+            [dn_one[b], move(dn_one[b], narrow_mask=2), block_input, d_middle[b]],
+            (2,),
+            (BF16,),
+            gains,
+        )
+        in_halves += [in_half, move(in_half, narrow_mask=1)]
+    block_output = place(out_halves, half_offs, tokens)
+    input_gradient = place(in_halves, half_offs, tokens)
+
+    att_grad, feed_grad, stat, gain, table_sum = norm_call(
+        wide, narrow, [att_group, feed_group], bucket, gain_at
+    )
+    results = adam_call(
+        att_grad,
+        feed_grad,
+        gain,
+        table_sum,
+        stat,
+        arguments[3:9],
+        firsts,
+        seconds,
+        heads,
+        hidden_cols,
+        direct=True,
+    )
+    return (block_output, input_gradient, stat[0, 0], *results)
+
+
 def solution(mesh):
     wide, narrow = mesh.shape["wide"], mesh.shape["narrow"]
+    body = direct_body if (wide, narrow) == (8, 4) else general_body
     state = (
         P(None, "wide", "narrow"),
         P("narrow", "wide"),

time: 494 us -> 355 us (0.72)
  Pallas kernels: 306 us -> 217 us
  starting transfers between devices: 72.9 us -> 16.8 us
  local copies, waits for them, and re-layouts: 23.6 us -> 47 us
  waiting for transfers between devices: 69.5 us -> 52.5 us
    pallas_call x8 -> x6, Pallas kernels: 215 us -> 145 us  [the longest x1 71.4 us: gather_attend(): pl.pallas_call(functools.partial(gather_attend_kernel, buffers, ends.shap...]
    ppermute x75 -> x24, starting transfers between devices: 72.9 us -> 16.8 us  [move(): return lax.ppermute(value, ('wide', 'narrow'), pairs)]
    ppermute x75 -> x24, waiting for transfers between devices: 69.5 us -> 52.5 us  [move(): return lax.ppermute(value, ('wide', 'narrow'), pairs)]
    slice x3 -> x8, local copies, waits for them, and re-layouts: 2.02 us -> 13 us  [the longest x3 6.87 us: direct_body(): value[b * length:(b + 1) * length]]
    pallas_call x6 -> x4, Pallas kernels: 27.1 us -> 17 us  [half_call(): pl.pallas_call(kernel, grid_spec=pltpu.PrefetchScalarGridSpec(num_scalar_...]
    pallas_call x2 -> x1, Pallas kernels: 16.7 us -> 7.59 us  [grad_call(): pl.pallas_call(kernel, in_specs=[pl.BlockSpec(memory_space=pltpu.SMEM)] +...]
    squeeze x2 -> x6, local copies, waits for them, and re-layouts: 0.03 us -> 8.15 us  [the longest x1 2.35 us: reduce_wide(): mixed = (evens[m] + move(odds[m], flip=1).astype(F32)).astype(BF16)]
    unnamed x217 -> x90, local copies, waits for them, and re-layouts: 20.3 us -> 21.1 us
  transfers between devices with their start and end apart: 75 -> 24, of which waited for: 18 -> 8; matrix products, arithmetic and copies ran while one was open for 6% -> 13% of each run, Pallas kernels for 48% -> 25%
where the time goes in v2:
time: 355 us; the launch traced here: 349 us
  Pallas kernels  217 us (61%)
  waiting for transfers between devices  52.5 us (15%)
  local copies, waits for them, and re-layouts  47 us (13%)
  starting transfers between devices  16.8 us (5%)
  other arithmetic  14.7 us (4%)
    pallas_call x1, Pallas kernels, gather_attend(): pl.pallas_call(functools.partial(gather_attend_kernel, buffers, ends.shap...  71.4 us
    pallas_call x1, Pallas kernels, feed_forward(): pl.pallas_call(functools.partial(feed_forward_kernel, buffers, hidden_col...  55.5 us
    ppermute x24, waiting for transfers between devices, move(): return lax.ppermute(value, ('wide', 'narrow'), pairs)  52.5 us
    pallas_call x2, Pallas kernels, back(): pl.pallas_call(functools.partial(back_kernel, buffer, ends.shape[1], head...  35.4 us
    unnamed x90, local copies, waits for them, and re-layouts  21.1 us
    pallas_call x4, Pallas kernels, half_call(): pl.pallas_call(kernel, grid_spec=pltpu.PrefetchScalarGridSpec(num_scalar_...  17 us
    ppermute x24, starting transfers between devices, move(): return lax.ppermute(value, ('wide', 'narrow'), pairs)  16.8 us
    pallas_call x1, Pallas kernels, norm_call(): pl.pallas_call(functools.partial(norm_kernel, wide, narrow, lists, gain_a...  12.3 us
  transfers between devices with their start and end apart: 24, of which 8 were waited for; matrix products, arithmetic and copies ran while one was open for 13% of the time, Pallas kernels for 25%

profile of v2, /device:TPU:0, one launch (start us, length us, event | category | flops | bytes accessed | tf_op | source)
XLA Modules:
  0.0 349.4 jit_solution(8802759815472913952)
XLA Ops:
  10.6 71.4 %gather_attend.1 = (bf16[1536,768]{1,0:T(8,128)(2,1)}, bf16[1536,576]{1,0:T(8,128)(2,1)}, bf16[4,1536,192]{2,1,0:T(8,128)(2,1)}, f32[1536,128]{1,0:T(8,128)}, f3...) custom-call(s32[2,12]{1,0:T(2,128)} %reduce_window_sum.11.ends_ref, ...), custom_call_target="tpu_custom_call" | custom-call | flops 17179869184 | bytes 25165824 | tf_op jit(solution)/shard_map/gather_attend/pallas_call | solution.py:1488
  82.1 55.5 %feed_forward.1 = (bf16[1536,768]{1,0:T(8,128)(2,1)}, f32[2,384,768]{2,1,0:T(8,128)}, f32[2,384,768]{2,1,0:T(8,128)}, bf16[2,384,768]{2,1,0:T(8,128)(2,1)}, f32[...) custom-call(bf16[1536,768]{1,0:T(8,128)(2,1)} %x_ref.7, bf16[1536,768]{1,0:T(8,128)(2,1)} %cot_ref.1, ...), custom_call_target="tpu_custom_call" | custom-call | flops 21474836480 | bytes 25165824 | tf_op jit(solution)/shard_map/feed_forward/pallas_call | solution.py:1696
  144.7 3.1 fusion.16
  149.8 17.6 %back.2 = (bf16[768,768]{1,0:T(8,128)(2,1)}, bf16[768,576]{1,0:T(8,128)(2,1)}, bf16[384,768]{1,0:T(8,128)(2,1)}, bf16[384,768]{1,0:T(8,128)(2,1)}, f32[8,768]{1,0:T(8,128)}, /*index=5*/f32[3,128,1408]{2,1,0:T(8,128)}) custom-call(s32[2,12]{1,0:T(2,128)} %reduce_window_sum.11.ends_ref, s32[1]{0:T(128)} %constant.198.clone.1.offs_ref, ...), custom_call_target="tpu_custom_call" | custom-call | flops 4529848320 | bytes 16777216 | tf_op jit(solution)/shard_map/back/pallas_call | solution.py:531
  167.5 17.8 %back.3 = (bf16[768,768]{1,0:T(8,128)(2,1)}, bf16[768,576]{1,0:T(8,128)(2,1)}, bf16[384,768]{1,0:T(8,128)(2,1)}, bf16[384,768]{1,0:T(8,128)(2,1)}, f32[8,768]{1,0:T(8,128)}, /*index=5*/f32[3,128,1408]{2,1,0:T(8,128)}) custom-call(s32[2,12]{1,0:T(2,128)} %reduce_window_sum.11.ends_ref, s32[1]{0:T(128)} %constant.198.clone.1.offs_ref, ...), custom_call_target="tpu_custom_call" | custom-call | flops 4529848320 | bytes 16777216 | tf_op jit(solution)/shard_map/back/pallas_call | solution.py:531
  189.6 3.2 fusion.15
  193.6 7.6 %attend_grad.1 = f32[768,832]{1,0:T(8,128)} custom-call(s32[1]{0:T(128)} %constant.198.clone.1.offs_ref, bf16[768,768]{1,0:T(8,128)(2,1)} %get-tuple-element.206.refs_0_, bf16[768,768]{1,0:T(8,128)(2,1)} %get-tuple-element.205.refs_1_, bf16[768,576]{1,0:T(8,128)(2,1)} %get-tuple-element.85.refs_2_, bf16[768,576]{1,0:T(8,128)(2,1)} %get-tuple-element.86.refs_3_, ...), custom_call_target="tpu_custom_call" | custom-call | flops 3623878656 | bytes 14680064 | tf_op jit(solution)/shard_map/attend_grad/pallas_call | solution.py:632
  208.6 2.4 collective-permute-done.15
  211.0 3.6 %collective-permute-done.13 = bf16[96,832]{1,0:T(8,128)(2,1)S(1)} collective-permute-done((bf16[96,832]{1,0:T(8,128)(2,1)S(1)}, bf16[96,832]{1,0:T(8,128)(2,1)S(1)}, u32[]{:S(2)}, u32[]{:S(2)}) %collective-permute-start.13) | collective-permute-done | bytes 159776 | tf_op jit(solution)/shard_map/ppermute | solution.py:1759
  218.0 6.6 %collective-permute-done.11 = bf16[96,832]{1,0:T(8,128)(2,1)S(1)} collective-permute-done((bf16[96,832]{1,0:T(8,128)(2,1)S(1)}, bf16[96,832]{1,0:T(8,128)(2,1)S(1)}, u32[]{:S(2)}, u32[]{:S(2)}) %collective-permute-start.11) | collective-permute-done | bytes 159776 | tf_op jit(solution)/shard_map/ppermute | solution.py:1759
  225.0 2.5 collective-permute-done.10.refs_1_
  236.0 3.8 %collective-permute-done.17.refs_6_ = bf16[96,1536]{1,0:T(8,128)(2,1)S(1)} collective-permute-done((bf16[96,1536]{1,0:T(8,128)(2,1)S(1)}, bf16[96,1536]{1,0:T(8,128)(2,1)S(1)}, u32[]{:S(2)}, u32[]{:S(2)}) %collective-permute-start.17) | collective-permute-done | bytes 294944 | tf_op jit(solution)/shard_map/ppermute | solution.py:1759
  241.9 11.6 %collective-permute-done.far = bf16[384,768]{1,0:T(8,128)(2,1)S(1)} collective-permute-done((bf16[384,768]{1,0:T(8,128)(2,1)S(1)}, bf16[384,768]{1,0:T(8,128)(2,1)S(1)}, u32[]{:S(2)}, u32[]{:S(2)}) %collective-permute-start) | collective-permute-done | bytes 589856 | tf_op jit(solution)/shard_map/ppermute | solution.py:1759
  254.0 12.1 %collective-permute-done.5.far = bf16[384,768]{1,0:T(8,128)(2,1)S(1)} collective-permute-done((bf16[384,768]{1,0:T(8,128)(2,1)S(1)}, bf16[384,768]{1,0:T(8,128)(2,1)S(1)}, u32[]{:S(2)}, u32[]{:S(2)}) %collective-permute-start.5) | collective-permute-done | bytes 589856 | tf_op jit(solution)/shard_map/ppermute | solution.py:1759
  266.4 9.8 %collective-permute-done.8.far = bf16[384,768]{1,0:T(8,128)(2,1)S(1)} collective-permute-done((bf16[384,768]{1,0:T(8,128)(2,1)S(1)}, bf16[384,768]{1,0:T(8,128)(2,1)S(1)}, u32[]{:S(2)}, u32[]{:S(2)}) %collective-permute-start.8) | collective-permute-done | bytes 589856 | tf_op jit(solution)/shard_map/ppermute | solution.py:1759
  278.3 4.0 %output.2.refs_0_ = bf16[384,768]{1,0:T(8,128)(2,1)} custom-call(s32[3]{0:T(128)} %pad_add_fusion.1.order_ref, bf16[384,768]{1,0:T(8,128)(2,1)} %copy-done.10, bf16[384,768]{1,0:T(8,128)(2,1)} %copy-done.20, f32[384,768]{1,0:T(8,128)} %get-tuple-element.214.middle_ref), custom_call_target="tpu_custom_call" | custom-call | flops 5898240 | bytes 3538944 | tf_op jit(solution)/shard_map/output/pallas_call | solution.py:381
  282.4 4.0 %output.3.refs_2_ = bf16[384,768]{1,0:T(8,128)(2,1)} custom-call(s32[3]{0:T(128)} %pad_add_fusion.1.order_ref, bf16[384,768]{1,0:T(8,128)(2,1)} %copy-done.9, bf16[384,768]{1,0:T(8,128)(2,1)} %copy-done.19, f32[384,768]{1,0:T(8,128)} %get-tuple-element.213.middle_ref), custom_call_target="tpu_custom_call" | custom-call | flops 5898240 | bytes 3538944 | tf_op jit(solution)/shard_map/output/pallas_call | solution.py:381
  286.4 4.4 %input.2.refs_0_ = bf16[384,768]{1,0:T(8,128)(2,1)} custom-call(s32[3]{0:T(128)} %pad_add_fusion.1.order_ref, bf16[384,768]{1,0:T(8,128)(2,1)} %copy-done.7, bf16[384,768]{1,0:T(8,128)(2,1)} %copy-done.21, bf16[1536,768]{1,0:T(8,128)(2,1)} %x_ref.7, f32[384,768]{1,0:T(8,128)} %get-tuple-element.208.d_ref, f32[8,768]{1,0:T(8,128)} %get-tuple-element.70.gains_ref), custom_call_target="tpu_custom_call" | custom-call | flops 5898240 | bytes 3538944 | tf_op jit(solution)/shard_map/input/pallas_call | solution.py:381
  290.9 4.6 %input.3.refs_2_ = bf16[384,768]{1,0:T(8,128)(2,1)} custom-call(s32[3]{0:T(128)} %pad_add_fusion.1.order_ref, bf16[384,768]{1,0:T(8,128)(2,1)} %copy-done.8, bf16[384,768]{1,0:T(8,128)(2,1)} %copy-done.22, bf16[1536,768]{1,0:T(8,128)(2,1)} %x_ref.7, f32[384,768]{1,0:T(8,128)} %get-tuple-element.207.d_ref, f32[8,768]{1,0:T(8,128)} %get-tuple-element.70.gains_ref), custom_call_target="tpu_custom_call" | custom-call | flops 5898240 | bytes 3538944 | tf_op jit(solution)/shard_map/input/pallas_call | solution.py:381
  305.2 5.1 %bucket.1.refs_10_ = f32[8,128]{1,0:T(8,128)} custom-call(f32[3,128,1408]{2,1,0:T(8,128)} %get-tuple-element.92.near_ref, f32[3,128,1408]{2,1,0:T(8,128)} %get-tuple-element.93.far_ref), custom_call_target="tpu_custom_call" | custom-call | flops 8388608 | bytes 4194304 | tf_op jit(solution)/shard_map/bucket/pallas_call | solution.py:1847
  310.9 12.3 %norm.1 = (f32[96,832]{1,0:T(8,128)}, f32[96,1536]{1,0:T(8,128)}, f32[8,128]{1,0:T(8,128)}, f32[8,128]{1,0:T(8,128)}, f32[32,128]{1,0:T(8,128)}) custom-call(f32[96,832]{1,0:T(8,128)} %get-tuple-element.195.refs_0_, bf16[96,832]{1,0:T(8,128)(2,1)} %copy-done.30, bf16[96,832]{1,0:T(8,128)(2,1)} %copy-done.33, bf16[96,832]{1,0:T(8,128)(2,1)} %copy-done.32, ...), custom_call_target="tpu_custom_call" | custom-call | flops 1048576 | bytes 4194304 | tf_op jit(solution)/shard_map/norm/pallas_call | solution.py:792
  324.4 4.3 %adam.1 = (f32[3,96,192]{2,1,0:T(8,128)}, f32[192,96]{1,0:T(8,128)}, f32[2,96,512]{2,1,0:T(8,128)}, f32[512,96]{1,0:T(8,128)}, f32[32,12]{1,0:T(8,128)}, /*index...) custom-call(f32[96,832]{1,0:T(8,128)} %get-tuple-element.95.att_ref,, ...), custom_call_target="tpu_custom_call" | custom-call | flops 4194304 | bytes 8388608 | tf_op jit(solution)/shard_map/adam/pallas_call | solution.py:863
  339.8 4.3 %place.2 = bf16[1536,768]{1,0:T(8,128)(2,1)} custom-call(s32[4]{0:T(128)} %pad_add_fusion.offs_ref, bf16[384,768]{1,0:T(8,128)(2,1)} %output.2.refs_0_, bf16[384,768]{1,0:T(8,128)(2,1)} %copy-done.16, bf16[384,768]{1,0:T(8,128)(2,1)} %output.3.refs_2_, bf16[384,768]{1,0:T(8,128)(2,1)} %copy-done.14), custom_call_target="tpu_custom_call" | custom-call | bytes 4718592 | tf_op jit(solution)/shard_map/place/pallas_call | solution.py:890
  344.9 4.3 %place.3 = bf16[1536,768]{1,0:T(8,128)(2,1)} custom-call(s32[4]{0:T(128)} %pad_add_fusion.offs_ref, bf16[384,768]{1,0:T(8,128)(2,1)} %input.2.refs_0_, bf16[384,768]{1,0:T(8,128)(2,1)} %copy-done.15, bf16[384,768]{1,0:T(8,128)(2,1)} %input.3.refs_2_, bf16[384,768]{1,0:T(8,128)(2,1)} %collective-permute-done.9.refs_3_), custom_call_target="tpu_custom_call" | custom-call | bytes 4718592 | tf_op jit(solution)/shard_map/place/pallas_call | solution.py:890
  (160 shorter events, 72.2 us)
Async XLA Ops:
  139.9 88.6 %collective-permute-start.22 = (bf16[96,1536]{1,0:T(8,128)(2,1)}, bf16[96,1536]{1,0:T(8,128)(2,1)}, u32[]{:S(2)}, u32[]{:S(2)}) collective-permute-start(bf16[96,1536]{1,0:T(8,128)(2,1)} %get-tuple-element.217), channel_id=1, source_target_pairs={{0,4},{1,5},{2,6},{3,7},{4,0},{5,1},{6,2},{7,3},{8,12},{9,13},{10,... | collective-permute-start | bytes 884744 | tf_op jit(solution)/shard_map/ppermute | solution.py:1759
  139.9 90.2 %collective-permute-start.20 = (bf16[96,1536]{1,0:T(8,128)(2,1)}, bf16[96,1536]{1,0:T(8,128)(2,1)}, u32[]{:S(2)}, u32[]{:S(2)}) collective-permute-start(bf16[96,1536]{1,0:T(8,128)(2,1)} %get-tuple-element.218), channel_id=1, source_target_pairs={{0,4},{1,5},{2,6},{3,7},{4,0},{5,1},{6,2},{7,3},{8,12},{9,13},{10,... | collective-permute-start | bytes 884744 | tf_op jit(solution)/shard_map/ppermute | solution.py:1759
  167.4 37.8 %collective-permute-start.4 = (bf16[384,768]{1,0:T(8,128)(2,1)}, bf16[384,768]{1,0:T(8,128)(2,1)}, u32[]{:S(2)}, u32[]{:S(2)}) collective-permute-start(bf16[384,768]{1,0:T(8,128)(2,1)} %get-tuple-element.80), channel_id=1, source_target_pairs={{0,1},{1,0},{2,3},{3,2},{4,5},{5,4},{6,7},{7,6},{8,9},{9,8},{10,11... | collective-permute-start | bytes 1769480 | tf_op jit(solution)/shard_map/ppermute | solution.py:1759
  185.3 29.3 %collective-permute-start.7 = (bf16[384,768]{1,0:T(8,128)(2,1)}, bf16[384,768]{1,0:T(8,128)(2,1)}, u32[]{:S(2)}, u32[]{:S(2)}) collective-permute-start(bf16[384,768]{1,0:T(8,128)(2,1)} %get-tuple-element.83), channel_id=1, source_target_pairs={{0,1},{1,0},{2,3},{3,2},{4,5},{5,4},{6,7},{7,6},{8,9},{9,8},{10,11... | collective-permute-start | bytes 1769480 | tf_op jit(solution)/shard_map/ppermute | solution.py:1759
  203.5 7.5 %collective-permute-start.15 = (bf16[96,832]{1,0:T(8,128)(2,1)}, bf16[96,832]{1,0:T(8,128)(2,1)}, u32[]{:S(2)}, u32[]{:S(2)}) collective-permute-start(bf16[96,832]{1,0:T(8,128)(2,1)} %get-tuple-element.196), channel_id=1, source_target_pairs={{0,4},{1,5},{2,6},{3,7},{4,0},{5,1},{6,2},{7,3},{8,12},{9,13},{10,... | collective-permute-start | bytes 479240 | tf_op jit(solution)/shard_map/ppermute | solution.py:1759
  205.2 9.3 %collective-permute-start.13 = (bf16[96,832]{1,0:T(8,128)(2,1)S(1)}, bf16[96,832]{1,0:T(8,128)(2,1)S(1)}, u32[]{:S(2)}, u32[]{:S(2)}) collective-permute-start(bf16[96,832]{1,0:T(8,128)(2,1)S(1)} %copy-done.29), channel_id=1, source_target_pairs={{0,4},{1,5},{2,6},{3,7},{4,0},{5,1},{6,2},{7,3},{8,12},{9,13},{10,... | collective-permute-start | bytes 479240 | tf_op jit(solution)/shard_map/ppermute | solution.py:1759
  211.0 21.4 %collective-permute-start.18 = (bf16[96,1536]{1,0:T(8,128)(2,1)S(1)}, bf16[96,1536]{1,0:T(8,128)(2,1)S(1)}, u32[]{:S(2)}, u32[]{:S(2)}) collective-permute-start(bf16[96,1536]{1,0:T(8,128)(2,1)S(1)} %copy-done.24), channel_id=1, source_target_pairs={{0,4},{1,5},{2,6},{3,7},{4,0},{5,1},{6,2},{7,3},{8,12},{9,13},{10,... | collective-permute-start | bytes 884744 | tf_op jit(solution)/shard_map/ppermute | solution.py:1759
  214.6 10.0 %collective-permute-start.11 = (bf16[96,832]{1,0:T(8,128)(2,1)S(1)}, bf16[96,832]{1,0:T(8,128)(2,1)S(1)}, u32[]{:S(2)}, u32[]{:S(2)}) collective-permute-start(bf16[96,832]{1,0:T(8,128)(2,1)S(1)} %copy-done.28), channel_id=1, source_target_pairs={{0,4},{1,5},{2,6},{3,7},{4,0},{5,1},{6,2},{7,3},{8,12},{9,13},{10,... | collective-permute-start | bytes 479240 | tf_op jit(solution)/shard_map/ppermute | solution.py:1759
  214.6 12.8 %collective-permute-start.10 = (bf16[96,832]{1,0:T(8,128)(2,1)S(1)}, bf16[96,832]{1,0:T(8,128)(2,1)S(1)}, u32[]{:S(2)}, u32[]{:S(2)}) collective-permute-start(bf16[96,832]{1,0:T(8,128)(2,1)S(1)} %copy-done.27), channel_id=1, source_target_pairs={{0,4},{1,5},{2,6},{3,7},{4,0},{5,1},{6,2},{7,3},{8,12},{9,13},{10,... | collective-permute-start | bytes 479240 | tf_op jit(solution)/shard_map/ppermute | solution.py:1759
  224.6 16.8 %collective-permute-start.2 = (bf16[384,768]{1,0:T(8,128)(2,1)S(1)}, bf16[384,768]{1,0:T(8,128)(2,1)S(1)}, u32[]{:S(2)}, u32[]{:S(2)}) collective-permute-start(bf16[384,768]{1,0:T(8,128)(2,1)S(1)} %get-tuple-element.221.near), channel_id=1, source_target_pairs={{0,2},{1,3},{2,0},{3,1},{4,6},{5,7},{6,4},{7,5},{8,10},{9,11},{10,... | collective-permute-start | bytes 1769480 | tf_op jit(solution)/shard_map/ppermute | solution.py:1759
  228.1 25.4 %collective-permute-start = (bf16[384,768]{1,0:T(8,128)(2,1)S(1)}, bf16[384,768]{1,0:T(8,128)(2,1)S(1)}, u32[]{:S(2)}, u32[]{:S(2)}) collective-permute-start(bf16[384,768]{1,0:T(8,128)(2,1)S(1)} %get-tuple-element.222.near), channel_id=1, source_target_pairs={{0,2},{1,3},{2,0},{3,1},{4,6},{5,7},{6,4},{7,5},{8,10},{9,11},{10,... | collective-permute-start | bytes 1769480 | tf_op jit(solution)/shard_map/ppermute | solution.py:1759
  228.5 37.6 %collective-permute-start.5 = (bf16[384,768]{1,0:T(8,128)(2,1)S(1)}, bf16[384,768]{1,0:T(8,128)(2,1)S(1)}, u32[]{:S(2)}, u32[]{:S(2)}) collective-permute-start(bf16[384,768]{1,0:T(8,128)(2,1)S(1)} %add_convert_fusion.1.near), channel_id=1, source_target_pairs={{0,2},{1,3},{2,0},{3,1},{4,6},{5,7},{6,4},{7,5},{8,10},{9,11},{10,... | collective-permute-start | bytes 1769480 | tf_op jit(solution)/shard_map/ppermute | solution.py:1759
  230.2 46.1 %collective-permute-start.8 = (bf16[384,768]{1,0:T(8,128)(2,1)S(1)}, bf16[384,768]{1,0:T(8,128)(2,1)S(1)}, u32[]{:S(2)}, u32[]{:S(2)}) collective-permute-start(bf16[384,768]{1,0:T(8,128)(2,1)S(1)} %add_convert_fusion.near), channel_id=1, source_target_pairs={{0,2},{1,3},{2,0},{3,1},{4,6},{5,7},{6,4},{7,5},{8,10},{9,11},{10,... | collective-permute-start | bytes 1769480 | tf_op jit(solution)/shard_map/ppermute | solution.py:1759
  232.4 7.4 %collective-permute-start.17 = (bf16[96,1536]{1,0:T(8,128)(2,1)S(1)}, bf16[96,1536]{1,0:T(8,128)(2,1)S(1)}, u32[]{:S(2)}, u32[]{:S(2)}) collective-permute-start(bf16[96,1536]{1,0:T(8,128)(2,1)S(1)} %copy-done.23), channel_id=1, source_target_pairs={{0,4},{1,5},{2,6},{3,7},{4,0},{5,1},{6,2},{7,3},{8,12},{9,13},{10,... | collective-permute-start | bytes 884744 | tf_op jit(solution)/shard_map/ppermute | solution.py:1759
  239.8 55.6 %collective-permute-start.16 = (bf16[96,832]{1,0:T(8,128)(2,1)S(1)}, bf16[96,832]{1,0:T(8,128)(2,1)S(1)}, u32[]{:S(2)}, u32[]{:S(2)}) collective-permute-start(bf16[96,832]{1,0:T(8,128)(2,1)S(1)} %get-tuple-element.192), channel_id=1, source_target_pairs={{0,24},{1,25},{2,26},{3,27},{4,28},{5,29},{6,30},{7,31},{8,0},{9,1... | collective-permute-start | bytes 479240 | tf_op jit(solution)/shard_map/ppermute | solution.py:1759
  241.4 54.7 %collective-permute-start.14 = (bf16[96,832]{1,0:T(8,128)(2,1)S(1)}, bf16[96,832]{1,0:T(8,128)(2,1)S(1)}, u32[]{:S(2)}, u32[]{:S(2)}) collective-permute-start(bf16[96,832]{1,0:T(8,128)(2,1)S(1)} %get-tuple-element.193), channel_id=1, source_target_pairs={{0,16},{1,17},{2,18},{3,19},{4,20},{5,21},{6,22},{7,23},{8,24},{9,... | collective-permute-start | bytes 479240 | tf_op jit(solution)/shard_map/ppermute | solution.py:1759
  253.5 42.7 %collective-permute-start.12 = (bf16[96,832]{1,0:T(8,128)(2,1)S(1)}, bf16[96,832]{1,0:T(8,128)(2,1)S(1)}, u32[]{:S(2)}, u32[]{:S(2)}) collective-permute-start(bf16[96,832]{1,0:T(8,128)(2,1)S(1)} %get-tuple-element.194), channel_id=1, source_target_pairs={{0,8},{1,9},{2,10},{3,11},{4,12},{5,13},{6,14},{7,15},{8,16},{9,17... | collective-permute-start | bytes 479240 | tf_op jit(solution)/shard_map/ppermute | solution.py:1759
  266.1 30.7 %collective-permute-start.23 = (bf16[96,1536]{1,0:T(8,128)(2,1)}, bf16[96,1536]{1,0:T(8,128)(2,1)S(1)}, u32[]{:S(2)}, u32[]{:S(2)}) collective-permute-start(bf16[96,1536]{1,0:T(8,128)(2,1)} %get-tuple-element.200), channel_id=1, source_target_pairs={{0,24},{1,25},{2,26},{3,27},{4,28},{5,29},{6,30},{7,31},{8,0},{9,1... | collective-permute-start | bytes 884744 | tf_op jit(solution)/shard_map/ppermute | solution.py:1759
  276.2 21.4 %collective-permute-start.21 = (bf16[96,1536]{1,0:T(8,128)(2,1)}, bf16[96,1536]{1,0:T(8,128)(2,1)}, u32[]{:S(2)}, u32[]{:S(2)}) collective-permute-start(bf16[96,1536]{1,0:T(8,128)(2,1)} %get-tuple-element.201), channel_id=1, source_target_pairs={{0,16},{1,17},{2,18},{3,19},{4,20},{5,21},{6,22},{7,23},{8,24},{9,... | collective-permute-start | bytes 884744 | tf_op jit(solution)/shard_map/ppermute | solution.py:1759
  295.4 15.5 %collective-permute-start.19 = (bf16[96,1536]{1,0:T(8,128)(2,1)}, bf16[96,1536]{1,0:T(8,128)(2,1)}, u32[]{:S(2)}, u32[]{:S(2)}) collective-permute-start(bf16[96,1536]{1,0:T(8,128)(2,1)} %get-tuple-element.202), channel_id=1, source_target_pairs={{0,8},{1,9},{2,10},{3,11},{4,12},{5,13},{6,14},{7,15},{8,16},{9,17... | collective-permute-start | bytes 884744 | tf_op jit(solution)/shard_map/ppermute | solution.py:1759
  296.1 42.1 %collective-permute-start.3 = (bf16[384,768]{1,0:T(8,128)(2,1)S(1)}, bf16[384,768]{1,0:T(8,128)(2,1)S(1)}, u32[]{:S(2)}, u32[]{:S(2)}) collective-permute-start(bf16[384,768]{1,0:T(8,128)(2,1)S(1)} %copy-done.3), channel_id=1, source_target_pairs={{0,1},{1,0},{2,3},{3,2},{4,5},{5,4},{6,7},{7,6},{8,9},{9,8},{10,11... | collective-permute-start | bytes 1769480 | tf_op jit(solution)/shard_map/ppermute | solution.py:1759
  296.2 42.0 %collective-permute-start.1 = (bf16[384,768]{1,0:T(8,128)(2,1)S(1)}, bf16[384,768]{1,0:T(8,128)(2,1)S(1)}, u32[]{:S(2)}, u32[]{:S(2)}) collective-permute-start(bf16[384,768]{1,0:T(8,128)(2,1)S(1)} %copy-done.2), channel_id=1, source_target_pairs={{0,1},{1,0},{2,3},{3,2},{4,5},{5,4},{6,7},{7,6},{8,9},{9,8},{10,11... | collective-permute-start | bytes 1769480 | tf_op jit(solution)/shard_map/ppermute | solution.py:1759
  296.9 47.2 %collective-permute-start.6 = (bf16[384,768]{1,0:T(8,128)(2,1)S(1)}, bf16[384,768]{1,0:T(8,128)(2,1)S(1)}, u32[]{:S(2)}, u32[]{:S(2)}) collective-permute-start(bf16[384,768]{1,0:T(8,128)(2,1)S(1)} %copy-done.1), channel_id=1, source_target_pairs={{0,1},{1,0},{2,3},{3,2},{4,5},{5,4},{6,7},{7,6},{8,9},{9,8},{10,11... | collective-permute-start | bytes 1769480 | tf_op jit(solution)/shard_map/ppermute | solution.py:1759
  297.6 46.5 %collective-permute-start.9 = (bf16[384,768]{1,0:T(8,128)(2,1)}, bf16[384,768]{1,0:T(8,128)(2,1)}, u32[]{:S(2)}, u32[]{:S(2)}) collective-permute-start(bf16[384,768]{1,0:T(8,128)(2,1)} %input.3.refs_2_), channel_id=1, source_target_pairs={{0,1},{1,0},{2,3},{3,2},{4,5},{5,4},{6,7},{7,6},{8,9},{9,8},{10,11... | collective-permute-start | bytes 1769480 | tf_op jit(solution)/shard_map/ppermute | solution.py:1759
  (39 other events, 421.8 us)

commit v3 on v2

--- a/solution.py
+++ b/solution.py
@@ -1722,6 +1722,392 @@
     )(x, cot, att, gains, obuf, fbuf)
 
 
+class Reduce:
+    def __init__(self, spot, even, odd, flipped, mixed, landed, sems_s, sems_r):
+        self.spot, self.even, self.odd = spot, even, odd
+        self.flipped, self.mixed, self.landed = flipped, mixed, landed
+        self.sems_s, self.sems_r = sems_s, sems_r
+
+    def over(self, m):
+        return remote(
+            self.odd.at[m], self.flipped.at[m], self.sems_s.at[m], self.sems_r.at[m], self.spot.flip
+        )
+
+    def along(self, m):
+        return remote(
+            self.mixed.at[m - 1],
+            self.landed.at[m - 1],
+            self.sems_s.at[3 + m],
+            self.sems_r.at[3 + m],
+            self.spot.along(m),
+        )
+
+    def begin(self):
+        for m in (2, 1, 3, 0):
+            self.over(m).start()
+
+    def relay(self, m):
+        self.over(m).wait_recv()
+        self.mixed[m - 1] = (self.even(m) + self.flipped[m].astype(F32)).astype(BF16)
+        self.along(m).start()
+
+    def result(self):
+        self.over(0).wait_recv()
+        value = self.even(0) + self.flipped[0].astype(F32)
+        for m in (1, 2, 3):
+            self.along(m).wait_recv()
+            value = value + self.landed[m - 1].astype(F32)
+        return value
+
+    def drain(self):
+        for m in range(4):
+            self.over(m).wait_send()
+        for m in (1, 2, 3):
+            self.along(m).wait_send()
+
+
+def back_all_kernel(
+    buffers,
+    slots,
+    heads,
+    ends_ref,
+    x_ref,
+    strip_ref,
+    qkv_ref,
+    log_ref,
+    low_ref,
+    att_ref,
+    normed_ref,
+    gains_ref,
+    pbuf,
+    obuf,
+    ff_sum,
+    middle_ref,
+    d_ref,
+    gain_two_ref,
+    feed_even,
+    feed_odd,
+    out_ref,
+    in_ref,
+    att_grad,
+    feed_grad,
+    bucket_ref,
+    qs,
+    kt,
+    ks,
+    vt,
+    gs,
+    qt,
+    gt,
+    dkt,
+    dvt,
+    dq,
+    dqkv,
+    dstrip,
+    total,
+    att_odd,
+    att_flip,
+    att_mix,
+    att_land,
+    feed_flip,
+    feed_mix,
+    feed_land,
+    ff_far,
+    dn_out,
+    dn_in,
+    dn_sum,
+    dn_far,
+    sends,
+    recvs,
+    red_s,
+    red_r,
+):
+    spot = Place()
+    spot.meet()
+    tokens, width = x_ref.shape
+    length = tokens // buffers
+    half = length // 2
+    head_cols = heads * DH
+    qkv_cols = 3 * head_cols
+    core = spot.core
+    rows_of = feed_even.shape[1]
+    gain_one = gains_ref[0:1]
+
+    def half_rows(b, which):
+        return pl.ds(pl.multiple_of(b * length + which * half, LANES), half)
+
+    def ff_across(b):
+        return remote(ff_sum.at[b], ff_far.at[b], sends.at[b], recvs.at[b], spot.across)
+
+    def dn_core(b):
+        return remote(dn_out.at[b], dn_in.at[b], sends.at[2 + b], recvs.at[2 + b], spot.beside)
+
+    def dn_across(b):
+        return remote(dn_sum.at[b], dn_far.at[b], sends.at[4 + b], recvs.at[4 + b], spot.across)
+
+    def out_core(b, which):
+        view = out_ref.at[half_rows(b, which)]
+        return remote(view, view, sends.at[6 + b], recvs.at[6 + b], spot.beside)
+
+    def in_core(b, which):
+        view = in_ref.at[half_rows(b, which)]
+        return remote(view, view, sends.at[8 + b], recvs.at[8 + b], spot.beside)
+
+    feed = Reduce(
+        spot,
+        lambda m: feed_even[m],
+        feed_odd,
+        feed_flip,
+        feed_mix,
+        feed_land,
+        red_s.at[0],
+        red_r.at[0],
+    )
+
+    def att_even(m):
+        owner = ((spot.z + m) % 4) * 2 + spot.x
+        return total[pl.ds(pl.multiple_of(owner * rows_of, 8), rows_of)]
+
+    att = Reduce(
+        spot, att_even, att_odd, att_flip, att_mix, att_land, red_s.at[1], red_r.at[1]
+    )
+    feed.begin()
+    for b in range(buffers):
+        ff_across(b).start()
+    dstrip[...] = jnp.zeros_like(dstrip)
+    blocks = length // LANES
+    gain_sums = jnp.zeros((8, width), F32)
+
+    for b in range(buffers):
+        base = b * length
+        rows = slice(base, base + length)
+        grads = mm(low_ref[rows], obuf[spot.n]).astype(BF16)
+        for h in range(heads):
+            qs[h] = qkv_ref[rows, h * DH : (h + 1) * DH]
+            ks[h] = qkv_ref[rows, head_cols + h * DH : head_cols + (h + 1) * DH]
+            values = qkv_ref[rows, 2 * head_cols + h * DH : 2 * head_cols + (h + 1) * DH]
+            qt[h] = qs[h].T
+            kt[h] = ks[h].T
+            vt[h] = values.T
+            gs[h] = grads[:, h * DH : (h + 1) * DH]
+            gt[h] = gs[h].T
+        dkt[...] = jnp.zeros_like(dkt)
+        dvt[...] = jnp.zeros_like(dvt)
+        seg_keys = segments(
+            lax.broadcasted_iota(jnp.int32, (1, length), 1), ends_ref, b, slots
+        )
+        events = {1: lambda: feed.relay(2), 2: lambda: feed.relay(1), 3: lambda: feed.relay(3)}
+
+        @pl.loop(0, blocks)
+        def _(block, b=b, base=base, seg_keys=seg_keys):
+            if b == 0:
+                for when, what in events.items():
+                    pl.when(block == when)(what)
+            begin = pl.multiple_of(block * LANES, LANES)
+            here = pl.ds(begin, LANES)
+            window = pl.ds(pl.multiple_of((blocks - 1 - block) * LANES, LANES), length)
+            seg_rows = segments(
+                lax.broadcasted_iota(jnp.int32, (LANES, 1), 0) + begin, ends_ref, b, slots
+            )
+            same = seg_rows == seg_keys
+            logs = log_ref[pl.ds(pl.multiple_of(base + begin, LANES), LANES)]
+            for h in range(heads):
+                scores = mm(qs[h, here], kt[h]) + strip_ref[h, :, window]
+                scores = jnp.where(same, scores, masked_score)
+                probs = jnp.exp(scores - logs[:, h : h + 1])
+                d_probs = mm(gs[h, here], vt[h])
+                inner = jnp.sum(probs * d_probs, axis=1, keepdims=True)
+                d_scores = (probs * (d_probs - inner)).astype(BF16)
+                dstrip[h, :, window] = dstrip[h, :, window] + d_scores.astype(F32)
+                dq[h, here] = mm(d_scores, ks[h]).astype(BF16)
+                dkt[h] = dkt[h] + mm(qt[h, :, here], d_scores)
+                dvt[h] = dvt[h] + mm(gt[h, :, here], probs.astype(BF16))
+
+        outs = [dq[h] for h in range(heads)]
+        outs += [dkt[h].T.astype(BF16) for h in range(heads)]
+        outs += [dvt[h].T.astype(BF16) for h in range(heads)]
+        dqkv[rows] = jnp.concatenate(outs, axis=1)
+        for keep in range(2):
+            which = core if keep else 1 - core
+            here = half_rows(b, which)
+            dn = mm(dqkv[here], pbuf[:, :qkv_cols], NT)
+            values = x_ref[here].astype(F32)
+            gain_sums = gain_sums + fold_rows(dn * values * rms_scale(values))
+            dn = dn.astype(BF16)
+            if keep:
+                dn_core(b).wait_recv()
+                dn_sum[b] = (dn.astype(F32) + dn_in[b].astype(F32)).astype(BF16)
+                dn_across(b).start()
+            else:
+                dn_out[b] = dn
+                dn_core(b).start()
+
+    def finish_out(b):
+        ff_across(b).wait_recv()
+
+        @pl.loop(0, 3)
+        def _(i):
+            span = pl.ds(pl.multiple_of(i * LANES, LANES), LANES)
+            here = pl.ds(pl.multiple_of(b * length + core * half + i * LANES, LANES), LANES)
+            joined = (ff_sum[b, span].astype(F32) + ff_far[b, span].astype(F32)).astype(BF16)
+            out_ref[here] = (middle_ref[b, span] + joined.astype(F32)).astype(BF16)
+
+        out_core(b, core).start()
+
+    def finish_in(b):
+        dn_across(b).wait_recv()
+
+        @pl.loop(0, 3)
+        def _(i):
+            span = pl.ds(pl.multiple_of(i * LANES, LANES), LANES)
+            here = pl.ds(pl.multiple_of(b * length + core * half + i * LANES, LANES), LANES)
+            upstream = dn_sum[b, span].astype(F32) + dn_far[b, span].astype(F32)
+            values = x_ref[here].astype(F32)
+            in_ref[here] = (
+                d_ref[b, span] + norm_back(values, rms_scale(values), gain_one, upstream)
+            ).astype(BF16)
+
+        in_core(b, core).start()
+
+    row = lax.broadcasted_iota(jnp.int32, (LANES, width), 0)
+    gain_rows = jnp.where(
+        row == DH,
+        jnp.sum(gain_sums, axis=0, keepdims=True),
+        jnp.where(row == DH + 1, jnp.sum(gain_two_ref[...], axis=0, keepdims=True), 0.0),
+    )
+    gain_cols = gain_rows.T
+    step = 256
+    for begin in range(0, width, step):
+        cols = slice(begin, begin + step)
+        total[cols, :qkv_cols] = mm(normed_ref[:, cols], dqkv[...], TN)
+        total[cols, qkv_cols : qkv_cols + DH] = gain_cols[cols, DH:]
+        total[cols, qkv_cols + DH :] = mm(low_ref[:, cols], att_ref[spot.n], TN)
+    for m in range(4):
+        owner = ((spot.z + m) % 4) * 2 + 1 - spot.x
+        att_odd[m] = total[pl.ds(pl.multiple_of(owner * rows_of, 8), rows_of)].astype(BF16)
+    att.begin()
+    feed_grad[...] = feed.result()
+    finish_out(0)
+    att.relay(2)
+    att.relay(1)
+    att.relay(3)
+    finish_out(1)
+    finish_in(0)
+
+    near_at = (blocks - 2) * LANES
+    near_row = lax.broadcasted_iota(jnp.int32, (LANES, 4 * LANES), 0)
+    diag = lax.broadcasted_iota(jnp.int32, (LANES, 4 * LANES), 1)[0:1]
+    offset = jnp.where(diag < 3 * LANES, diag - LANES, diag - 5 * LANES)
+    ids = bucket_of(offset)
+    lane = lax.broadcasted_iota(jnp.int32, (1, LANES), 1)
+    pick = lax.broadcasted_iota(jnp.int32, (LANES, 4 * LANES), 0)
+    onehot = jnp.where(pick == ids, 1.0, 0.0)
+    out = jnp.zeros((1, LANES), F32)
+    for h in range(heads):
+        left = jnp.sum(jnp.sum(dstrip[h, :, :near_at], axis=0, keepdims=True), axis=1, keepdims=True)
+        right = jnp.sum(
+            jnp.sum(dstrip[h, :, near_at + 3 * LANES :], axis=0, keepdims=True), axis=1, keepdims=True
+        )
+        near = jnp.concatenate(
+            [dstrip[h, :, near_at : near_at + 3 * LANES], jnp.zeros((LANES, LANES), F32)], axis=1
+        )
+        for k in range(7):
+            near = jnp.where(
+                (near_row // (1 << k)) % 2 == 1, pltpu.roll(near, 4 * LANES - (1 << k), 1), near
+            )
+        sums = jnp.sum(near, axis=0, keepdims=True)
+        binned = lax.dot_general(
+            jnp.broadcast_to(sums, (8, 4 * LANES)),
+            onehot,
+            NT,
+            precision=lax.Precision.HIGHEST,
+            preferred_element_type=F32,
+        )[0:1]
+        binned = binned + jnp.where(lane == 15, left, 0.0) + jnp.where(lane == 31, right, 0.0)
+        binned = jnp.where(lane < 32, binned, 0.0)
+        out = out + (pltpu.roll(binned, 32 * h, 1) if h else binned)
+    bucket_ref[...] = jnp.broadcast_to(out, (8, LANES))
+
+    att_grad[...] = att.result()
+    finish_in(1)
+    for b in range(buffers):
+        out_core(b, 1 - core).wait_recv()
+        in_core(b, 1 - core).wait_recv()
+        ff_across(b).wait_send()
+        dn_core(b).wait_send()
+        dn_across(b).wait_send()
+        out_core(b, core).wait_send()
+        in_core(b, core).wait_send()
+    feed.drain()
+    att.drain()
+
+
+def back_all(
+    ends, x, strip, qkv, logs, low, att, normed, gains, pbuf, obuf, ff_sum, middle, d_middle,
+    gain_two, feed_even, feed_odd, length
+):
+    tokens, width = x.shape
+    buffers = tokens // length
+    half = length // 2
+    heads = strip.shape[0]
+    rows, feed_cols = feed_even.shape[1:]
+    head_cols = heads * DH
+    att_cols = 4 * head_cols + DH
+    vmem = pl.BlockSpec(memory_space=pltpu.VMEM)
+    operands = [
+        x, strip, qkv, logs, low, att, normed, gains, pbuf, obuf, ff_sum, middle, d_middle,
+        gain_two, feed_even, feed_odd
+    ]
+    wide_heads = pltpu.VMEM((heads, length, DH), BF16)
+    tall_heads = pltpu.VMEM((heads, DH, length), BF16)
+    return pl.pallas_call(
+        functools.partial(back_all_kernel, buffers, ends.shape[1], heads),
+        in_specs=[pl.BlockSpec(memory_space=pltpu.SMEM)] + [vmem] * len(operands),
+        out_specs=[vmem] * 5,
+        out_shape=[
+            jax.ShapeDtypeStruct((tokens, width), BF16),
+            jax.ShapeDtypeStruct((tokens, width), BF16),
+            jax.ShapeDtypeStruct((rows, att_cols), F32),
+            jax.ShapeDtypeStruct((rows, feed_cols), F32),
+            jax.ShapeDtypeStruct((8, LANES), F32),
+        ],
+        scratch_shapes=[
+            wide_heads,
+            tall_heads,
+            wide_heads,
+            tall_heads,
+            wide_heads,
+            tall_heads,
+            tall_heads,
+            pltpu.VMEM((heads, DH, length), F32),
+            pltpu.VMEM((heads, DH, length), F32),
+            wide_heads,
+            pltpu.VMEM((tokens, 3 * head_cols), BF16),
+            pltpu.VMEM(strip.shape, F32),
+            pltpu.VMEM((width, att_cols), F32),
+            pltpu.VMEM((4, rows, att_cols), BF16),
+            pltpu.VMEM((4, rows, att_cols), BF16),
+            pltpu.VMEM((3, rows, att_cols), BF16),
+            pltpu.VMEM((3, rows, att_cols), BF16),
+            pltpu.VMEM((4, rows, feed_cols), BF16),
+            pltpu.VMEM((3, rows, feed_cols), BF16),
+            pltpu.VMEM((3, rows, feed_cols), BF16),
+        ]
+        + [pltpu.VMEM((buffers, half, width), BF16)] * 5
+        + [
+            pltpu.SemaphoreType.DMA((10,)),
+            pltpu.SemaphoreType.DMA((10,)),
+            pltpu.SemaphoreType.DMA((2, 7)),
+            pltpu.SemaphoreType.DMA((2, 7)),
+        ],
+        compiler_params=params(collective_id=3, has_side_effects=True),
+        cost_estimate=pl.CostEstimate(
+            flops=20 << 30, bytes_accessed=32 << 20, transcendentals=4 << 20
+        ),
+        name="back_all",
+    )(ends, *operands)
+
+
 def direct_body(wide, narrow, *arguments):
     (
         block_input,
@@ -1743,30 +2129,9 @@
     head_cols = project_weight.shape[2]
     heads = head_cols // DH
     hidden_cols = expand_weight.shape[2]
-    w = lax.axis_index("wide")
     n = lax.axis_index("narrow")
-    core = n % 2
-
-    def move(value, wide_step=0, flip=0, narrow_mask=0):
-        def target(a):
-            return ((a // 2 + wide_step) % 4) * 2 + (a % 2 ^ flip)
-
-        pairs = [
-            (a * narrow + b, target(a) * narrow + (b ^ narrow_mask))
-            for a in range(wide)
-            for b in range(narrow)
-        ]
-        return lax.ppermute(value, ("wide", "narrow"), pairs)
-
-    def reduce_wide(evens, odds):
-        kept = [evens[0], move(odds[0], flip=1)]
-        for m in (1, 2, 3):
-            mixed = (evens[m] + move(odds[m], flip=1).astype(F32)).astype(BF16)
-            kept.append(move(mixed, wide_step=m))
-        return kept
 
     ends = jnp.cumsum(lengths, axis=1)
-    order = jnp.stack([1 - core, core, n // 2])
     strip = bias_strip(bucket_bias, n, heads, length)
     normed_one, qkv, att, logs, gains, pbuf, obuf, fbuf = gather_attend(
         ends,
@@ -1782,109 +2147,29 @@
     low, d_middle, middle, ff_sum, gain_two, feed_even, feed_odd = feed_forward(
         block_input, cotangent, att, gains, obuf, fbuf, length, rows
     )
-    feed_group = reduce_wide(feed_even, feed_odd)
-
-    def core_sum(kept, sent):
-        return (kept.astype(F32) + move(sent, narrow_mask=1).astype(F32)).astype(BF16)
-
-    offs = jnp.zeros((1,), jnp.int32)
-    own = lax.dynamic_index_in_dim(obuf, n, 0, keepdims=False)
-    att_own = lax.dynamic_index_in_dim(att, n, 0, keepdims=False)
-    dqkv, dn_one, sums_one, strips = [], [], [], []
-    half = length // 2
-    for b in range(buffers):
-        part = lambda which: lax.dynamic_slice_in_dim(low, b * length + which * half, half, 0)
-        span = slice(b * length, (b + 1) * length)
-        _, grads, dn_send, dn_keep, sums, dstrip = back(
-            b,
-            ends,
-            offs,
-            order,
-            part(core),
-            part(1 - core),
-            qkv[span],
-            logs[span],
-            strip,
-            block_input,
-            [own],
-            [pbuf],
-            heads,
-        )
-        dqkv.append(grads)
-        sums_one.append(sums)
-        strips.append(dstrip)
-        dn_one.append(core_sum(dn_keep, dn_send))
-
+    block_output, input_gradient, att_grad, feed_grad, bucket = back_all(
+        ends,
+        block_input,
+        strip,
+        qkv,
+        logs,
+        low,
+        att,
+        normed_one,
+        gains,
+        pbuf,
+        obuf,
+        ff_sum,
+        middle,
+        d_middle,
+        gain_two,
+        feed_even,
+        feed_odd,
+        length,
+    )
     gain_at = 3 * head_cols
-    halves = lambda value: [value[b * length : (b + 1) * length] for b in range(buffers)]
-    (att_total,) = grad_call(
-        functools.partial(attend_grad_kernel, 1, heads),
-        "attend_grad",
-        offs,
-        [
-            *halves(normed_one),
-            *dqkv,
-            *halves(low),
-            *halves(att_own),
-            jnp.stack(sums_one + [gain_two, jnp.zeros_like(gain_two)]),
-        ],
-        width,
-        gain_at + DH + head_cols,
-        1,
-        rows,
-        2 * tokens * width * 4 * head_cols,
-    )
-    near = [
-        lax.dynamic_slice_in_dim(att_total, ((w // 2 + m) % 4 * 2 + w % 2) * rows, rows, 0)
-        for m in range(4)
-    ]
-    far = [
-        lax.dynamic_slice_in_dim(att_total, ((w // 2 + m) % 4 * 2 + 1 - w % 2) * rows, rows, 0)
-        for m in range(4)
-    ]
-    att_group = reduce_wide(near, [value.astype(BF16) for value in far])
-    vmem = pl.BlockSpec(memory_space=pltpu.VMEM)
-    bucket = pl.pallas_call(
-        functools.partial(bucket_kernel, heads),
-        in_specs=[vmem, vmem],
-        out_specs=vmem,
-        out_shape=jax.ShapeDtypeStruct((8, LANES), F32),
-        compiler_params=params(),
-        cost_estimate=pl.CostEstimate(flops=8 << 20, bytes_accessed=4 << 20, transcendentals=0),
-        name="bucket",
-    )(*strips)
-
-    half_offs = jnp.stack(
-        [b * length + which * half for b in range(buffers) for which in (core, 1 - core)]
-    )
-    out_halves, in_halves = [], []
-    for b in range(buffers):
-        (out_half,) = half_call(
-            output_kernel,
-            "output",
-            b,
-            order,
-            [ff_sum[b], move(ff_sum[b], narrow_mask=2), middle[b]],
-            (),
-            (BF16,),
-        )
-        out_halves += [out_half, move(out_half, narrow_mask=1)]
-        (in_half,) = half_call(
-            input_kernel,
-            "input",
-            b,
-            order,
-            [dn_one[b], move(dn_one[b], narrow_mask=2), block_input, d_middle[b]],
-            (2,),
-            (BF16,),
-            gains,
-        )
-        in_halves += [in_half, move(in_half, narrow_mask=1)]
-    block_output = place(out_halves, half_offs, tokens)
-    input_gradient = place(in_halves, half_offs, tokens)
-
     att_grad, feed_grad, stat, gain, table_sum = norm_call(
-        wide, narrow, [att_group, feed_group], bucket, gain_at
+        wide, narrow, [[att_grad], [feed_grad]], bucket, gain_at
     )
     results = adam_call(
         att_grad,

time: 355 us -> 250 us (0.70); the launches traced: 349 us -> 250 us
  waiting for transfers between devices: 52.5 us -> 0 us
  local copies, waits for them, and re-layouts: 47 us -> 21 us
  starting transfers between devices: 16.8 us -> 0 us
  other arithmetic: 14.7 us -> 5.55 us
  Pallas kernels: 217 us -> 223 us
    ppermute x24 -> x0, waiting for transfers between devices: 52.5 us -> none  [move(): return lax.ppermute(value, ('wide', 'narrow'), pairs)]
    ppermute x24 -> x0, starting transfers between devices: 16.8 us -> none  [move(): return lax.ppermute(value, ('wide', 'narrow'), pairs)]
    slice x5 -> x0, local copies, waits for them, and re-layouts: 10.9 us -> none  [the longest x3 6.87 us: direct_body(): value[b * length:(b + 1) * length]]
    squeeze x6 -> x0, local copies, waits for them, and re-layouts: 8.15 us -> none  [the longest x1 2.35 us: reduce_wide(): mixed = (evens[m] + move(odds[m], flip=1).astype(F32)).astype(BF16)]
    pallas_call x10 -> x1, Pallas kernels: 73.6 us -> 80.8 us  [back_all(): pl.pallas_call(functools.partial(back_all_kernel, buffers, ends.shape[1],...]
    convert_element_type x4 -> x0, other arithmetic: 6.41 us -> none  [the longest x2 3.83 us: reduce_wide(): mixed = (evens[m] + move(odds[m], flip=1).astype(F32)).astype(BF16)]
    unnamed x90 -> x32, local copies, waits for them, and re-layouts: 21.1 us -> 18 us
  transfers between devices with their start and end apart: 24 -> 0, of which waited for: 8 -> 0; matrix products, arithmetic and copies ran while one was open for 13% -> 0% of each run, Pallas kernels for 25% -> 0%
where the time goes in v3:
time: 250 us
  Pallas kernels  223 us (89%)
  local copies, waits for them, and re-layouts  21 us (8%)
  other arithmetic  5.55 us (2%)
    pallas_call x1, Pallas kernels, back_all(): pl.pallas_call(functools.partial(back_all_kernel, buffers, ends.shape[1],...  80.8 us
    pallas_call x1, Pallas kernels, gather_attend(): pl.pallas_call(functools.partial(gather_attend_kernel, buffers, ends.shap...  71.7 us
    pallas_call x1, Pallas kernels, feed_forward(): pl.pallas_call(functools.partial(feed_forward_kernel, buffers, hidden_col...  55.3 us
    unnamed x32, local copies, waits for them, and re-layouts  18 us
    pallas_call x1, Pallas kernels, norm_call(): pl.pallas_call(functools.partial(norm_kernel, wide, narrow, lists, gain_a...  10.4 us

profile of v3, /device:TPU:0, one launch (start us, length us, event | category | flops | bytes accessed | tf_op | source)
XLA Modules:
  0.0 249.9 jit_solution(12689016622904294967)
XLA Ops:
  0.7 1.4 broadcast_compare_fusion.27
  2.1 0.7 dynamic-slice_bitcast_fusion
  3.6 1.9 select_add_fusion
  5.9 1.5 pad_maximum_fusion.strip_ref
  7.4 0.8 copy.55.sw_ref.refs_3_
  8.2 0.7 reduce_window_sum.11.ends_ref
  9.0 71.7 %gather_attend.1 = (bf16[1536,768]{1,0:T(8,128)(2,1)}, bf16[1536,576]{1,0:T(8,128)(2,1)}, bf16[4,1536,192]{2,1,0:T(8,128)(2,1)}, f32[1536,128]{1,0:T(8,128)}, f3...) custom-call(s32[2,12]{1,0:T(2,128)} %reduce_window_sum.11.ends_ref, ...), custom_call_target="tpu_custom_call" | custom-call | flops 17179869184 | bytes 25165824 | tf_op jit(solution)/shard_map/gather_attend/pallas_call | solution.py:1488
  80.6 55.3 %feed_forward.1 = (bf16[1536,768]{1,0:T(8,128)(2,1)}, f32[2,384,768]{2,1,0:T(8,128)}, f32[2,384,768]{2,1,0:T(8,128)}, bf16[2,384,768]{2,1,0:T(8,128)(2,1)}, f32[...) custom-call(bf16[1536,768]{1,0:T(8,128)(2,1)} %x_ref.5, bf16[1536,768]{1,0:T(8,128)(2,1)} %cot_ref.1, ...), custom_call_target="tpu_custom_call" | custom-call | flops 21474836480 | bytes 25165824 | tf_op jit(solution)/shard_map/feed_forward/pallas_call | solution.py:1696
  136.0 80.8 %back_all.1 = (bf16[1536,768]{1,0:T(8,128)(2,1)}, bf16[1536,768]{1,0:T(8,128)(2,1)}, f32[96,832]{1,0:T(8,128)}, f32[96,1536]{1,0:T(8,128)}, f32[8,128]{1,0:T(8,128)}) custom-call(s32[2,12]{1,0:T(2,128)} %reduce_window_sum.11.ends_ref, bf16[1536,768]{1,0:T(8,128)(2,1)} %x_ref.5, f32[3,128,1408]{2,1,0:T(8,128)} %pad_maximum_fusion.strip_ref, ...), custom_call_target="tpu_custom_call" | custom-call | flops 21474836480 | bytes 33554432 | tf_op jit(solution)/shard_map/back_all/pallas_call | solution.py:2063
  216.8 10.4 %norm.1 = (f32[96,832]{1,0:T(8,128)}, f32[96,1536]{1,0:T(8,128)}, f32[8,128]{1,0:T(8,128)}, f32[8,128]{1,0:T(8,128)}, f32[32,128]{1,0:T(8,128)}) custom-call(f32[96,832]{1,0:T(8,128)} %get-tuple-element.81.refs_0_, f32[96,1536]{1,0:T(8,128)} %get-tuple-element.82.refs_1_, f32[8,128]{1,0:T(8,128)} %get-tuple-element.83.refs_2_), custom_call_target="tpu_custom_call" | custom-call | flops 1048576 | bytes 4194304 | tf_op jit(solution)/shard_map/norm/pallas_call | solution.py:792
  227.2 0.8 copy.58.refs_9_
  228.0 0.8 copy.60.refs_15_
  229.5 0.7 copy.59.refs_10_
  230.9 4.4 %adam.1 = (f32[3,96,192]{2,1,0:T(8,128)}, f32[192,96]{1,0:T(8,128)}, f32[2,96,512]{2,1,0:T(8,128)}, f32[512,96]{1,0:T(8,128)}, f32[32,12]{1,0:T(8,128)}, /*index...) custom-call(f32[96,832]{1,0:T(8,128)} %get-tuple-element.85.att_ref,, ...), custom_call_target="tpu_custom_call" | custom-call | flops 4194304 | bytes 8388608 | tf_op jit(solution)/shard_map/adam/pallas_call | solution.py:863
  235.3 1.8 copy.62
  237.1 1.8 copy.64
  238.8 1.8 copy.66
  240.6 1.4 copy.63
  242.0 1.4 copy.65
  243.4 1.4 copy.67
  244.7 1.2 slice.129
  245.9 1.4 copy.70
  247.3 1.1 copy-done
  248.5 1.4 copy.71
  (24 shorter events, 2.6 us)
Async XLA Ops:
  5.9 1.5 copy-start.2
  5.9 2.3 copy-start.8
  135.9 91.2 %copy-start.3 = (f32[512,96]{0,1:T(8,128)S(1)}, f32[512,96]{0,1:T(8,128)}, u32[]{:S(2)}) copy-start(f32[512,96]{0,1:T(8,128)} %param.33) | copy-start | bytes 589828
  135.9 92.1 %copy-start.4 = (f32[512,96]{0,1:T(8,128)S(1)}, f32[512,96]{0,1:T(8,128)}, u32[]{:S(2)}) copy-start(f32[512,96]{0,1:T(8,128)} %param.39) | copy-start | bytes 589828
  135.9 92.9 %copy-start.5 = (f32[32,12]{0,1:T(8,128)S(1)}, f32[32,12]{0,1:T(8,128)}, u32[]{:S(2)}) copy-start(f32[32,12]{0,1:T(8,128)} %param.28) | copy-start | bytes 4612
  135.9 93.6 %copy-start.6 = (f32[32,12]{0,1:T(8,128)S(1)}, f32[32,12]{0,1:T(8,128)}, u32[]{:S(2)}) copy-start(f32[32,12]{0,1:T(8,128)} %param.34) | copy-start | bytes 4612
  136.0 94.3 %copy-start.7 = (f32[32,12]{0,1:T(8,128)S(1)}, f32[32,12]{0,1:T(8,128)}, u32[]{:S(2)}) copy-start(f32[32,12]{0,1:T(8,128)} %param.40) | copy-start | bytes 4612
  230.9 15.0 %copy-start.1 = (bf16[1536,768]{1,0:T(8,128)(2,1)S(1)}, bf16[1536,768]{1,0:T(8,128)(2,1)}, u32[]{:S(2)}) copy-start(bf16[1536,768]{1,0:T(8,128)(2,1)} %get-tuple-element.232) | copy-start | bytes 7077892
  245.9 2.5 %copy-start = (bf16[1536,768]{1,0:T(8,128)(2,1)S(1)}, bf16[1536,768]{1,0:T(8,128)(2,1)}, u32[]{:S(2)}) copy-start(bf16[1536,768]{1,0:T(8,128)(2,1)} %get-tuple-element.233) | copy-start | bytes 7077892

commit v4 on v1

--- a/solution.py
+++ b/solution.py
@@ -812,7 +812,7 @@
     )(*operands)
 
 
-def adam_kernel(heads, hidden_cols, att_ref, feed_ref, gain_ref, table_ref, stat_ref, *refs):
+def adam_kernel(heads, hidden_cols, parts, att_ref, feed_ref, gain_ref, table_ref, stat_ref, *refs):
     weights, firsts, seconds = refs[:6], refs[6:12], refs[12:18]
     outs = refs[18:36]
     o_pad, s_pad = refs[36:]
@@ -835,12 +835,18 @@
 
     for i in range(3):
         update(0, i, att_ref[:, i * head_cols : (i + 1) * head_cols])
-    for i in range(2):
-        update(2, i, feed_ref[:, i * hidden_cols : (i + 1) * hidden_cols])
+    part = hidden_cols // parts
+    for j in range(parts):
+        span = slice(j * part, (j + 1) * part)
+        for i in range(2):
+            begin = (3 * j + i) * part if parts > 1 else i * part
+            update(2, (i, slice(None), span), feed_ref[:, begin : begin + part])
     o_pad[...] = jnp.zeros_like(o_pad)
     s_pad[...] = jnp.zeros_like(s_pad)
     o_pad[0:rows] = att_ref[:, gain_at + DH :]
-    s_pad[0:rows] = feed_ref[:, 2 * hidden_cols :]
+    for j in range(parts):
+        begin = (3 * j + 2) * part
+        s_pad[0:rows, j * part : (j + 1) * part] = feed_ref[:, begin : begin + part]
     update(1, slice(None), o_pad[...].T[:head_cols, :rows])
     update(3, slice(None), s_pad[...].T[:, :rows])
     columns = weights[4].shape[1]
@@ -848,12 +854,14 @@
     update(5, slice(None), gain_ref[1:3, :rows])
 
 
-def adam_call(att, feed_grad, gain, table, stat, params_in, firsts, seconds, heads, hidden_cols):
+def adam_call(
+    att, feed_grad, gain, table, stat, params_in, firsts, seconds, heads, hidden_cols, direct=False
+):
     vmem = pl.BlockSpec(memory_space=pltpu.VMEM)
     operands = [att, feed_grad, gain, table, stat, *params_in, *firsts, *seconds]
     pad_cols = att.shape[1] - (3 * heads * DH + DH)
     return pl.pallas_call(
-        functools.partial(adam_kernel, heads, hidden_cols),
+        functools.partial(adam_kernel, heads, hidden_cols, 2 if direct else 1),
         in_specs=[vmem] * len(operands),
         out_specs=[vmem] * 18,
         out_shape=[jax.ShapeDtypeStruct(a.shape, F32) for a in params_in] * 3,
@@ -867,30 +875,27 @@
     )(*operands)
 
 
-def place_kernel(half, offs_ref, *refs):
-    pieces = refs[:-2]
-    out_ref, sems = refs[-2:]
-    copies = []
-    for at, piece in enumerate(pieces):
-        begin = pl.multiple_of(offs_ref[at], LANES)
-        copies.append(
-            pltpu.make_async_copy(piece, out_ref.at[pl.ds(begin, half)], sems.at[at])
-        )
-    for copy in copies:
-        copy.start()
-    for copy in copies:
-        copy.wait()
+def place_kernel(offs_ref, *refs):
+    step = pl.program_id(0)
+    for at, piece in enumerate(refs[:-1]):
+
+        @pl.when(step == at)
+        def _(piece=piece):
+            refs[-1][...] = piece[...]
 
 
 def place(pieces, offs, rows):
     half, width = pieces[0].shape
-    hbm = pl.BlockSpec(memory_space=ANY)
+    count = len(pieces)
     return pl.pallas_call(
-        functools.partial(place_kernel, half),
-        in_specs=[pl.BlockSpec(memory_space=pltpu.SMEM)] + [hbm] * len(pieces),
-        out_specs=hbm,
+        place_kernel,
+        grid_spec=pltpu.PrefetchScalarGridSpec(
+            num_scalar_prefetch=1,
+            grid=(count,),
+            in_specs=[pl.BlockSpec((half, width), lambda i, *_: (0, 0))] * count,
+            out_specs=pl.BlockSpec((half, width), lambda i, offs: (offs[i] // half, 0)),
+        ),
         out_shape=jax.ShapeDtypeStruct((rows, width), pieces[0].dtype),
-        scratch_shapes=[pltpu.SemaphoreType.DMA((len(pieces),))],
         compiler_params=params(),
         cost_estimate=pl.CostEstimate(
             flops=0, bytes_accessed=4 * rows * width, transcendentals=0
@@ -899,7 +904,30 @@
     )(offs, *pieces)
 
 
-def body(wide, narrow, *arguments):
+def bias_strip(bucket_bias, n, heads, length):
+    table = lax.dynamic_slice_in_dim(bucket_bias, n * heads, heads, 1).T
+    blocks = length // LANES
+    near_r = (
+        jnp.arange(3 * LANES, dtype=jnp.int32)[None, :]
+        - LANES
+        - jnp.arange(LANES, dtype=jnp.int32)[:, None]
+    )
+    near_ids = bucket_of(near_r)
+    near = sum(
+        jnp.where(near_ids == b, table[:, b][:, None, None], 0.0) for b in range(32) if b != 16
+    )
+    far_shape = (heads, LANES, (blocks - 2) * LANES)
+    return jnp.concatenate(
+        [
+            jnp.broadcast_to(table[:, 15][:, None, None], far_shape),
+            near,
+            jnp.broadcast_to(table[:, 31][:, None, None], far_shape),
+        ],
+        axis=2,
+    )
+
+
+def general_body(wide, narrow, *arguments):
     (
         block_input,
         cotangent,
@@ -923,7 +951,6 @@
     w = lax.axis_index("wide")
     n = lax.axis_index("narrow")
     core = n % 2
-    direct = wide == 8 and rows % 16 == 0
 
     def swap(value, wide_mask, narrow_mask):
         pairs = [
@@ -934,33 +961,12 @@
         return lax.ppermute(value, ("wide", "narrow"), pairs)
 
     def gather(piece):
-        if not direct:
-            return [lax.all_gather(piece, "wide", axis=0, tiled=True)]
-        found = {0: piece}
-        for mask in (2, 4, 6):
-            found[mask] = swap(piece, mask, 0)
-        for mask in (0, 2, 4, 6):
-            found[mask + 1] = swap(found[mask], 1, 0)
-        return [found[mask] for mask in range(8)]
+        return [lax.all_gather(piece, "wide", axis=0, tiled=True)]
 
     def reduce_wide(outs):
-        if not direct:
-            return [lax.psum_scatter(outs[0], "wide", scatter_dimension=0, tiled=True)]
-        evens, odds = outs[:4], outs[4:]
-        got = []
-        for e in (1, 2, 3, 0):
-            came = swap(odds[e], 1, 0)
-            if e:
-                mixed = (evens[e] + came.astype(F32)).astype(BF16)
-                got.append(swap(mixed, 2 * e, 0))
-            else:
-                kept = [evens[0], came]
-        return kept + got
-
-    if direct:
-        offs = (jnp.arange(8, dtype=jnp.int32) ^ w) * rows
-    else:
-        offs = jnp.zeros((1,), jnp.int32)
+        return [lax.psum_scatter(outs[0], "wide", scatter_dimension=0, tiled=True)]
+
+    offs = jnp.zeros((1,), jnp.int32)
     order = jnp.stack([1 - core, core, n // 2])
 
     p_piece = jnp.concatenate(
@@ -984,26 +990,7 @@
     s_pieces = gather(shrink_weight.astype(BF16).T)
 
     ends = jnp.cumsum(lengths, axis=1)
-    table = lax.dynamic_slice_in_dim(bucket_bias, n * heads, heads, 1).T
-    blocks = length // LANES
-    near_r = (
-        jnp.arange(3 * LANES, dtype=jnp.int32)[None, :]
-        - LANES
-        - jnp.arange(LANES, dtype=jnp.int32)[:, None]
-    )
-    near_ids = bucket_of(near_r)
-    near = sum(
-        jnp.where(near_ids == b, table[:, b][:, None, None], 0.0) for b in range(32) if b != 16
-    )
-    far_shape = (heads, LANES, (blocks - 2) * LANES)
-    strip = jnp.concatenate(
-        [
-            jnp.broadcast_to(table[:, 15][:, None, None], far_shape),
-            near,
-            jnp.broadcast_to(table[:, 31][:, None, None], far_shape),
-        ],
-        axis=2,
-    )
+    strip = bias_strip(bucket_bias, n, heads, length)
 
     normed_one, qkv, atts, logs, fours = [], [], [], [], []
     for b in range(buffers):
@@ -1057,7 +1044,7 @@
         d_middles.append(d_middle)
         lows.append((low, swap(low, 0, 1)))
 
-    count = 8 if direct else 1
+    count = 1
     feed_outs = grad_call(
         functools.partial(feed_grad_kernel, count, hidden_cols),
         "feed_grad",
@@ -1169,8 +1156,1023 @@
     return (block_output, input_gradient, stat[0, 0], *results)
 
 
+class Place:
+    def __init__(self, wide, narrow):
+        self.wide, self.narrow = wide, narrow
+        self.w = lax.axis_index("wide")
+        self.n = lax.axis_index("narrow")
+        self.me = self.w * narrow + self.n
+        self.z, self.x = self.w // 2, self.w % 2
+        self.y, self.core = self.n // 2, self.n % 2
+        self.n_far = (self.n + 2) % 4
+        self.n_beside = self.n + 1 - 2 * self.core
+        self.n_diag = (self.n_beside + 2) % 4
+        self.across = (self.w, self.n_far)
+        self.beside = (self.w, self.n_beside)
+        self.flip = (self.z * 2 + 1 - self.x, self.n)
+
+    def along(self, m):
+        return (((self.z + m) % 4) * 2 + self.x, self.n)
+
+    def near_owner(self, m):
+        return ((self.z + m) % 4) * 2 + self.x
+
+    def far_owner(self, m):
+        return ((self.z + m) % 4) * 2 + 1 - self.x
+
+    def peer(self, k):
+        device = (self.me + k) % (self.wide * self.narrow)
+        return device, (device // self.narrow, device % self.narrow)
+
+
+def remote(source, target, send_sem, recv_sem, peer):
+    return pltpu.make_async_remote_copy(
+        src_ref=source,
+        dst_ref=target,
+        send_sem=send_sem,
+        recv_sem=recv_sem,
+        device_id=peer,
+        device_id_type=MESH,
+    )
+
+
+class Gather:
+    def __init__(self, spot, view, ssem, rsem):
+        self.spot, self.view, self.ssem, self.rsem = spot, view, ssem, rsem
+
+    def copy(self, owner, slot, peer):
+        return remote(
+            self.view(owner), self.view(owner), self.ssem.at[slot], self.rsem.at[owner], peer
+        )
+
+    def begin(self):
+        for m in (2, 1, 3):
+            self.copy(self.spot.w, m - 1, self.spot.along(m)).start()
+        self.copy(self.spot.w, 3, self.spot.flip).start()
+
+    def forward(self):
+        for m in (3, 1, 2):
+            owner = self.spot.near_owner(4 - m)
+            self.copy(owner, 0, self.spot.flip).wait_recv()
+            self.copy(owner, 3 + m, self.spot.flip).start()
+
+    def finish(self):
+        for m in range(4):
+            self.copy(self.spot.far_owner(4 - m), 0, self.spot.flip).wait_recv()
+
+    def drain(self):
+        for m in (1, 2, 3):
+            self.copy(self.spot.w, m - 1, self.spot.along(m)).wait_send()
+        for m in range(4):
+            self.copy(self.spot.near_owner(4 - m), 3 + m, self.spot.flip).wait_send()
+
+
+class Reduce:
+    def __init__(self, spot, even, odd, flipped, mixed, landed, sems_s, sems_r):
+        self.spot, self.even, self.odd = spot, even, odd
+        self.flipped, self.mixed, self.landed = flipped, mixed, landed
+        self.sems_s, self.sems_r = sems_s, sems_r
+
+    def over(self, m):
+        return remote(
+            self.odd(m), self.flipped.at[m], self.sems_s.at[m], self.sems_r.at[m], self.spot.flip
+        )
+
+    def along(self, m):
+        return remote(
+            self.mixed.at[m - 1],
+            self.landed.at[m - 1],
+            self.sems_s.at[3 + m],
+            self.sems_r.at[3 + m],
+            self.spot.along(m),
+        )
+
+    def begin(self):
+        for m in (2, 1, 3, 0):
+            self.over(m).start()
+
+    def relay(self):
+        for m in (2, 1, 3):
+            self.over(m).wait_recv()
+            self.mixed[m - 1] = (
+                self.even(m).astype(F32) + self.flipped[m].astype(F32)
+            ).astype(BF16)
+            self.along(m).start()
+
+    def result(self):
+        self.over(0).wait_recv()
+        value = self.even(0).astype(F32) + self.flipped[0].astype(F32)
+        for m in (1, 2, 3):
+            self.along(m).wait_recv()
+            value = value + self.landed[m - 1].astype(F32)
+        return value
+
+    def drain(self):
+        for m in range(4):
+            self.over(m).wait_send()
+        for m in (1, 2, 3):
+            self.along(m).wait_send()
+
+
+def segments_of(index, lengths_ref, buffer, slots):
+    end = lengths_ref[buffer, 0]
+    total = (index >= end).astype(jnp.int32)
+    for slot in range(1, slots):
+        end = end + lengths_ref[buffer, slot]
+        total = total + (index >= end).astype(jnp.int32)
+    return total
+
+
+def layer_kernel(dims, *refs):
+    buffers, slots, heads, hidden_cols, wide, narrow = dims
+    (
+        lengths_ref,
+        bias_ref,
+        x_ref,
+        cot_ref,
+        pw_ref,
+        ow_ref,
+        ew_ref,
+        sw_ref,
+        gn_ref,
+        out_ref,
+        in_ref,
+        p_grad,
+        o_grad,
+        feed_grad,
+        stat_ref,
+        gain_ref,
+        table_ref,
+        strip,
+        dstrip,
+        pbuf,
+        obuf,
+        fbuf,
+        att_ref,
+        qkv_ref,
+        log_ref,
+        low_ref,
+        middle_ref,
+        hid,
+        dg,
+        total,
+        opad,
+        gpad,
+        feed_flip,
+        feed_mix,
+        feed_land,
+        o_even,
+        o_odd,
+        o_flip,
+        o_mix,
+        o_land,
+        p_odd,
+        p_flip,
+        p_mix,
+        p_land,
+        ff_out,
+        ff_in,
+        ff_sum,
+        dn_out,
+        dn_in,
+        dn_sum,
+        dn_far,
+        ws,
+        kt,
+        vt,
+        qt,
+        gt,
+        dkt,
+        dvt,
+        gain_two_sum,
+        block,
+        inbox,
+        gather_s,
+        gather_r,
+        lone_s,
+        lone_r,
+        red_s,
+        red_r,
+        norm_s,
+        norm_r,
+        credit,
+    ) = refs
+    spot = Place(wide, narrow)
+    core = spot.core
+    devices = wide * narrow
+    tokens, width = x_ref.shape
+    length = tokens // buffers
+    half = length // 2
+    head_cols = heads * DH
+    qkv_cols = 3 * head_cols
+    part = hidden_cols // 2
+    chunk = 3 * part
+    blocks = length // LANES
+    owned = gn_ref.shape[1]
+    normed_one, normed_two = in_ref, out_ref
+    barrier = pltpu.get_barrier_semaphore()
+
+    @pl.loop(1, devices)
+    def _(k):
+        pl.semaphore_signal(barrier, inc=1, device_id=spot.peer(k)[1], device_id_type=MESH)
+
+    def at_rows(owner):
+        return pl.ds(pl.multiple_of(owner * owned, 16), owned)
+
+    def lone(view_from, view_to, slot, peer):
+        return remote(view_from, view_to, lone_s.at[slot], lone_r.at[slot], peer)
+
+    mine = at_rows(spot.w)
+    gpad[...] = jnp.zeros_like(gpad)
+    gpad[0:2, 0:owned] = gn_ref[...]
+    pbuf[mine] = jnp.concatenate(
+        [pw_ref[0], pw_ref[1], pw_ref[2], gpad[...].T[:owned, :DH]], axis=1
+    ).astype(BF16)
+    opad[...] = jnp.zeros_like(opad)
+    opad[0:head_cols, 0:owned] = ow_ref[...]
+    obuf[spot.n, mine] = opad[...].T[:owned, :head_cols].astype(BF16)
+    pl.semaphore_wait(barrier, devices - 1)
+    split = 3 * LANES
+    projections = [
+        Gather(
+            spot,
+            lambda v, span=span: pbuf.at[at_rows(v), span],
+            gather_s.at[at],
+            gather_r.at[at],
+        )
+        for at, span in enumerate((slice(0, split), slice(split, qkv_cols + DH)))
+    ]
+    for group in projections:
+        group.begin()
+    o_views = [
+        lambda v: obuf.at[spot.n, at_rows(v)],
+        lambda v: obuf.at[spot.n_far, at_rows(v)],
+    ]
+    outs_gather = [
+        Gather(spot, view, gather_s.at[2 + at], gather_r.at[2 + at])
+        for at, view in enumerate(o_views)
+    ]
+    lone(o_views[0](spot.w), o_views[0](spot.w), 0, spot.across).start()
+    for j in range(2):
+        span = slice(j * part, (j + 1) * part)
+        fbuf[mine, j * chunk : j * chunk + part] = ew_ref[0, :, span].astype(BF16)
+        fbuf[mine, j * chunk + part : j * chunk + 2 * part] = ew_ref[1, :, span].astype(BF16)
+        fbuf[mine, j * chunk + 2 * part : (j + 1) * chunk] = sw_ref[:, span].astype(BF16)
+    piece = chunk // 2
+    feeds_gather = [
+        Gather(
+            spot,
+            lambda v, at=at: fbuf.at[at_rows(v), at * piece : (at + 1) * piece],
+            gather_s.at[4 + at],
+            gather_r.at[4 + at],
+        )
+        for at in range(4)
+    ]
+
+    near_at = (blocks - 2) * LANES
+    near_end = near_at + 3 * LANES
+    near_ids = bucket_of(
+        lax.broadcasted_iota(jnp.int32, (LANES, 3 * LANES), 1)
+        - LANES
+        - lax.broadcasted_iota(jnp.int32, (LANES, 3 * LANES), 0)
+    )
+    for h in range(heads):
+        head = spot.n * heads + h
+        near = jnp.zeros((LANES, 3 * LANES), F32)
+        for b in range(32):
+            if b != 16:
+                near = jnp.where(near_ids == b, bias_ref[head, b], near)
+        strip[h, :, near_at:near_end] = near
+        strip[h, :, :near_at] = jnp.full((LANES, near_at), bias_ref[head, 15])
+        strip[h, :, near_end:] = jnp.full((LANES, near_at), bias_ref[head, 31])
+    dstrip[...] = jnp.zeros_like(dstrip)
+    gain_two_sum[...] = jnp.zeros_like(gain_two_sum)
+
+    for group in projections:
+        group.forward()
+    lone(o_views[1](spot.w), o_views[1](spot.w), 0, spot.across).wait_recv()
+    for group in outs_gather:
+        group.begin()
+    feeds_gather[0].begin()
+    for group in projections:
+        group.finish()
+
+    gains = pbuf[:, 4 * LANES :].astype(F32).T[qkv_cols - 4 * LANES : qkv_cols - 4 * LANES + 8]
+    gain_one, gain_two = gains[0:1], gains[1:2]
+
+    def relay_outs():
+        for group in outs_gather:
+            group.forward()
+        feeds_gather[1].begin()
+
+    def relay_feed(at):
+        def act():
+            feeds_gather[at].forward()
+            if at + 2 < 4:
+                feeds_gather[at + 2].begin()
+
+        return act
+
+    def outs_beside():
+        for group in outs_gather:
+            group.finish()
+        lone(obuf.at[spot.n], obuf.at[spot.n], 1, spot.beside).start()
+        lone(obuf.at[spot.n_far], obuf.at[spot.n_far], 2, spot.beside).start()
+
+    def att_view(which, b):
+        return att_ref.at[which, b * length : (b + 1) * length]
+
+    def att_copy(which, b, slot, peer):
+        return lone(att_view(which, b), att_view(which, b), 3 + 3 * b + slot, peer)
+
+    def att_send(b):
+        att_copy(spot.n, b, 0, spot.across).start()
+        att_copy(spot.n, b, 1, spot.beside).start()
+
+    def att_relay(b):
+        att_copy(spot.n_far, b, 0, spot.across).wait_recv()
+        att_copy(spot.n_far, b, 2, spot.beside).start()
+
+    step = 256
+    qkv_events = ({}, {1: relay_feed(2)})
+    att_events = (
+        {1: relay_outs, 3: relay_feed(0), 5: relay_feed(1)},
+        {0: outs_beside, 1: relay_feed(3), 3: lambda: att_relay(0)},
+    )
+
+    def fire(events, at):
+        for when, what in events.items():
+            pl.when(at == when)(what)
+
+    for b in range(buffers):
+        base = b * length
+
+        @pl.loop(0, length // step)
+        def _(at, b=b, base=base):
+            fire(qkv_events[b], at)
+            begin = pl.multiple_of(at * step, step)
+            here = pl.ds(begin, step)
+            span = pl.ds(pl.multiple_of(base + begin, step), step)
+            values = x_ref[span].astype(F32)
+            normed = (values * rms_scale(values) * gain_one).astype(BF16)
+            normed_one[span] = normed
+            qkv = mm(normed, pbuf[...]).astype(BF16)
+            qkv_ref[span] = qkv[:, :qkv_cols]
+            for h in range(heads):
+                k_at = head_cols + h * DH
+                v_at = 2 * head_cols + h * DH
+                kt[h, :, here] = qkv[:, k_at : k_at + DH].T
+                ws[h, here] = qkv[:, v_at : v_at + DH]
+
+        seg_keys = segments_of(
+            lax.broadcasted_iota(jnp.int32, (1, length), 1), lengths_ref, b, slots
+        )
+
+        @pl.loop(0, blocks)
+        def _(at, b=b, base=base, seg_keys=seg_keys):
+            fire(att_events[b], at)
+            begin = pl.multiple_of(at * LANES, LANES)
+            span = pl.ds(pl.multiple_of(base + begin, LANES), LANES)
+            window = pl.ds(pl.multiple_of((blocks - 1 - at) * LANES, LANES), length)
+            seg_rows = segments_of(
+                lax.broadcasted_iota(jnp.int32, (LANES, 1), 0) + begin, lengths_ref, b, slots
+            )
+            same = seg_rows == seg_keys
+            lane = lax.broadcasted_iota(jnp.int32, (LANES, LANES), 1)
+            logs = jnp.zeros((LANES, LANES), F32)
+            queries = qkv_ref[span, :head_cols]
+            outs = []
+            for h in range(heads):
+                scores = mm(queries[:, h * DH : (h + 1) * DH], kt[h]) + strip[h, :, window]
+                scores = jnp.where(same, scores, masked_score)
+                row_max = jnp.max(scores, axis=1, keepdims=True)
+                raised = jnp.exp(scores - row_max)
+                sums = jnp.sum(raised, axis=1, keepdims=True)
+                probs = (raised * (1.0 / sums)).astype(BF16)
+                outs.append(mm(probs, ws[h]).astype(BF16))
+                logs = jnp.where(lane == h, row_max + jnp.log(sums), logs)
+            log_ref[span] = logs
+            att_ref[spot.n, span] = jnp.concatenate(outs, axis=1)
+
+        att_send(b)
+
+    k0 = 0.7978845608028654
+    k1 = 0.044715
+
+    def half_rows(b, which):
+        return pl.ds(pl.multiple_of(b * length + which * half, LANES), half)
+
+    def ff_core(b):
+        return lone(ff_out.at[b], ff_in.at[b], 9 + b, spot.beside)
+
+    def ff_across(b):
+        return lone(ff_sum.at[b], ff_in.at[b], 11 + b, spot.across)
+
+    def dn_core(b, turn):
+        return lone(dn_out.at[b], dn_in.at[b], 13 + 2 * turn + b, spot.beside)
+
+    def dn_across(b, turn):
+        return lone(dn_sum.at[b], dn_far.at[b], 17 + 2 * turn + b, spot.across)
+
+    def low_core(b, which):
+        view = low_ref.at[half_rows(b, which)]
+        return lone(view, view, 21 + b, spot.beside)
+
+    def out_core(b, which):
+        view = out_ref.at[half_rows(b, which)]
+        return lone(view, view, 23 + b, spot.beside)
+
+    def in_core(b, which):
+        view = in_ref.at[half_rows(b, which)]
+        return lone(view, view, 25 + b, spot.beside)
+
+    def att_ready(b):
+        att_copy(spot.n_beside, b, 1, spot.beside).wait_recv()
+        att_copy(spot.n_diag, b, 2, spot.beside).wait_recv()
+
+    def first_feed():
+        att_ready(0)
+        lone(obuf.at[spot.n_beside], obuf.at[spot.n_beside], 1, spot.beside).wait_recv()
+        lone(obuf.at[spot.n_diag], obuf.at[spot.n_diag], 2, spot.beside).wait_recv()
+        feeds_gather[0].finish()
+        feeds_gather[1].finish()
+        feeds_gather[2].finish()
+        feeds_gather[3].finish()
+
+    @pl.loop(0, 2 * buffers)
+    def _(i):
+        fire({0: first_feed, 1: lambda: att_relay(1), 2: lambda: att_ready(1)}, i)
+        b = i // 2
+        keep = i % 2
+        which = (1 - core) * (1 - keep) + core * keep
+        rows = half_rows(b, which)
+        attention = mm(att_ref[0, rows], obuf[0], NT)
+        for a in range(1, 4):
+            attention = attention + mm(att_ref[a, rows], obuf[a], NT)
+        middle = x_ref[rows].astype(F32) + attention
+        scale_two = rms_scale(middle)
+        normed_rows = (middle * scale_two * gain_two).astype(BF16)
+        normed_two[rows] = normed_rows
+        cot = cot_ref[rows]
+        for j in range(2):
+            at = j * chunk
+            both = mm(normed_rows, fbuf[:, at : at + 2 * part])
+            gate, up = both[:, :part], both[:, part:]
+            square = gate * gate
+            tanh = jnp.tanh(k0 * (gate + k1 * (square * gate)))
+            lift = 0.5 * (1.0 + tanh)
+            active = gate * lift
+            slope = lift + (0.5 * gate) * (1.0 - tanh * tanh) * (k0 + (3.0 * k0 * k1) * square)
+            d_hidden = mm(cot, fbuf[:, at + 2 * part : at + 3 * part])
+            hid[rows, j * part : (j + 1) * part] = (active * up).astype(BF16)
+            dg[rows, 2 * j * part : (2 * j + 1) * part] = (d_hidden * up * slope).astype(BF16)
+            dg[rows, (2 * j + 1) * part : (2 * j + 2) * part] = (d_hidden * active).astype(BF16)
+        dn = mm(dg[rows, : 2 * part], fbuf[:, : 2 * part], NT) + mm(
+            dg[rows, 2 * part :], fbuf[:, chunk : chunk + 2 * part], NT
+        )
+        gain_two_sum[...] = gain_two_sum[...] + fold_rows(dn * middle * scale_two)
+        dn = dn.astype(BF16)
+        ff = (
+            mm(hid[rows, :part], fbuf[:, 2 * part : chunk], NT)
+            + mm(hid[rows, part:], fbuf[:, chunk + 2 * part :], NT)
+        ).astype(BF16)
+
+        @pl.when(keep == 0)
+        def _():
+            dn_out[b] = dn
+            dn_core(b, 0).start()
+            ff_out[b] = ff
+            ff_core(b).start()
+
+        @pl.when(keep == 1)
+        def _():
+            middle_ref[b] = middle
+            ff_core(b).wait_recv()
+            ff_sum[b] = (ff.astype(F32) + ff_in[b].astype(F32)).astype(BF16)
+            dn_core(b, 0).wait_recv()
+            dn_sum[b] = (dn.astype(F32) + dn_in[b].astype(F32)).astype(BF16)
+            dn_across(b, 0).start()
+
+    def own_block(b, i):
+        span = pl.ds(pl.multiple_of(i * LANES, LANES), LANES)
+        here = pl.ds(pl.multiple_of(b * length + core * half + i * LANES, LANES), LANES)
+        return span, here
+
+    def finish_middle(b):
+        dn_across(b, 0).wait_recv()
+        ff_across(b).start()
+
+        @pl.loop(0, half // LANES)
+        def _(i):
+            span, here = own_block(b, i)
+            upstream = dn_sum[b, span].astype(F32) + dn_far[b, span].astype(F32)
+            middle = middle_ref[b, span]
+            d_middle = cot_ref[here].astype(F32) + norm_back(
+                middle, rms_scale(middle), gain_two, upstream
+            )
+            low_ref[here] = d_middle.astype(BF16)
+
+        pl.semaphore_signal(credit.at[b], inc=1, device_id=spot.across, device_id_type=MESH)
+        low_core(b, core).start()
+
+    finish_middle(0)
+
+    for group in feeds_gather:
+        group.drain()
+    for b in range(buffers):
+        att_copy(spot.n_far, b, 2, spot.beside).wait_send()
+    for j in range(2):
+        for begin in range(0, width, step):
+            cols = slice(begin, begin + step)
+            total[cols, : 2 * part] = mm(
+                normed_two[:, cols], dg[:, 2 * j * part : (2 * j + 2) * part], TN
+            )
+            total[cols, 2 * part :] = mm(cot_ref[:, cols], hid[:, j * part : (j + 1) * part], TN)
+        span = slice(j * chunk, (j + 1) * chunk)
+        for m in range(4):
+            even = total[pl.ds(pl.multiple_of(spot.near_owner(m) * owned, 8), owned)]
+            odd = total[pl.ds(pl.multiple_of(spot.far_owner(m) * owned, 8), owned)]
+            fbuf[m * owned : (m + 1) * owned, span] = even.astype(BF16)
+            fbuf[(4 + m) * owned : (5 + m) * owned, span] = odd.astype(BF16)
+    feed_red = Reduce(
+        spot,
+        lambda m: fbuf[m * owned : (m + 1) * owned],
+        lambda m: fbuf.at[(4 + m) * owned : (5 + m) * owned],
+        feed_flip,
+        feed_mix,
+        feed_land,
+        red_s.at[0],
+        red_r.at[0],
+    )
+    feed_red.begin()
+
+    out_red = Reduce(
+        spot,
+        lambda m: o_even[m],
+        lambda m: o_odd.at[m],
+        o_flip,
+        o_mix,
+        o_land,
+        red_s.at[1],
+        red_r.at[1],
+    )
+
+    def out_weight_grad():
+        for begin in range(0, width, step):
+            cols = slice(begin, begin + step)
+            total[cols, :head_cols] = mm(low_ref[:, cols], att_ref[spot.n], TN)
+        for m in range(4):
+            even = total[pl.ds(pl.multiple_of(spot.near_owner(m) * owned, 8), owned), :head_cols]
+            odd = total[pl.ds(pl.multiple_of(spot.far_owner(m) * owned, 8), owned), :head_cols]
+            o_even[m] = even
+            o_odd[m] = odd.astype(BF16)
+        out_red.begin()
+
+    gain_sums = jnp.zeros((8, width), F32)
+    back_events = (
+        {2: feed_red.relay, 4: lambda: finish_middle(1)},
+        {2: out_red.relay},
+    )
+    for b in range(buffers):
+        base = b * length
+        rows = slice(base, base + length)
+        low_core(b, 1 - core).wait_recv()
+        if b == 1:
+            out_weight_grad()
+        grads = mm(low_ref[rows], obuf[spot.n]).astype(BF16)
+        att_ref[spot.n_far, :length] = grads
+        for h in range(heads):
+            keys = qkv_ref[rows, head_cols + h * DH : head_cols + (h + 1) * DH]
+            values = qkv_ref[rows, 2 * head_cols + h * DH : 2 * head_cols + (h + 1) * DH]
+            ws[h] = keys
+            kt[h] = keys.T
+            vt[h] = values.T
+            qt[h] = qkv_ref[rows, h * DH : (h + 1) * DH].T
+            gt[h] = grads[:, h * DH : (h + 1) * DH].T
+        dkt[...] = jnp.zeros_like(dkt)
+        dvt[...] = jnp.zeros_like(dvt)
+        seg_keys = segments_of(
+            lax.broadcasted_iota(jnp.int32, (1, length), 1), lengths_ref, b, slots
+        )
+
+        @pl.loop(0, blocks)
+        def _(at, b=b, base=base, seg_keys=seg_keys):
+            fire(back_events[b], at)
+            begin = pl.multiple_of(at * LANES, LANES)
+            here = pl.ds(begin, LANES)
+            span = pl.ds(pl.multiple_of(base + begin, LANES), LANES)
+            window = pl.ds(pl.multiple_of((blocks - 1 - at) * LANES, LANES), length)
+            seg_rows = segments_of(
+                lax.broadcasted_iota(jnp.int32, (LANES, 1), 0) + begin, lengths_ref, b, slots
+            )
+            same = seg_rows == seg_keys
+            logs = log_ref[span]
+            queries = qkv_ref[span, :head_cols]
+            incoming = att_ref[spot.n_far, here]
+            outs = []
+            for h in range(heads):
+                cols = slice(h * DH, (h + 1) * DH)
+                scores = mm(queries[:, cols], kt[h]) + strip[h, :, window]
+                scores = jnp.where(same, scores, masked_score)
+                probs = jnp.exp(scores - logs[:, h : h + 1])
+                d_probs = mm(incoming[:, cols], vt[h])
+                inner = jnp.sum(probs * d_probs, axis=1, keepdims=True)
+                d_scores = (probs * (d_probs - inner)).astype(BF16)
+                dstrip[h, :, window] = dstrip[h, :, window] + d_scores.astype(F32)
+                outs.append(mm(d_scores, ws[h]).astype(BF16))
+                dkt[h] = dkt[h] + mm(qt[h, :, here], d_scores)
+                dvt[h] = dvt[h] + mm(gt[h, :, here], probs.astype(BF16))
+            dg[span, :head_cols] = jnp.concatenate(outs, axis=1)
+
+        outs = [dkt[h].T.astype(BF16) for h in range(heads)]
+        outs += [dvt[h].T.astype(BF16) for h in range(heads)]
+        dg[rows, head_cols:qkv_cols] = jnp.concatenate(outs, axis=1)
+        for keep in range(2):
+            which = core if keep else 1 - core
+            here = half_rows(b, which)
+            if keep == 0:
+                dn_core(b, 0).wait_send()
+            else:
+                dn_across(b, 0).wait_send()
+            dn = mm(dg[here, :qkv_cols], pbuf[:, :qkv_cols], NT)
+            values = x_ref[here].astype(F32)
+            gain_sums = gain_sums + fold_rows(dn * values * rms_scale(values))
+            dn = dn.astype(BF16)
+            if keep == 0:
+                dn_out[b] = dn
+                dn_core(b, 1).start()
+            else:
+                dn_core(b, 1).wait_recv()
+                dn_sum[b] = (dn.astype(F32) + dn_in[b].astype(F32)).astype(BF16)
+                pl.semaphore_wait(credit.at[b], 1)
+                dn_across(b, 1).start()
+
+    row = lax.broadcasted_iota(jnp.int32, (LANES, width), 0)
+    gain_rows = jnp.where(
+        row == DH,
+        jnp.sum(gain_sums, axis=0, keepdims=True),
+        jnp.where(row == DH + 1, jnp.sum(gain_two_sum[...], axis=0, keepdims=True), 0.0),
+    )
+    gain_cols = gain_rows.T
+    p_cols = qkv_cols + DH
+    for begin in range(0, width, step):
+        cols = slice(begin, begin + step)
+        total[cols, :qkv_cols] = mm(normed_one[:, cols], dg[:, :qkv_cols], TN)
+        total[cols, qkv_cols:p_cols] = gain_cols[cols, DH:]
+    for m in range(4):
+        odd = total[pl.ds(pl.multiple_of(spot.far_owner(m) * owned, 8), owned), :p_cols]
+        p_odd[m] = odd.astype(BF16)
+    p_red = Reduce(
+        spot,
+        lambda m: total[pl.ds(pl.multiple_of(spot.near_owner(m) * owned, 8), owned), :p_cols],
+        lambda m: p_odd.at[m],
+        p_flip,
+        p_mix,
+        p_land,
+        red_s.at[2],
+        red_r.at[2],
+    )
+    p_red.begin()
+
+    def finish_out(b):
+        ff_across(b).wait_recv()
+
+        @pl.loop(0, half // LANES)
+        def _(i):
+            span, here = own_block(b, i)
+            joined = (ff_sum[b, span].astype(F32) + ff_in[b, span].astype(F32)).astype(BF16)
+            out_ref[here] = (middle_ref[b, span] + joined.astype(F32)).astype(BF16)
+
+        out_core(b, core).start()
+
+    def finish_in(b):
+        dn_across(b, 1).wait_recv()
+
+        @pl.loop(0, half // LANES)
+        def _(i):
+            span, here = own_block(b, i)
+            upstream = dn_sum[b, span].astype(F32) + dn_far[b, span].astype(F32)
+            values = x_ref[here].astype(F32)
+            in_ref[here] = (
+                low_ref[here].astype(F32)
+                + norm_back(values, rms_scale(values), gain_one, upstream)
+            ).astype(BF16)
+
+        in_core(b, core).start()
+
+    finish_out(0)
+    finish_out(1)
+    feed_value = feed_red.result()
+    feed_grad[...] = feed_value
+    squares = jnp.sum(jnp.sum(feed_value * feed_value, axis=1, keepdims=True), axis=0, keepdims=True)
+    o_value = out_red.result()
+    o_grad[...] = o_value
+    squares = squares + jnp.sum(
+        jnp.sum(o_value * o_value, axis=1, keepdims=True), axis=0, keepdims=True
+    )
+    p_red.relay()
+    for b in range(buffers):
+        out_core(b, 1 - core).wait_recv()
+    finish_in(0)
+
+    near_row = lax.broadcasted_iota(jnp.int32, (LANES, 4 * LANES), 0)
+    diag = lax.broadcasted_iota(jnp.int32, (1, 4 * LANES), 1)
+    ids = bucket_of(jnp.where(diag < 3 * LANES, diag - LANES, diag - 5 * LANES))
+    lane = lax.broadcasted_iota(jnp.int32, (1, LANES), 1)
+    onehot = jnp.where(near_row == ids, 1.0, 0.0)
+    bucket_line = jnp.zeros((1, LANES), F32)
+    for h in range(heads):
+        left = jnp.sum(jnp.sum(dstrip[h, :, :near_at], axis=0, keepdims=True), axis=1, keepdims=True)
+        right = jnp.sum(
+            jnp.sum(dstrip[h, :, near_end:], axis=0, keepdims=True), axis=1, keepdims=True
+        )
+        near = jnp.concatenate(
+            [dstrip[h, :, near_at:near_end], jnp.zeros((LANES, LANES), F32)], axis=1
+        )
+        for k in range(7):
+            near = jnp.where(
+                (near_row // (1 << k)) % 2 == 1, pltpu.roll(near, 4 * LANES - (1 << k), 1), near
+            )
+        binned = lax.dot_general(
+            jnp.broadcast_to(jnp.sum(near, axis=0, keepdims=True), (8, 4 * LANES)),
+            onehot,
+            NT,
+            precision=lax.Precision.HIGHEST,
+            preferred_element_type=F32,
+        )[0:1]
+        binned = binned + jnp.where(lane == 15, left, 0.0) + jnp.where(lane == 31, right, 0.0)
+        binned = jnp.where(lane < 32, binned, 0.0)
+        bucket_line = bucket_line + (pltpu.roll(binned, 32 * h, 1) if h else binned)
+
+    p_value = p_red.result()
+    p_grad[...] = p_value
+    p_lane = lax.broadcasted_iota(jnp.int32, p_value.shape, 1)
+    squared = jnp.where(p_lane < qkv_cols, p_value * p_value, 0.0)
+    squares = squares + jnp.sum(jnp.sum(squared, axis=1, keepdims=True), axis=0, keepdims=True)
+    low_lane = qkv_cols // LANES * LANES
+    gpad[...] = jnp.zeros_like(gpad)
+    gpad[0:owned, : p_cols - low_lane] = p_value[:, low_lane:]
+    turned = gpad[...].T
+    here = qkv_cols - low_lane
+    row8 = lax.broadcasted_iota(jnp.int32, (8, LANES), 0)
+    line = jnp.where(row8 == 0, squares, 0.0)
+    line = jnp.where(row8 == 1, turned[here : here + 1], line)
+    line = jnp.where(row8 == 2, turned[here + 1 : here + 2], line)
+    line = jnp.where(row8 == 3, bucket_line, line)
+    block[...] = line
+    inbox[spot.me] = line
+
+    @pl.loop(1, devices)
+    def _(k):
+        peer, where = spot.peer(k)
+        remote(block, inbox.at[spot.me], norm_s.at[k], norm_r.at[devices - k], where).start()
+
+    finish_in(1)
+
+    @pl.loop(1, devices)
+    def _(k):
+        peer, where = spot.peer(k)
+        copy = remote(block, inbox.at[peer], norm_s.at[k], norm_r.at[k], where)
+        copy.wait_send()
+        copy.wait_recv()
+
+    columns = [jnp.zeros((8, LANES), F32) for _ in range(narrow)]
+    gain_square = jnp.zeros((8, LANES), F32)
+    square_total = jnp.zeros((8, LANES), F32)
+    for a in range(wide):
+        summed = jnp.zeros((8, LANES), F32)
+        for c in range(narrow):
+            got = inbox[a * narrow + c]
+            summed = summed + got
+            columns[c] = columns[c] + got
+        square_total = square_total + summed
+        gain_square = gain_square + summed * summed
+    own = inbox[spot.w * narrow]
+    for c in range(1, narrow):
+        own = own + inbox[spot.w * narrow + c]
+    gain_ref[...] = own
+    gain_square = jnp.where((row8 == 1) | (row8 == 2), gain_square, 0.0)
+    norm_square = square_total[0:1, 0:1] + jnp.sum(
+        jnp.sum(gain_square, axis=1, keepdims=True), axis=0, keepdims=True
+    )
+    table_row = lax.broadcasted_iota(jnp.int32, (16, LANES), 0)
+    table = jnp.zeros((16, LANES), F32)
+    for c in range(narrow):
+        got = columns[c][3:4]
+        norm_square = norm_square + jnp.sum(got * got, axis=1, keepdims=True)
+        for h in range(heads):
+            moved = pltpu.roll(got, LANES - 32 * h, 1) if h else got
+            table = jnp.where(table_row == c * heads + h, moved, table)
+    table_ref[...] = table
+    global_norm = jnp.sqrt(norm_square)
+    factor = jnp.minimum(1.0, clip_limit / (global_norm + 1e-06))
+    stat_ref[...] = jnp.where(row8 == 0, global_norm, factor)
+
+    for b in range(buffers):
+        in_core(b, 1 - core).wait_recv()
+        for slot, which, peer in (
+            (0, spot.n, spot.across),
+            (1, spot.n, spot.beside),
+        ):
+            att_copy(which, b, slot, peer).wait_send()
+        ff_core(b).wait_send()
+        ff_across(b).wait_send()
+        dn_core(b, 1).wait_send()
+        dn_across(b, 1).wait_send()
+        low_core(b, core).wait_send()
+        out_core(b, core).wait_send()
+        in_core(b, core).wait_send()
+    lone(o_views[0](spot.w), o_views[0](spot.w), 0, spot.across).wait_send()
+    lone(obuf.at[spot.n], obuf.at[spot.n], 1, spot.beside).wait_send()
+    lone(obuf.at[spot.n_far], obuf.at[spot.n_far], 2, spot.beside).wait_send()
+    for group in projections + outs_gather:
+        group.drain()
+    for group in (feed_red, out_red, p_red):
+        group.drain()
+
+
+def layer(wide, narrow, lengths, bias, x, cot, pw, ow, ew, sw, gn):
+    tokens, width = x.shape
+    buffers, slots = lengths.shape
+    length = tokens // buffers
+    half = length // 2
+    head_cols = pw.shape[2]
+    heads = head_cols // DH
+    hidden_cols = ew.shape[2]
+    rows = gn.shape[1]
+    devices = wide * narrow
+    qkv_cols = 3 * head_cols
+    p_cols = qkv_cols + DH
+    feed_cols = 3 * hidden_cols
+    strip_shape = (heads, LANES, (2 * (length // LANES) - 1) * LANES)
+    vmem = pl.BlockSpec(memory_space=pltpu.VMEM)
+    smem = pl.BlockSpec(memory_space=pltpu.SMEM)
+    halves = pltpu.VMEM((buffers, half, width), BF16)
+    tall = pltpu.VMEM((heads, DH, length), BF16)
+    dma = pltpu.SemaphoreType.DMA
+
+    def pieces(count, cols, kind=BF16):
+        return pltpu.VMEM((count, rows, cols), kind)
+
+    return pl.pallas_call(
+        functools.partial(layer_kernel, (buffers, slots, heads, hidden_cols, wide, narrow)),
+        in_specs=[smem, smem] + [vmem] * 7,
+        out_specs=[vmem] * 8,
+        out_shape=[
+            jax.ShapeDtypeStruct((tokens, width), BF16),
+            jax.ShapeDtypeStruct((tokens, width), BF16),
+            jax.ShapeDtypeStruct((rows, p_cols), F32),
+            jax.ShapeDtypeStruct((rows, head_cols), F32),
+            jax.ShapeDtypeStruct((rows, feed_cols), F32),
+            jax.ShapeDtypeStruct((8, LANES), F32),
+            jax.ShapeDtypeStruct((8, LANES), F32),
+            jax.ShapeDtypeStruct((16, LANES), F32),
+        ],
+        scratch_shapes=[
+            pltpu.VMEM(strip_shape, F32),
+            pltpu.VMEM(strip_shape, F32),
+            pltpu.VMEM((width, p_cols), BF16),
+            pltpu.VMEM((narrow, width, head_cols), BF16),
+            pltpu.VMEM((width, feed_cols), BF16),
+            pltpu.VMEM((narrow, tokens, head_cols), BF16),
+            pltpu.VMEM((tokens, qkv_cols), BF16),
+            pltpu.VMEM((tokens, LANES), F32),
+            pltpu.VMEM((tokens, width), BF16),
+            pltpu.VMEM((buffers, half, width), F32),
+            pltpu.VMEM((tokens, hidden_cols), BF16),
+            pltpu.VMEM((tokens, 2 * hidden_cols), BF16),
+            pltpu.VMEM((width, feed_cols // 2), F32),
+            pltpu.VMEM((2 * LANES, LANES), F32),
+            pltpu.VMEM((LANES, LANES), F32),
+            pieces(4, feed_cols),
+            pieces(3, feed_cols),
+            pieces(3, feed_cols),
+            pieces(4, head_cols, F32),
+            pieces(4, head_cols),
+            pieces(4, head_cols),
+            pieces(3, head_cols),
+            pieces(3, head_cols),
+            pieces(4, p_cols),
+            pieces(4, p_cols),
+            pieces(3, p_cols),
+            pieces(3, p_cols),
+        ]
+        + [halves] * 7
+        + [
+            pltpu.VMEM((heads, length, DH), BF16),
+            tall,
+            tall,
+            tall,
+            tall,
+            pltpu.VMEM((heads, DH, length), F32),
+            pltpu.VMEM((heads, DH, length), F32),
+            pltpu.VMEM((8, width), F32),
+            pltpu.VMEM((8, LANES), F32),
+            pltpu.VMEM((devices, 8, LANES), F32),
+            dma((8, 7)),
+            dma((8, wide)),
+            dma((27,)),
+            dma((27,)),
+            dma((3, 7)),
+            dma((3, 7)),
+            dma((devices,)),
+            dma((devices,)),
+            pltpu.SemaphoreType.REGULAR((buffers,)),
+        ],
+        compiler_params=pltpu.CompilerParams(
+            vmem_limit_bytes=64 << 20, collective_id=0, has_side_effects=True
+        ),
+        cost_estimate=pl.CostEstimate(
+            flops=60 << 30, bytes_accessed=24 << 20, transcendentals=16 << 20
+        ),
+        name="layer",
+    )(lengths, bias, x, cot, pw, ow, ew, sw, gn)
+
+
+def update_kernel(heads, hidden_cols, p_ref, o_ref, feed_ref, stat_ref, gain_ref, table_ref, *refs):
+    weights, firsts, seconds = refs[:6], refs[6:12], refs[12:18]
+    outs, norm_ref, o_pad = refs[18:36], refs[36], refs[37]
+    factor = stat_ref[1:2, 0:1]
+    norm_ref[0, 0] = jnp.sum(stat_ref[0:1, 0:1])
+    head_cols = heads * DH
+    rows = p_ref.shape[0]
+
+    def update(which, index, gradient):
+        results = adam_update(
+            weights[which][index],
+            firsts[which][index],
+            seconds[which][index],
+            factor * gradient,
+            step_rates[which],
+            decay_rates[which],
+        )
+        for at in range(3):
+            outs[6 * at + which][index] = results[at]
+
+    for i in range(3):
+        update(0, i, p_ref[:, i * head_cols : (i + 1) * head_cols])
+    part = hidden_cols // 2
+    for j in range(2):
+        span = slice(j * part, (j + 1) * part)
+        for i in range(2):
+            begin = (3 * j + i) * part
+            update(2, (i, slice(None), span), feed_ref[:, begin : begin + part])
+        begin = (3 * j + 2) * part
+        update(3, (slice(None), span), feed_ref[:, begin : begin + part])
+    o_pad[...] = jnp.zeros_like(o_pad)
+    o_pad[0:rows, 0:head_cols] = o_ref[...]
+    update(1, slice(None), o_pad[...].T[:head_cols, :rows])
+    depth, columns = weights[4].shape
+    update(4, slice(None), table_ref[:depth, :columns])
+    update(5, slice(None), gain_ref[1:3, :rows])
+
+
+def update_call(grads, params_in, firsts, seconds, heads, hidden_cols):
+    vmem = pl.BlockSpec(memory_space=pltpu.VMEM)
+    operands = [*grads, *params_in, *firsts, *seconds]
+    return pl.pallas_call(
+        functools.partial(update_kernel, heads, hidden_cols),
+        in_specs=[vmem] * len(operands),
+        out_specs=[vmem] * 18 + [pl.BlockSpec(memory_space=pltpu.SMEM)],
+        out_shape=[jax.ShapeDtypeStruct(a.shape, F32) for a in params_in] * 3
+        + [jax.ShapeDtypeStruct((1, 1), F32)],
+        scratch_shapes=[pltpu.VMEM((LANES, 2 * LANES), F32)],
+        compiler_params=params(),
+        cost_estimate=pl.CostEstimate(flops=4 << 20, bytes_accessed=8 << 20, transcendentals=0),
+        name="update",
+    )(*operands)
+
+
+def direct_body(wide, narrow, *arguments):
+    block_input, cotangent, lengths = arguments[:3]
+    turned = (3, 4)
+    flat = [
+        value.T if at % 6 in turned else value for at, value in enumerate(arguments[3:21])
+    ]
+    weights, firsts, seconds = flat[:6], flat[6:12], flat[12:18]
+    project, output, expand, shrink, bias, gains = weights
+    block_output, input_gradient, *grads = layer(
+        wide,
+        narrow,
+        lengths,
+        bias,
+        block_input,
+        cotangent,
+        project,
+        output,
+        expand,
+        shrink,
+        gains,
+    )
+    heads = project.shape[2] // DH
+    *results, norm = update_call(grads, weights, firsts, seconds, heads, expand.shape[2])
+    results = [value.T if at % 6 in turned else value for at, value in enumerate(results)]
+    return (block_output, input_gradient, norm.reshape(()), *results)
+
+
 def solution(mesh):
     wide, narrow = mesh.shape["wide"], mesh.shape["narrow"]
+    body = direct_body if (wide, narrow) == (8, 4) else general_body
     state = (
         P(None, "wide", "narrow"),
         P("narrow", "wide"),

time: 494 us -> 182 us (0.37); the launches traced: 488 us -> 182 us
  Pallas kernels: 306 us -> 177 us
  starting transfers between devices: 72.9 us -> 0 us
  waiting for transfers between devices: 69.5 us -> 0 us
  local copies, waits for them, and re-layouts: 23.6 us -> 3.92 us
  other arithmetic: 13.8 us -> 0 us
    pallas_call x19 -> x2, Pallas kernels: 306 us -> 177 us  [the longest x1 173 us: layer(): pl.pallas_call(functools.partial(layer_kernel, (buffers, slots, heads, hi...]
    ppermute x75 -> x0, starting transfers between devices: 72.9 us -> none  [swap(): return lax.ppermute(value, ('wide', 'narrow'), pairs)]
    ppermute x75 -> x0, waiting for transfers between devices: 69.5 us -> none  [swap(): return lax.ppermute(value, ('wide', 'narrow'), pairs)]
    unnamed x217 -> x6, local copies, waits for them, and re-layouts: 20.3 us -> 3.92 us
  transfers between devices with their start and end apart: 75 -> 0, of which waited for: 18 -> 0; matrix products, arithmetic and copies ran while one was open for 6% -> 0% of each run, Pallas kernels for 48% -> 0%
where the time goes in v4:
time: 182 us
  Pallas kernels  177 us (97%)
  local copies, waits for them, and re-layouts  3.92 us (2%)
    pallas_call x1, Pallas kernels, layer(): pl.pallas_call(functools.partial(layer_kernel, (buffers, slots, heads, hi...  173 us
    pallas_call x1, Pallas kernels, update_call(): pl.pallas_call(functools.partial(update_kernel, heads, hidden_cols), in_s...  4.56 us
    unnamed x6, local copies, waits for them, and re-layouts  3.92 us

profile of v4, /device:TPU:0, one launch (start us, length us, event | category | flops | bytes accessed | tf_op | source)
XLA Modules:
  0.0 181.9 jit_solution(7572368925749394846)
XLA Ops:
  0.7 172.7 %layer.1 = (bf16[1536,768]{1,0:T(8,128)(2,1)}, bf16[1536,768]{1,0:T(8,128)(2,1)}, f32[96,640]{1,0:T(8,128)}, f32[96,192]{1,0:T(8,128)}, f32[96,1536]{1,0:T(8,128...) custom-call(s32[2,12]{1,0:T(2,128)} %refs_0_.2, f32[12,32]{1,0:T(8,128)} %bitcast.17, ...), custom_call_target="tpu_custom_call" | custom-call | flops 64424509440 | bytes 25165824 | tf_op jit(solution)/shard_map/layer/pallas_call | solution.py:2017
  173.3 0.0 copy-start.1
  173.3 4.6 %update.1 = (f32[3,96,192]{2,1,0:T(8,128)}, f32[192,96]{1,0:T(8,128)}, f32[2,96,512]{2,1,0:T(8,128)}, f32[96,512]{1,0:T(8,128)}, f32[12,32]{1,0:T(8,128)}, /*ind...) custom-call(f32[96,640]{1,0:T(8,128)} %get-tuple-element.50.p_ref, ...), custom_call_target="tpu_custom_call" | custom-call | flops 4194304 | bytes 8388608 | tf_op jit(solution)/shard_map/update/pallas_call | solution.py:2133
  177.9 0.0 copy-done.1
  177.9 0.0 copy-start
  177.9 1.4 copy.44
  179.3 1.1 copy-done
  180.4 1.4 copy.45
Async XLA Ops:
  173.3 4.6 %copy-start.1 = (bf16[1536,768]{1,0:T(8,128)(2,1)S(1)}, bf16[1536,768]{1,0:T(8,128)(2,1)}, u32[]{:S(2)}) copy-start(bf16[1536,768]{1,0:T(8,128)(2,1)} %get-tuple-element.96) | copy-start | bytes 7077892
  177.9 2.5 %copy-start = (bf16[1536,768]{1,0:T(8,128)(2,1)S(1)}, bf16[1536,768]{1,0:T(8,128)(2,1)}, u32[]{:S(2)}) copy-start(bf16[1536,768]{1,0:T(8,128)(2,1)} %get-tuple-element.97) | copy-start | bytes 7077892

commit v5 on v4

--- a/solution.py
+++ b/solution.py
@@ -1197,34 +1197,56 @@
 
 
 class Gather:
-    def __init__(self, spot, view, ssem, rsem):
+    def __init__(self, spot, view, ssem, rsem, flip_first=False):
         self.spot, self.view, self.ssem, self.rsem = spot, view, ssem, rsem
+        self.flip_first = flip_first
 
     def copy(self, owner, slot, peer):
         return remote(
             self.view(owner), self.view(owner), self.ssem.at[slot], self.rsem.at[owner], peer
         )
 
+    def landed(self, owner):
+        self.copy(owner, 0, self.spot.flip).wait_recv()
+
     def begin(self):
+        if self.flip_first:
+            self.copy(self.spot.w, 3, self.spot.flip).start()
         for m in (2, 1, 3):
             self.copy(self.spot.w, m - 1, self.spot.along(m)).start()
-        self.copy(self.spot.w, 3, self.spot.flip).start()
+        if not self.flip_first:
+            self.copy(self.spot.w, 3, self.spot.flip).start()
 
     def forward(self):
+        if self.flip_first:
+            owner = self.spot.far_owner(0)
+            self.landed(owner)
+            for m in (2, 1, 3):
+                self.copy(owner, 3 + m, self.spot.along(m)).start()
+            return
         for m in (3, 1, 2):
             owner = self.spot.near_owner(4 - m)
-            self.copy(owner, 0, self.spot.flip).wait_recv()
+            self.landed(owner)
             self.copy(owner, 3 + m, self.spot.flip).start()
 
     def finish(self):
-        for m in range(4):
-            self.copy(self.spot.far_owner(4 - m), 0, self.spot.flip).wait_recv()
+        if self.flip_first:
+            for m in (1, 2, 3):
+                self.landed(self.spot.near_owner(4 - m))
+        else:
+            self.landed(self.spot.far_owner(0))
+        for m in (1, 2, 3):
+            self.landed(self.spot.far_owner(4 - m))
 
     def drain(self):
+        self.copy(self.spot.w, 3, self.spot.flip).wait_send()
         for m in (1, 2, 3):
             self.copy(self.spot.w, m - 1, self.spot.along(m)).wait_send()
-        for m in range(4):
-            self.copy(self.spot.near_owner(4 - m), 3 + m, self.spot.flip).wait_send()
+            if self.flip_first:
+                owner, peer = self.spot.far_owner(0), self.spot.along(m)
+            else:
+                owner, peer = self.spot.near_owner(4 - m), self.spot.flip
+            self.copy(owner, 3 + m, peer).wait_send()
 
 
 class Reduce:
@@ -1235,13 +1257,13 @@
 
     def over(self, m):
         return remote(
-            self.odd(m), self.flipped.at[m], self.sems_s.at[m], self.sems_r.at[m], self.spot.flip
+            self.odd(m), self.flipped(m), self.sems_s.at[m], self.sems_r.at[m], self.spot.flip
         )
 
     def along(self, m):
         return remote(
-            self.mixed.at[m - 1],
-            self.landed.at[m - 1],
+            self.mixed(m - 1),
+            self.landed(m - 1),
             self.sems_s.at[3 + m],
             self.sems_r.at[3 + m],
             self.spot.along(m),
@@ -1251,20 +1273,20 @@
         for m in (2, 1, 3, 0):
             self.over(m).start()
 
-    def relay(self):
-        for m in (2, 1, 3):
+    def relay(self, *ms):
+        for m in ms:
             self.over(m).wait_recv()
-            self.mixed[m - 1] = (
-                self.even(m).astype(F32) + self.flipped[m].astype(F32)
+            self.mixed(m - 1)[...] = (
+                self.even(m).astype(F32) + self.flipped(m)[...].astype(F32)
             ).astype(BF16)
             self.along(m).start()
 
     def result(self):
         self.over(0).wait_recv()
-        value = self.even(0).astype(F32) + self.flipped[0].astype(F32)
+        value = self.even(0).astype(F32) + self.flipped(0)[...].astype(F32)
         for m in (1, 2, 3):
             self.along(m).wait_recv()
-            value = value + self.landed[m - 1].astype(F32)
+            value = value + self.landed(m - 1)[...].astype(F32)
         return value
 
     def drain(self):
@@ -1288,8 +1310,8 @@
     (
         lengths_ref,
         bias_ref,
-        x_ref,
-        cot_ref,
+        x_hbm,
+        cot_hbm,
         pw_ref,
         ow_ref,
         ew_ref,
@@ -1303,6 +1325,8 @@
         stat_ref,
         gain_ref,
         table_ref,
+        x_ref,
+        cot_ref,
         strip,
         dstrip,
         pbuf,
@@ -1356,6 +1380,7 @@
         norm_s,
         norm_r,
         credit,
+        load,
     ) = refs
     spot = Place(wide, narrow)
     core = spot.core
@@ -1370,6 +1395,12 @@
     blocks = length // LANES
     owned = gn_ref.shape[1]
     normed_one, normed_two = in_ref, out_ref
+    loads = [
+        pltpu.make_async_copy(x_hbm, x_ref, load.at[0]),
+        pltpu.make_async_copy(cot_hbm, cot_ref, load.at[1]),
+    ]
+    for copy in loads:
+        copy.start()
     barrier = pltpu.get_barrier_semaphore()
 
     @pl.loop(1, devices)
@@ -1388,9 +1419,6 @@
     pbuf[mine] = jnp.concatenate(
         [pw_ref[0], pw_ref[1], pw_ref[2], gpad[...].T[:owned, :DH]], axis=1
     ).astype(BF16)
-    opad[...] = jnp.zeros_like(opad)
-    opad[0:head_cols, 0:owned] = ow_ref[...]
-    obuf[spot.n, mine] = opad[...].T[:owned, :head_cols].astype(BF16)
     pl.semaphore_wait(barrier, devices - 1)
     split = 3 * LANES
     projections = [
@@ -1404,6 +1432,9 @@
     ]
     for group in projections:
         group.begin()
+    opad[...] = jnp.zeros_like(opad)
+    opad[0:head_cols, 0:owned] = ow_ref[...]
+    obuf[spot.n, mine] = opad[...].T[:owned, :head_cols].astype(BF16)
     o_views = [
         lambda v: obuf.at[spot.n, at_rows(v)],
         lambda v: obuf.at[spot.n_far, at_rows(v)],
@@ -1425,6 +1456,7 @@
             lambda v, at=at: fbuf.at[at_rows(v), at * piece : (at + 1) * piece],
             gather_s.at[4 + at],
             gather_r.at[4 + at],
+            flip_first=at == 3,
         )
         for at in range(4)
     ]
@@ -1445,17 +1477,17 @@
         strip[h, :, near_at:near_end] = near
         strip[h, :, :near_at] = jnp.full((LANES, near_at), bias_ref[head, 15])
         strip[h, :, near_end:] = jnp.full((LANES, near_at), bias_ref[head, 31])
+    lone(o_views[1](spot.w), o_views[1](spot.w), 0, spot.across).wait_recv()
+    for group in outs_gather + feeds_gather:
+        group.begin()
     dstrip[...] = jnp.zeros_like(dstrip)
     gain_two_sum[...] = jnp.zeros_like(gain_two_sum)
 
-    for group in projections:
-        group.forward()
-    lone(o_views[1](spot.w), o_views[1](spot.w), 0, spot.across).wait_recv()
-    for group in outs_gather:
-        group.begin()
-    feeds_gather[0].begin()
+    projections[0].forward()
+    projections[1].forward()
     for group in projections:
         group.finish()
+    loads[0].wait()
 
     gains = pbuf[:, 4 * LANES :].astype(F32).T[qkv_cols - 4 * LANES : qkv_cols - 4 * LANES + 8]
     gain_one, gain_two = gains[0:1], gains[1:2]
@@ -1463,15 +1495,6 @@
     def relay_outs():
         for group in outs_gather:
             group.forward()
-        feeds_gather[1].begin()
-
-    def relay_feed(at):
-        def act():
-            feeds_gather[at].forward()
-            if at + 2 < 4:
-                feeds_gather[at + 2].begin()
-
-        return act
 
     def outs_beside():
         for group in outs_gather:
@@ -1494,10 +1517,10 @@
         att_copy(spot.n_far, b, 2, spot.beside).start()
 
     step = 256
-    qkv_events = ({}, {1: relay_feed(2)})
+    qkv_events = ({}, {0: feeds_gather[0].forward})
     att_events = (
-        {1: relay_outs, 3: relay_feed(0), 5: relay_feed(1)},
-        {0: outs_beside, 1: relay_feed(3), 3: lambda: att_relay(0)},
+        {2: relay_outs, 5: feeds_gather[3].forward},
+        {0: outs_beside, 3: lambda: att_relay(0), 4: feeds_gather[1].forward},
     )
 
     def fire(events, at):
@@ -1586,72 +1609,101 @@
         view = in_ref.at[half_rows(b, which)]
         return lone(view, view, 25 + b, spot.beside)
 
-    def att_ready(b):
-        att_copy(spot.n_beside, b, 1, spot.beside).wait_recv()
-        att_copy(spot.n_diag, b, 2, spot.beside).wait_recv()
-
-    def first_feed():
-        att_ready(0)
+    def outs_ready():
+        loads[1].wait()
         lone(obuf.at[spot.n_beside], obuf.at[spot.n_beside], 1, spot.beside).wait_recv()
         lone(obuf.at[spot.n_diag], obuf.at[spot.n_diag], 2, spot.beside).wait_recv()
+
+    def first_feed():
+        feeds_gather[2].forward()
         feeds_gather[0].finish()
         feeds_gather[1].finish()
+
+    def last_feed():
+        att_relay(1)
         feeds_gather[2].finish()
         feeds_gather[3].finish()
 
-    @pl.loop(0, 2 * buffers)
-    def _(i):
-        fire({0: first_feed, 1: lambda: att_relay(1), 2: lambda: att_ready(1)}, i)
-        b = i // 2
-        keep = i % 2
-        which = (1 - core) * (1 - keep) + core * keep
-        rows = half_rows(b, which)
-        attention = mm(att_ref[0, rows], obuf[0], NT)
-        for a in range(1, 4):
-            attention = attention + mm(att_ref[a, rows], obuf[a], NT)
-        middle = x_ref[rows].astype(F32) + attention
-        scale_two = rms_scale(middle)
-        normed_rows = (middle * scale_two * gain_two).astype(BF16)
-        normed_two[rows] = normed_rows
-        cot = cot_ref[rows]
-        for j in range(2):
-            at = j * chunk
-            both = mm(normed_rows, fbuf[:, at : at + 2 * part])
-            gate, up = both[:, :part], both[:, part:]
-            square = gate * gate
-            tanh = jnp.tanh(k0 * (gate + k1 * (square * gate)))
-            lift = 0.5 * (1.0 + tanh)
-            active = gate * lift
-            slope = lift + (0.5 * gate) * (1.0 - tanh * tanh) * (k0 + (3.0 * k0 * k1) * square)
-            d_hidden = mm(cot, fbuf[:, at + 2 * part : at + 3 * part])
-            hid[rows, j * part : (j + 1) * part] = (active * up).astype(BF16)
-            dg[rows, 2 * j * part : (2 * j + 1) * part] = (d_hidden * up * slope).astype(BF16)
-            dg[rows, (2 * j + 1) * part : (2 * j + 2) * part] = (d_hidden * active).astype(BF16)
-        dn = mm(dg[rows, : 2 * part], fbuf[:, : 2 * part], NT) + mm(
-            dg[rows, 2 * part :], fbuf[:, chunk : chunk + 2 * part], NT
-        )
-        gain_two_sum[...] = gain_two_sum[...] + fold_rows(dn * middle * scale_two)
-        dn = dn.astype(BF16)
-        ff = (
-            mm(hid[rows, :part], fbuf[:, 2 * part : chunk], NT)
-            + mm(hid[rows, part:], fbuf[:, chunk + 2 * part :], NT)
-        ).astype(BF16)
-
-        @pl.when(keep == 0)
-        def _():
-            dn_out[b] = dn
-            dn_core(b, 0).start()
-            ff_out[b] = ff
-            ff_core(b).start()
-
-        @pl.when(keep == 1)
-        def _():
-            middle_ref[b] = middle
-            ff_core(b).wait_recv()
-            ff_sum[b] = (ff.astype(F32) + ff_in[b].astype(F32)).astype(BF16)
-            dn_core(b, 0).wait_recv()
-            dn_sum[b] = (dn.astype(F32) + dn_in[b].astype(F32)).astype(BF16)
-            dn_across(b, 0).start()
+    def half_of(b, keep):
+        return half_rows(b, (1 - core) * (1 - keep) + core * keep)
+
+    def hidden_part(j, rows, normed_rows):
+        at = j * chunk
+        both = mm(normed_rows, fbuf[:, at : at + 2 * part])
+        gate, up = both[:, :part], both[:, part:]
+        square = gate * gate
+        tanh = jnp.tanh(k0 * (gate + k1 * (square * gate)))
+        lift = 0.5 * (1.0 + tanh)
+        active = gate * lift
+        slope = lift + (0.5 * gate) * (1.0 - tanh * tanh) * (k0 + (3.0 * k0 * k1) * square)
+        d_hidden = mm(cot_ref[rows], fbuf[:, at + 2 * part : at + 3 * part])
+        hid[rows, j * part : (j + 1) * part] = (active * up).astype(BF16)
+        dg[rows, 2 * j * part : (2 * j + 1) * part] = (d_hidden * up * slope).astype(BF16)
+        dg[rows, (2 * j + 1) * part : (2 * j + 2) * part] = (d_hidden * active).astype(BF16)
+
+    @pl.loop(0, buffers)
+    def _(b):
+        def att_ready():
+            span = pl.ds(pl.multiple_of(b * length, LANES), length)
+            for slot, which in ((4, spot.n_beside), (5, spot.n_diag)):
+                view = att_ref.at[which, span]
+                lone(view, view, slot + 3 * b, spot.beside).wait_recv()
+
+        att_ready()
+
+        @pl.loop(0, 2)
+        def _(keep):
+            pl.when((b == 0) & (keep == 0))(outs_ready)
+            rows = half_of(b, keep)
+            attention = mm(att_ref[0, rows], obuf[0], NT)
+            for a in range(1, 4):
+                attention = attention + mm(att_ref[a, rows], obuf[a], NT)
+            middle = x_ref[rows].astype(F32) + attention
+            normed_rows = (middle * rms_scale(middle) * gain_two).astype(BF16)
+            normed_two[rows] = normed_rows
+
+            @pl.when(keep == 1)
+            def _():
+                middle_ref[b] = middle
+
+            pl.when((b == 0) & (keep == 0))(first_feed)
+            hidden_part(0, rows, normed_two[rows])
+
+        pl.when(b == 0)(last_feed)
+
+        @pl.loop(0, 2)
+        def _(keep):
+            rows = half_of(b, keep)
+            normed_rows = normed_two[rows]
+            hidden_part(1, rows, normed_rows)
+            dn = mm(dg[rows, : 2 * part], fbuf[:, : 2 * part], NT) + mm(
+                dg[rows, 2 * part :], fbuf[:, chunk : chunk + 2 * part], NT
+            )
+            gain_two_sum[...] = gain_two_sum[...] + fold_rows(dn * normed_rows.astype(F32))
+            dn = dn.astype(BF16)
+
+            @pl.when(keep == 0)
+            def _():
+                dn_out[b] = dn
+                dn_core(b, 0).start()
+
+            ff = (
+                mm(hid[rows, :part], fbuf[:, 2 * part : chunk], NT)
+                + mm(hid[rows, part:], fbuf[:, chunk + 2 * part :], NT)
+            ).astype(BF16)
+
+            @pl.when(keep == 0)
+            def _():
+                ff_out[b] = ff
+                ff_core(b).start()
+
+            @pl.when(keep == 1)
+            def _():
+                ff_core(b).wait_recv()
+                ff_sum[b] = (ff.astype(F32) + ff_in[b].astype(F32)).astype(BF16)
+                dn_core(b, 0).wait_recv()
+                dn_sum[b] = (dn.astype(F32) + dn_in[b].astype(F32)).astype(BF16)
+                dn_across(b, 0).start()
 
     def own_block(b, i):
         span = pl.ds(pl.multiple_of(i * LANES, LANES), LANES)
@@ -1660,7 +1712,6 @@
 
     def finish_middle(b):
         dn_across(b, 0).wait_recv()
-        ff_across(b).start()
 
         @pl.loop(0, half // LANES)
         def _(i):
@@ -1675,12 +1726,11 @@
         pl.semaphore_signal(credit.at[b], inc=1, device_id=spot.across, device_id_type=MESH)
         low_core(b, core).start()
 
-    finish_middle(0)
-
     for group in feeds_gather:
         group.drain()
     for b in range(buffers):
         att_copy(spot.n_far, b, 2, spot.beside).wait_send()
+    feed_reds = []
     for j in range(2):
         for begin in range(0, width, step):
             cols = slice(begin, begin + step)
@@ -1694,27 +1744,30 @@
             odd = total[pl.ds(pl.multiple_of(spot.far_owner(m) * owned, 8), owned)]
             fbuf[m * owned : (m + 1) * owned, span] = even.astype(BF16)
             fbuf[(4 + m) * owned : (5 + m) * owned, span] = odd.astype(BF16)
-    feed_red = Reduce(
-        spot,
-        lambda m: fbuf[m * owned : (m + 1) * owned],
-        lambda m: fbuf.at[(4 + m) * owned : (5 + m) * owned],
-        feed_flip,
-        feed_mix,
-        feed_land,
-        red_s.at[0],
-        red_r.at[0],
-    )
-    feed_red.begin()
+        red = Reduce(
+            spot,
+            lambda m, span=span: fbuf[m * owned : (m + 1) * owned, span],
+            lambda m, span=span: fbuf.at[(4 + m) * owned : (5 + m) * owned, span],
+            lambda m, span=span: feed_flip.at[m, :, span],
+            lambda m, span=span: feed_mix.at[m, :, span],
+            lambda m, span=span: feed_land.at[m, :, span],
+            red_s.at[j],
+            red_r.at[j],
+        )
+        red.begin()
+        feed_reds.append(red)
+    finish_middle(0)
+    feed_reds[0].relay(2, 1)
 
     out_red = Reduce(
         spot,
         lambda m: o_even[m],
         lambda m: o_odd.at[m],
-        o_flip,
-        o_mix,
-        o_land,
-        red_s.at[1],
-        red_r.at[1],
+        lambda m: o_flip.at[m],
+        lambda m: o_mix.at[m],
+        lambda m: o_land.at[m],
+        red_s.at[2],
+        red_r.at[2],
     )
 
     def out_weight_grad():
@@ -1729,9 +1782,18 @@
         out_red.begin()
 
     gain_sums = jnp.zeros((8, width), F32)
+    def second_middle():
+        finish_middle(1)
+        ff_across(1).start()
+
     back_events = (
-        {2: feed_red.relay, 4: lambda: finish_middle(1)},
-        {2: out_red.relay},
+        {
+            0: lambda: feed_reds[0].relay(3),
+            2: lambda: ff_across(0).start(),
+            3: lambda: feed_reds[1].relay(2),
+            5: lambda: (feed_reds[1].relay(1), second_middle())[1],
+        },
+        {0: lambda: feed_reds[1].relay(3), 3: lambda: out_red.relay(2, 1), 4: lambda: out_red.relay(3)},
     )
     for b in range(buffers):
         base = b * length
@@ -1811,28 +1873,39 @@
     gain_rows = jnp.where(
         row == DH,
         jnp.sum(gain_sums, axis=0, keepdims=True),
-        jnp.where(row == DH + 1, jnp.sum(gain_two_sum[...], axis=0, keepdims=True), 0.0),
+        jnp.where(
+            row == DH + 1, jnp.sum(gain_two_sum[...], axis=0, keepdims=True) / gain_two, 0.0
+        ),
     )
     gain_cols = gain_rows.T
     p_cols = qkv_cols + DH
-    for begin in range(0, width, step):
-        cols = slice(begin, begin + step)
-        total[cols, :qkv_cols] = mm(normed_one[:, cols], dg[:, :qkv_cols], TN)
-        total[cols, qkv_cols:p_cols] = gain_cols[cols, DH:]
-    for m in range(4):
-        odd = total[pl.ds(pl.multiple_of(spot.far_owner(m) * owned, 8), owned), :p_cols]
-        p_odd[m] = odd.astype(BF16)
-    p_red = Reduce(
-        spot,
-        lambda m: total[pl.ds(pl.multiple_of(spot.near_owner(m) * owned, 8), owned), :p_cols],
-        lambda m: p_odd.at[m],
-        p_flip,
-        p_mix,
-        p_land,
-        red_s.at[2],
-        red_r.at[2],
-    )
-    p_red.begin()
+    p_reds = []
+    for at, span in enumerate((slice(0, split), slice(split, p_cols))):
+        stop = min(span.stop, qkv_cols)
+        for begin in range(0, width, step):
+            cols = slice(begin, begin + step)
+            total[cols, span.start : stop] = mm(
+                normed_one[:, cols], dg[:, span.start : stop], TN
+            )
+            if at:
+                total[cols, qkv_cols:p_cols] = gain_cols[cols, DH:]
+        for m in range(4):
+            odd = total[pl.ds(pl.multiple_of(spot.far_owner(m) * owned, 8), owned), span]
+            p_odd[m, :, span] = odd.astype(BF16)
+        red = Reduce(
+            spot,
+            lambda m, span=span: total[
+                pl.ds(pl.multiple_of(spot.near_owner(m) * owned, 8), owned), span
+            ],
+            lambda m, span=span: p_odd.at[m, :, span],
+            lambda m, span=span: p_flip.at[m, :, span],
+            lambda m, span=span: p_mix.at[m, :, span],
+            lambda m, span=span: p_land.at[m, :, span],
+            red_s.at[3 + at],
+            red_r.at[3 + at],
+        )
+        red.begin()
+        p_reds.append(red)
 
     def finish_out(b):
         ff_across(b).wait_recv()
@@ -1860,17 +1933,21 @@
 
         in_core(b, core).start()
 
+    def square_of(value):
+        return jnp.sum(jnp.sum(value * value, axis=1, keepdims=True), axis=0, keepdims=True)
+
     finish_out(0)
+    p_reds[0].relay(2, 1, 3)
     finish_out(1)
-    feed_value = feed_red.result()
-    feed_grad[...] = feed_value
-    squares = jnp.sum(jnp.sum(feed_value * feed_value, axis=1, keepdims=True), axis=0, keepdims=True)
-    o_value = out_red.result()
-    o_grad[...] = o_value
-    squares = squares + jnp.sum(
-        jnp.sum(o_value * o_value, axis=1, keepdims=True), axis=0, keepdims=True
-    )
-    p_red.relay()
+    squares = jnp.zeros((1, 1), F32)
+    for j in range(2):
+        value = feed_reds[j].result()
+        feed_grad[:, j * chunk : (j + 1) * chunk] = value
+        squares = squares + square_of(value)
+    p_reds[1].relay(2, 1, 3)
+    value = out_red.result()
+    o_grad[...] = value
+    squares = squares + square_of(value)
     for b in range(buffers):
         out_core(b, 1 - core).wait_recv()
     finish_in(0)
@@ -1904,14 +1981,16 @@
         binned = jnp.where(lane < 32, binned, 0.0)
         bucket_line = bucket_line + (pltpu.roll(binned, 32 * h, 1) if h else binned)
 
-    p_value = p_red.result()
-    p_grad[...] = p_value
-    p_lane = lax.broadcasted_iota(jnp.int32, p_value.shape, 1)
-    squared = jnp.where(p_lane < qkv_cols, p_value * p_value, 0.0)
-    squares = squares + jnp.sum(jnp.sum(squared, axis=1, keepdims=True), axis=0, keepdims=True)
+    value = p_reds[0].result()
+    p_grad[:, :split] = value
+    squares = squares + square_of(value)
+    value = p_reds[1].result()
+    p_grad[:, split:] = value
+    kept = lax.broadcasted_iota(jnp.int32, value.shape, 1) < qkv_cols - split
+    squares = squares + square_of(jnp.where(kept, value, 0.0))
     low_lane = qkv_cols // LANES * LANES
     gpad[...] = jnp.zeros_like(gpad)
-    gpad[0:owned, : p_cols - low_lane] = p_value[:, low_lane:]
+    gpad[0:owned, : p_cols - low_lane] = value[:, low_lane - split :]
     turned = gpad[...].T
     here = qkv_cols - low_lane
     row8 = lax.broadcasted_iota(jnp.int32, (8, LANES), 0)
@@ -1987,7 +2066,7 @@
     lone(obuf.at[spot.n_far], obuf.at[spot.n_far], 2, spot.beside).wait_send()
     for group in projections + outs_gather:
         group.drain()
-    for group in (feed_red, out_red, p_red):
+    for group in feed_reds + p_reds + [out_red]:
         group.drain()
 
 
@@ -2016,7 +2095,8 @@
 
     return pl.pallas_call(
         functools.partial(layer_kernel, (buffers, slots, heads, hidden_cols, wide, narrow)),
-        in_specs=[smem, smem] + [vmem] * 7,
+        in_specs=[smem, smem, pl.BlockSpec(memory_space=ANY), pl.BlockSpec(memory_space=ANY)]
+        + [vmem] * 5,
         out_specs=[vmem] * 8,
         out_shape=[
             jax.ShapeDtypeStruct((tokens, width), BF16),
@@ -2029,6 +2109,8 @@
             jax.ShapeDtypeStruct((16, LANES), F32),
         ],
         scratch_shapes=[
+            pltpu.VMEM((tokens, width), BF16),
+            pltpu.VMEM((tokens, width), BF16),
             pltpu.VMEM(strip_shape, F32),
             pltpu.VMEM(strip_shape, F32),
             pltpu.VMEM((width, p_cols), BF16),
@@ -2073,11 +2155,12 @@
             dma((8, wide)),
             dma((27,)),
             dma((27,)),
-            dma((3, 7)),
-            dma((3, 7)),
+            dma((5, 7)),
+            dma((5, 7)),
             dma((devices,)),
             dma((devices,)),
             pltpu.SemaphoreType.REGULAR((buffers,)),
+            dma((2,)),
         ],
         compiler_params=pltpu.CompilerParams(
             vmem_limit_bytes=64 << 20, collective_id=0, has_side_effects=True
@@ -2089,9 +2172,29 @@
     )(lengths, bias, x, cot, pw, ow, ew, sw, gn)
 
 
-def update_kernel(heads, hidden_cols, p_ref, o_ref, feed_ref, stat_ref, gain_ref, table_ref, *refs):
+def update_kernel(
+    heads, hidden_cols, from_out, from_in, p_ref, o_ref, feed_ref, stat_ref, gain_ref, table_ref, *refs
+):
     weights, firsts, seconds = refs[:6], refs[6:12], refs[12:18]
-    outs, norm_ref, o_pad = refs[18:36], refs[36], refs[37]
+    outs, norm_ref, to_out, to_in, o_pad, held, sems = refs[18:36], *refs[36:]
+    pairs = ((from_out, to_out), (from_in, to_in))
+    rows = from_out.shape[0] // 2
+    ways = []
+    for which, (source, target) in enumerate(pairs):
+        for part in range(2):
+            span = slice(part * rows, (part + 1) * rows)
+            at = 2 * which + part
+            ways.append(
+                (
+                    pltpu.make_async_copy(source.at[span], held.at[which, span], sems.at[0, at]),
+                    pltpu.make_async_copy(held.at[which, span], target.at[span], sems.at[1, at]),
+                )
+            )
+    for inward, _ in ways:
+        inward.start()
+    for inward, outward in ways:
+        inward.wait()
+        outward.start()
     factor = stat_ref[1:2, 0:1]
     norm_ref[0, 0] = jnp.sum(stat_ref[0:1, 0:1])
     head_cols = heads * DH
@@ -2125,20 +2228,28 @@
     depth, columns = weights[4].shape
     update(4, slice(None), table_ref[:depth, :columns])
     update(5, slice(None), gain_ref[1:3, :rows])
-
-
-def update_call(grads, params_in, firsts, seconds, heads, hidden_cols):
+    for _, outward in ways:
+        outward.wait()
+
+
+def update_call(activations, grads, params_in, firsts, seconds, heads, hidden_cols):
     vmem = pl.BlockSpec(memory_space=pltpu.VMEM)
-    operands = [*grads, *params_in, *firsts, *seconds]
+    hbm = pl.BlockSpec(memory_space=ANY)
+    operands = [*activations, *grads, *params_in, *firsts, *seconds]
     return pl.pallas_call(
         functools.partial(update_kernel, heads, hidden_cols),
-        in_specs=[vmem] * len(operands),
-        out_specs=[vmem] * 18 + [pl.BlockSpec(memory_space=pltpu.SMEM)],
+        in_specs=[hbm] * 2 + [vmem] * (len(operands) - 2),
+        out_specs=[vmem] * 18 + [pl.BlockSpec(memory_space=pltpu.SMEM)] + [hbm] * 2,
         out_shape=[jax.ShapeDtypeStruct(a.shape, F32) for a in params_in] * 3
-        + [jax.ShapeDtypeStruct((1, 1), F32)],
-        scratch_shapes=[pltpu.VMEM((LANES, 2 * LANES), F32)],
+        + [jax.ShapeDtypeStruct((1, 1), F32)]
+        + [jax.ShapeDtypeStruct(a.shape, a.dtype) for a in activations],
+        scratch_shapes=[
+            pltpu.VMEM((LANES, 2 * LANES), F32),
+            pltpu.VMEM((2, *activations[0].shape), BF16),
+            pltpu.SemaphoreType.DMA((2, 4)),
+        ],
         compiler_params=params(),
-        cost_estimate=pl.CostEstimate(flops=4 << 20, bytes_accessed=8 << 20, transcendentals=0),
+        cost_estimate=pl.CostEstimate(flops=4 << 20, bytes_accessed=16 << 20, transcendentals=0),
         name="update",
     )(*operands)
 
@@ -2165,7 +2276,9 @@
         gains,
     )
     heads = project.shape[2] // DH
-    *results, norm = update_call(grads, weights, firsts, seconds, heads, expand.shape[2])
+    *results, norm, block_output, input_gradient = update_call(
+        (block_output, input_gradient), grads, weights, firsts, seconds, heads, expand.shape[2]
+    )
     results = [value.T if at % 6 in turned else value for at, value in enumerate(results)]
     return (block_output, input_gradient, norm.reshape(()), *results)
 

time: 182 us -> 167 us (0.918)
  Pallas kernels: 177 us -> 166 us
  local copies, waits for them, and re-layouts: 3.92 us -> 0 us
    pallas_call x1, Pallas kernels: 173 us -> 158 us  [layer(): pl.pallas_call(functools.partial(layer_kernel, (buffers, slots, heads, hi...]
    unnamed x6 -> x0, local copies, waits for them, and re-layouts: 3.92 us -> none
    pallas_call x1, Pallas kernels: 4.56 us -> 7.91 us  [update_call(): pl.pallas_call(functools.partial(update_kernel, heads, hidden_cols), in_s...]
where the time goes in v5:
time: 167 us; the launch traced here: 166 us
  Pallas kernels  166 us (99%)
    pallas_call x1, Pallas kernels, layer(): pl.pallas_call(functools.partial(layer_kernel, (buffers, slots, heads, hi...  158 us
    pallas_call x1, Pallas kernels, update_call(): pl.pallas_call(functools.partial(update_kernel, heads, hidden_cols), in_s...  7.91 us

profile of v5, /device:TPU:0, one launch (start us, length us, event | category | flops | bytes accessed | tf_op | source)
XLA Modules:
  0.0 166.5 jit_solution(17124245276030638717)
XLA Ops:
  0.7 157.7 %layer.1 = (bf16[1536,768]{1,0:T(8,128)(2,1)}, bf16[1536,768]{1,0:T(8,128)(2,1)}, f32[96,640]{1,0:T(8,128)}, f32[96,192]{1,0:T(8,128)}, f32[96,1536]{1,0:T(8,128...) custom-call(s32[2,12]{1,0:T(2,128)} %refs_0_.2, f32[12,32]{1,0:T(8,128)} %bitcast.17, ...), custom_call_target="tpu_custom_call" | custom-call | flops 64424509440 | bytes 25165824 | tf_op jit(solution)/shard_map/layer/pallas_call | solution.py:2096
  158.4 7.9 %update.1 = (f32[3,96,192]{2,1,0:T(8,128)}, f32[192,96]{1,0:T(8,128)}, f32[2,96,512]{2,1,0:T(8,128)}, f32[96,512]{1,0:T(8,128)}, f32[12,32]{1,0:T(8,128)}, /*ind...) custom-call(bf16[1536,768]{1,0:T(8,128)(2,1)} %get-tuple-element.50., ...), custom_call_target="tpu_custom_call" | custom-call | flops 4194304 | bytes 16777216 | tf_op jit(solution)/shard_map/update/pallas_call | solution.py:2239

commit v6 on v5

--- a/solution.py
+++ b/solution.py
@@ -1209,44 +1209,70 @@
     def landed(self, owner):
         self.copy(owner, 0, self.spot.flip).wait_recv()
 
+    def start(self, owner, slot, peer):
+        self.copy(owner, slot, peer).start()
+
+    def sent(self, owner, slot, peer):
+        self.copy(owner, slot, peer).wait_send()
+
+    def fan(self, owner, slot, act):
+        z = self.spot.z
+        act(owner, slot + 1, self.spot.along(2))
+        pl.when(z != 3)(lambda: act(owner, slot, self.spot.along(1)))
+        pl.when(z != 0)(lambda: act(owner, slot + 2, self.spot.along(3)))
+
+    def pass_on(self, owner, slot, act):
+        z = self.spot.z
+        pl.when(z == 2)(lambda: act(owner, slot, self.spot.along(1)))
+        pl.when(z == 1)(lambda: act(owner, slot, self.spot.along(3)))
+
     def begin(self):
         if self.flip_first:
-            self.copy(self.spot.w, 3, self.spot.flip).start()
-        for m in (2, 1, 3):
-            self.copy(self.spot.w, m - 1, self.spot.along(m)).start()
+            self.start(self.spot.w, 3, self.spot.flip)
+        self.fan(self.spot.w, 0, self.start)
         if not self.flip_first:
-            self.copy(self.spot.w, 3, self.spot.flip).start()
+            self.start(self.spot.w, 3, self.spot.flip)
 
     def forward(self):
         if self.flip_first:
             owner = self.spot.far_owner(0)
             self.landed(owner)
-            for m in (2, 1, 3):
-                self.copy(owner, 3 + m, self.spot.along(m)).start()
+            self.fan(owner, 4, self.start)
             return
-        for m in (3, 1, 2):
+        owner = self.spot.near_owner(2)
+        self.landed(owner)
+        self.pass_on(owner, 7, self.start)
+        self.start(owner, 5, self.spot.flip)
+        early = 1 + 2 * ((3 - self.spot.z) // 3)
+        for m in (early, 4 - early):
             owner = self.spot.near_owner(4 - m)
             self.landed(owner)
-            self.copy(owner, 3 + m, self.spot.flip).start()
+            self.start(owner, 3 + m, self.spot.flip)
+
+    def middle(self):
+        for owner, slot in ((self.spot.near_owner(2), 7), (self.spot.far_owner(2), 8)):
+            self.landed(owner)
+            self.pass_on(owner, slot, self.start)
 
     def finish(self):
         if self.flip_first:
+            for m in (1, 3):
+                self.landed(self.spot.near_owner(m))
+                self.landed(self.spot.far_owner(m))
+        else:
+            for m in range(4):
+                self.landed(self.spot.far_owner(m))
+
+    def drain(self):
+        self.sent(self.spot.w, 3, self.spot.flip)
+        self.fan(self.spot.w, 0, self.sent)
+        self.pass_on(self.spot.near_owner(2), 7, self.sent)
+        if self.flip_first:
+            self.fan(self.spot.far_owner(0), 4, self.sent)
+            self.pass_on(self.spot.far_owner(2), 8, self.sent)
+        else:
             for m in (1, 2, 3):
-                self.landed(self.spot.near_owner(4 - m))
-        else:
-            self.landed(self.spot.far_owner(0))
-        for m in (1, 2, 3):
-            self.landed(self.spot.far_owner(4 - m))
-
-    def drain(self):
-        self.copy(self.spot.w, 3, self.spot.flip).wait_send()
-        for m in (1, 2, 3):
-            self.copy(self.spot.w, m - 1, self.spot.along(m)).wait_send()
-            if self.flip_first:
-                owner, peer = self.spot.far_owner(0), self.spot.along(m)
-            else:
-                owner, peer = self.spot.near_owner(4 - m), self.spot.flip
-            self.copy(owner, 3 + m, peer).wait_send()
+                self.sent(self.spot.near_owner(4 - m), 3 + m, self.spot.flip)
 
 
 class Reduce:
@@ -1449,16 +1475,16 @@
         fbuf[mine, j * chunk : j * chunk + part] = ew_ref[0, :, span].astype(BF16)
         fbuf[mine, j * chunk + part : j * chunk + 2 * part] = ew_ref[1, :, span].astype(BF16)
         fbuf[mine, j * chunk + 2 * part : (j + 1) * chunk] = sw_ref[:, span].astype(BF16)
-    piece = chunk // 2
+    feed_cuts = (0, 256, 512, 768, 1024, 1280, 1536)
     feeds_gather = [
         Gather(
             spot,
-            lambda v, at=at: fbuf.at[at_rows(v), at * piece : (at + 1) * piece],
+            lambda v, at=at: fbuf.at[at_rows(v), feed_cuts[at] : feed_cuts[at + 1]],
             gather_s.at[4 + at],
             gather_r.at[4 + at],
-            flip_first=at == 3,
-        )
-        for at in range(4)
+            flip_first=at in (5,),
+        )
+        for at in range(len(feed_cuts) - 1)
     ]
 
     near_at = (blocks - 2) * LANES
@@ -1492,6 +1518,10 @@
     gains = pbuf[:, 4 * LANES :].astype(F32).T[qkv_cols - 4 * LANES : qkv_cols - 4 * LANES + 8]
     gain_one, gain_two = gains[0:1], gains[1:2]
 
+    def relay_feeds(*ats):
+        for at in ats:
+            feeds_gather[at].forward()
+
     def relay_outs():
         for group in outs_gather:
             group.forward()
@@ -1519,8 +1549,8 @@
     step = 256
     qkv_events = ({}, {0: feeds_gather[0].forward})
     att_events = (
-        {2: relay_outs, 5: feeds_gather[3].forward},
-        {0: outs_beside, 3: lambda: att_relay(0), 4: feeds_gather[1].forward},
+        {1: relay_outs, 2: lambda: relay_feeds(5)},
+        {0: lambda: (outs_beside(), relay_feeds(1))[1], 1: feeds_gather[2].forward, 2: feeds_gather[3].forward},
     )
 
     def fire(events, at):
@@ -1551,22 +1581,27 @@
             lax.broadcasted_iota(jnp.int32, (1, length), 1), lengths_ref, b, slots
         )
 
-        @pl.loop(0, blocks)
+        @pl.loop(0, blocks // 2)
         def _(at, b=b, base=base, seg_keys=seg_keys):
             fire(att_events[b], at)
-            begin = pl.multiple_of(at * LANES, LANES)
-            span = pl.ds(pl.multiple_of(base + begin, LANES), LANES)
-            window = pl.ds(pl.multiple_of((blocks - 1 - at) * LANES, LANES), length)
+            begin = pl.multiple_of(at * 2 * LANES, 2 * LANES)
+            span = pl.ds(pl.multiple_of(base + begin, 2 * LANES), 2 * LANES)
+            windows = [
+                pl.ds(pl.multiple_of((blocks - 1 - r - 2 * at) * LANES, LANES), length)
+                for r in range(2)
+            ]
             seg_rows = segments_of(
-                lax.broadcasted_iota(jnp.int32, (LANES, 1), 0) + begin, lengths_ref, b, slots
+                lax.broadcasted_iota(jnp.int32, (2 * LANES, 1), 0) + begin, lengths_ref, b, slots
             )
             same = seg_rows == seg_keys
-            lane = lax.broadcasted_iota(jnp.int32, (LANES, LANES), 1)
-            logs = jnp.zeros((LANES, LANES), F32)
+            lane = lax.broadcasted_iota(jnp.int32, (2 * LANES, LANES), 1)
+            logs = jnp.zeros((2 * LANES, LANES), F32)
             queries = qkv_ref[span, :head_cols]
             outs = []
             for h in range(heads):
-                scores = mm(queries[:, h * DH : (h + 1) * DH], kt[h]) + strip[h, :, window]
+                scores = mm(queries[:, h * DH : (h + 1) * DH], kt[h]) + jnp.concatenate(
+                    [strip[h, :, window] for window in windows], axis=0
+                )
                 scores = jnp.where(same, scores, masked_score)
                 row_max = jnp.max(scores, axis=1, keepdims=True)
                 raised = jnp.exp(scores - row_max)
@@ -1578,6 +1613,8 @@
             att_ref[spot.n, span] = jnp.concatenate(outs, axis=1)
 
         att_send(b)
+        if b == 1:
+            att_relay(0)
 
     k0 = 0.7978845608028654
     k1 = 0.044715
@@ -1615,14 +1652,17 @@
         lone(obuf.at[spot.n_diag], obuf.at[spot.n_diag], 2, spot.beside).wait_recv()
 
     def first_feed():
-        feeds_gather[2].forward()
+        feeds_gather[4].forward()
+        feeds_gather[5].middle()
         feeds_gather[0].finish()
         feeds_gather[1].finish()
+        feeds_gather[2].finish()
 
     def last_feed():
         att_relay(1)
-        feeds_gather[2].finish()
         feeds_gather[3].finish()
+        feeds_gather[4].finish()
+        feeds_gather[5].finish()
 
     def half_of(b, keep):
         return half_rows(b, (1 - core) * (1 - keep) + core * keep)
@@ -2151,8 +2191,8 @@
             pltpu.VMEM((8, width), F32),
             pltpu.VMEM((8, LANES), F32),
             pltpu.VMEM((devices, 8, LANES), F32),
-            dma((8, 7)),
-            dma((8, wide)),
+            dma((12, 9)),
+            dma((12, wide)),
             dma((27,)),
             dma((27,)),
             dma((5, 7)),

time: 167 us -> 161 us (0.964)
  Pallas kernels: 166 us -> 160 us
    pallas_call x1, Pallas kernels: 158 us -> 152 us  [layer(): pl.pallas_call(functools.partial(layer_kernel, (buffers, slots, heads, hi...]
where the time goes in v6:
time: 161 us
  Pallas kernels  160 us (99%)
    pallas_call x1, Pallas kernels, layer(): pl.pallas_call(functools.partial(layer_kernel, (buffers, slots, heads, hi...  152 us
    pallas_call x1, Pallas kernels, update_call(): pl.pallas_call(functools.partial(update_kernel, heads, hidden_cols), in_s...  7.91 us

profile of v6, /device:TPU:0, one launch (start us, length us, event | category | flops | bytes accessed | tf_op | source)
XLA Modules:
  0.0 160.8 jit_solution(5315189065663185766)
XLA Ops:
  0.7 152.1 %layer.1 = (bf16[1536,768]{1,0:T(8,128)(2,1)}, bf16[1536,768]{1,0:T(8,128)(2,1)}, f32[96,640]{1,0:T(8,128)}, f32[96,192]{1,0:T(8,128)}, f32[96,1536]{1,0:T(8,128...) custom-call(s32[2,12]{1,0:T(2,128)} %refs_0_.2, f32[12,32]{1,0:T(8,128)} %bitcast.17, ...), custom_call_target="tpu_custom_call" | custom-call | flops 64424509440 | bytes 25165824 | tf_op jit(solution)/shard_map/layer/pallas_call | solution.py:2136
  152.7 7.9 %update.1 = (f32[3,96,192]{2,1,0:T(8,128)}, f32[192,96]{1,0:T(8,128)}, f32[2,96,512]{2,1,0:T(8,128)}, f32[96,512]{1,0:T(8,128)}, f32[12,32]{1,0:T(8,128)}, /*ind...) custom-call(bf16[1536,768]{1,0:T(8,128)(2,1)} %get-tuple-element.50., ...), custom_call_target="tpu_custom_call" | custom-call | flops 4194304 | bytes 16777216 | tf_op jit(solution)/shard_map/update/pallas_call | solution.py:2279

commit v7 on v6

--- a/solution.py
+++ b/solution.py
@@ -1407,6 +1407,8 @@
         norm_r,
         credit,
         load,
+        att_s,
+        att_r,
     ) = refs
     spot = Place(wide, narrow)
     core = spot.core
@@ -1532,25 +1534,28 @@
         lone(obuf.at[spot.n], obuf.at[spot.n], 1, spot.beside).start()
         lone(obuf.at[spot.n_far], obuf.at[spot.n_far], 2, spot.beside).start()
 
-    def att_view(which, b):
-        return att_ref.at[which, b * length : (b + 1) * length]
-
-    def att_copy(which, b, slot, peer):
-        return lone(att_view(which, b), att_view(which, b), 3 + 3 * b + slot, peer)
-
-    def att_send(b):
-        att_copy(spot.n, b, 0, spot.across).start()
-        att_copy(spot.n, b, 1, spot.beside).start()
-
-    def att_relay(b):
-        att_copy(spot.n_far, b, 0, spot.across).wait_recv()
-        att_copy(spot.n_far, b, 2, spot.beside).start()
-
     step = 256
-    qkv_events = ({}, {0: feeds_gather[0].forward})
+    strides = length // step
+
+    def att_piece(which, b, at, kind, peer):
+        span = pl.ds(pl.multiple_of(b * length + at * step, step), step)
+        view = att_ref.at[which, span]
+        slot = (kind * buffers + b) * strides + at
+        return remote(view, view, att_s.at[slot], att_r.at[slot], peer)
+
+    def att_send(b, at):
+        att_piece(spot.n, b, at, 0, spot.across).start()
+        att_piece(spot.n, b, at, 1, spot.beside).start()
+
+    def att_relay(b, pieces):
+        for at in pieces:
+            att_piece(spot.n_far, b, at, 0, spot.across).wait_recv()
+            att_piece(spot.n_far, b, at, 2, spot.beside).start()
+
+    qkv_events = ({}, {0: feeds_gather[1].forward})
     att_events = (
-        {1: relay_outs, 2: lambda: relay_feeds(5)},
-        {0: lambda: (outs_beside(), relay_feeds(1))[1], 1: feeds_gather[2].forward, 2: feeds_gather[3].forward},
+        {0: relay_outs, 1: lambda: relay_feeds(5), 2: feeds_gather[0].forward},
+        {0: lambda: (outs_beside(), relay_feeds(2))[1], 1: feeds_gather[3].forward, 2: lambda: (relay_feeds(4), att_relay(0, range(1)))[1]},
     )
 
     def fire(events, at):
@@ -1611,10 +1616,10 @@
                 logs = jnp.where(lane == h, row_max + jnp.log(sums), logs)
             log_ref[span] = logs
             att_ref[spot.n, span] = jnp.concatenate(outs, axis=1)
-
-        att_send(b)
+            att_send(b, at)
+
         if b == 1:
-            att_relay(0)
+            att_relay(0, range(1, strides))
 
     k0 = 0.7978845608028654
     k1 = 0.044715
@@ -1652,14 +1657,13 @@
         lone(obuf.at[spot.n_diag], obuf.at[spot.n_diag], 2, spot.beside).wait_recv()
 
     def first_feed():
-        feeds_gather[4].forward()
         feeds_gather[5].middle()
         feeds_gather[0].finish()
         feeds_gather[1].finish()
         feeds_gather[2].finish()
 
     def last_feed():
-        att_relay(1)
+        att_relay(1, range(strides))
         feeds_gather[3].finish()
         feeds_gather[4].finish()
         feeds_gather[5].finish()
@@ -1684,10 +1688,9 @@
     @pl.loop(0, buffers)
     def _(b):
         def att_ready():
-            span = pl.ds(pl.multiple_of(b * length, LANES), length)
-            for slot, which in ((4, spot.n_beside), (5, spot.n_diag)):
-                view = att_ref.at[which, span]
-                lone(view, view, slot + 3 * b, spot.beside).wait_recv()
+            for at in range(strides):
+                att_piece(spot.n_beside, b, at, 1, spot.beside).wait_recv()
+                att_piece(spot.n_diag, b, at, 2, spot.beside).wait_recv()
 
         att_ready()
 
@@ -1769,7 +1772,8 @@
     for group in feeds_gather:
         group.drain()
     for b in range(buffers):
-        att_copy(spot.n_far, b, 2, spot.beside).wait_send()
+        for at in range(strides):
+            att_piece(spot.n_far, b, at, 2, spot.beside).wait_send()
     feed_reds = []
     for j in range(2):
         for begin in range(0, width, step):
@@ -2089,11 +2093,9 @@
 
     for b in range(buffers):
         in_core(b, 1 - core).wait_recv()
-        for slot, which, peer in (
-            (0, spot.n, spot.across),
-            (1, spot.n, spot.beside),
-        ):
-            att_copy(which, b, slot, peer).wait_send()
+        for at in range(strides):
+            att_piece(spot.n, b, at, 0, spot.across).wait_send()
+            att_piece(spot.n, b, at, 1, spot.beside).wait_send()
         ff_core(b).wait_send()
         ff_across(b).wait_send()
         dn_core(b, 1).wait_send()
@@ -2201,6 +2203,8 @@
             dma((devices,)),
             pltpu.SemaphoreType.REGULAR((buffers,)),
             dma((2,)),
+            dma((3 * buffers * (length // 256),)),
+            dma((3 * buffers * (length // 256),)),
         ],
         compiler_params=pltpu.CompilerParams(
             vmem_limit_bytes=64 << 20, collective_id=0, has_side_effects=True

time: 161 us -> 159 us (0.988)
  Pallas kernels: 160 us -> 158 us
    pallas_call x1, Pallas kernels: 152 us -> 150 us  [layer(): pl.pallas_call(functools.partial(layer_kernel, (buffers, slots, heads, hi...]
where the time goes in v7:
time: 159 us
  Pallas kernels  158 us (99%)
    pallas_call x1, Pallas kernels, layer(): pl.pallas_call(functools.partial(layer_kernel, (buffers, slots, heads, hi...  150 us
    pallas_call x1, Pallas kernels, update_call(): pl.pallas_call(functools.partial(update_kernel, heads, hidden_cols), in_s...  7.91 us

profile of v7, /device:TPU:0, one launch (start us, length us, event | category | flops | bytes accessed | tf_op | source)
XLA Modules:
  0.0 159.2 jit_solution(13995339472728452394)
XLA Ops:
  0.7 150.4 %layer.1 = (bf16[1536,768]{1,0:T(8,128)(2,1)}, bf16[1536,768]{1,0:T(8,128)(2,1)}, f32[96,640]{1,0:T(8,128)}, f32[96,192]{1,0:T(8,128)}, f32[96,1536]{1,0:T(8,128...) custom-call(s32[2,12]{1,0:T(2,128)} %refs_0_.2, f32[12,32]{1,0:T(8,128)} %bitcast.17, ...), custom_call_target="tpu_custom_call" | custom-call | flops 64424509440 | bytes 25165824 | tf_op jit(solution)/shard_map/layer/pallas_call | solution.py:2138
  151.1 7.9 %update.1 = (f32[3,96,192]{2,1,0:T(8,128)}, f32[192,96]{1,0:T(8,128)}, f32[2,96,512]{2,1,0:T(8,128)}, f32[96,512]{1,0:T(8,128)}, f32[12,32]{1,0:T(8,128)}, /*ind...) custom-call(bf16[1536,768]{1,0:T(8,128)(2,1)} %get-tuple-element.50., ...), custom_call_target="tpu_custom_call" | custom-call | flops 4194304 | bytes 16777216 | tf_op jit(solution)/shard_map/update/pallas_call | solution.py:2283

commit v8 on v7

--- a/solution.py
+++ b/solution.py
@@ -1409,6 +1409,8 @@
         load,
         att_s,
         att_r,
+        last_s,
+        last_r,
     ) = refs
     spot = Place(wide, narrow)
     core = spot.core
@@ -1647,9 +1649,20 @@
         view = out_ref.at[half_rows(b, which)]
         return lone(view, view, 23 + b, spot.beside)
 
-    def in_core(b, which):
-        view = in_ref.at[half_rows(b, which)]
-        return lone(view, view, 25 + b, spot.beside)
+    lasts = half // LANES
+
+    def in_core(b, which, i):
+        begin = pl.multiple_of(b * length + which * half + i * LANES, LANES)
+        view = in_ref.at[pl.ds(begin, LANES)]
+        at = lasts * (buffers + b) + i
+        return remote(view, view, last_s.at[at], last_r.at[at], spot.beside)
+
+    def dn_last(b, i):
+        span = pl.ds(pl.multiple_of(i * LANES, LANES), LANES)
+        at = lasts * b + i
+        return remote(
+            dn_sum.at[b, span], dn_far.at[b, span], last_s.at[at], last_r.at[at], spot.across
+        )
 
     def outs_ready():
         loads[1].wait()
@@ -1911,7 +1924,8 @@
                 dn_core(b, 1).wait_recv()
                 dn_sum[b] = (dn.astype(F32) + dn_in[b].astype(F32)).astype(BF16)
                 pl.semaphore_wait(credit.at[b], 1)
-                dn_across(b, 1).start()
+                for i in range(lasts):
+                    dn_last(b, i).start()
 
     row = lax.broadcasted_iota(jnp.int32, (LANES, width), 0)
     gain_rows = jnp.where(
@@ -1963,10 +1977,9 @@
         out_core(b, core).start()
 
     def finish_in(b):
-        dn_across(b, 1).wait_recv()
-
         @pl.loop(0, half // LANES)
         def _(i):
+            dn_last(b, i).wait_recv()
             span, here = own_block(b, i)
             upstream = dn_sum[b, span].astype(F32) + dn_far[b, span].astype(F32)
             values = x_ref[here].astype(F32)
@@ -1974,8 +1987,7 @@
                 low_ref[here].astype(F32)
                 + norm_back(values, rms_scale(values), gain_one, upstream)
             ).astype(BF16)
-
-        in_core(b, core).start()
+            in_core(b, core, i).start()
 
     def square_of(value):
         return jnp.sum(jnp.sum(value * value, axis=1, keepdims=True), axis=0, keepdims=True)
@@ -2092,17 +2104,19 @@
     stat_ref[...] = jnp.where(row8 == 0, global_norm, factor)
 
     for b in range(buffers):
-        in_core(b, 1 - core).wait_recv()
+        for i in range(lasts):
+            in_core(b, 1 - core, i).wait_recv()
         for at in range(strides):
             att_piece(spot.n, b, at, 0, spot.across).wait_send()
             att_piece(spot.n, b, at, 1, spot.beside).wait_send()
         ff_core(b).wait_send()
         ff_across(b).wait_send()
         dn_core(b, 1).wait_send()
-        dn_across(b, 1).wait_send()
+        for i in range(lasts):
+            dn_last(b, i).wait_send()
+            in_core(b, core, i).wait_send()
         low_core(b, core).wait_send()
         out_core(b, core).wait_send()
-        in_core(b, core).wait_send()
     lone(o_views[0](spot.w), o_views[0](spot.w), 0, spot.across).wait_send()
     lone(obuf.at[spot.n], obuf.at[spot.n], 1, spot.beside).wait_send()
     lone(obuf.at[spot.n_far], obuf.at[spot.n_far], 2, spot.beside).wait_send()
@@ -2205,6 +2219,8 @@
             dma((2,)),
             dma((3 * buffers * (length // 256),)),
             dma((3 * buffers * (length // 256),)),
+            dma((2 * buffers * (half // LANES),)),
+            dma((2 * buffers * (half // LANES),)),
         ],
         compiler_params=pltpu.CompilerParams(
             vmem_limit_bytes=64 << 20, collective_id=0, has_side_effects=True

time: 159 us -> 159 us (level)
  no operation moved by 1% of the time
where the time goes in v8:
time: 159 us; the launch traced here: 158 us
  Pallas kernels  158 us (99%)
    pallas_call x1, Pallas kernels, layer(): pl.pallas_call(functools.partial(layer_kernel, (buffers, slots, heads, hi...  150 us
    pallas_call x1, Pallas kernels, update_call(): pl.pallas_call(functools.partial(update_kernel, heads, hidden_cols), in_s...  7.91 us

profile of v8, /device:TPU:0, one launch (start us, length us, event | category | flops | bytes accessed | tf_op | source)
XLA Modules:
  0.0 158.4 jit_solution(8461872228012502359)
XLA Ops:
  0.7 149.7 %layer.1 = (bf16[1536,768]{1,0:T(8,128)(2,1)}, bf16[1536,768]{1,0:T(8,128)(2,1)}, f32[96,640]{1,0:T(8,128)}, f32[96,192]{1,0:T(8,128)}, f32[96,1536]{1,0:T(8,128...) custom-call(s32[2,12]{1,0:T(2,128)} %refs_0_.2, f32[12,32]{1,0:T(8,128)} %bitcast.17, ...), custom_call_target="tpu_custom_call" | custom-call | flops 64424509440 | bytes 25165824 | tf_op jit(solution)/shard_map/layer/pallas_call | solution.py:2152
  150.3 7.9 %update.1 = (f32[3,96,192]{2,1,0:T(8,128)}, f32[192,96]{1,0:T(8,128)}, f32[2,96,512]{2,1,0:T(8,128)}, f32[96,512]{1,0:T(8,128)}, f32[12,32]{1,0:T(8,128)}, /*ind...) custom-call(bf16[1536,768]{1,0:T(8,128)(2,1)} %get-tuple-element.50., ...), custom_call_target="tpu_custom_call" | custom-call | flops 4194304 | bytes 16777216 | tf_op jit(solution)/shard_map/update/pallas_call | solution.py:2299
